TPU v7x, 512 devices: a whole 4x8x8 slice. The times are simulated.
512 devices in a mesh: sec: 32 (over x, z), mpo: 16 (over y, core).
Axes of the slice: x: 4, y: 8, z: 8, core: 2. Of those that a mesh axis runs over, the one named last changes fastest.
Arguments:
- psi_blocks: bfloat16 [256, 256, 256], P('sec'), may hold values from -6 to 6
- left_env: bfloat16 [64, 256, 256], P('mpo'), may hold values from -0.375 to 0.375
- right_env: bfloat16 [64, 256, 256], P('mpo'), may hold values from -0.046875 to 0.046875
- dest_index: int32 [16, 32, 32, 1], P('mpo', 'sec'), may hold values from 0 to 31; in each aligned block of 32 rows (0 to 31, 32 to 63, ..., all dimensions but the last counted through in order) at most 2 rows name the same one
- dest_slot: int32 [16, 32, 32], P('mpo', 'sec'), may hold values from 0 to 7
Outputs:
- sigma_blocks: float32 [256, 256, 256], P('sec', 'mpo')
Inputs may be any that keep to these rules, and one draw needn't show every extreme that they name: `dest_index`: in the 32 pairs of one device (fixed j and i), at most 2 name the same index of sec, and some device has exactly 2 for one index.
All inputs are finite; a program needn't handle non-finite values.
Results may differ from a plain program's by a relative error of at most 0.0041.
Values may be sent and summed in bfloat16 or wider, within the bound.
No kernel may reach another device: no remote copies, remote signals or barrier semaphores. Data moves between devices by JAX's collectives and lax.ppermute only.
A program may use at most 128 MiB of HBM per device.

v0:
```python
import jax
import jax.numpy as jnp
from jax import lax
from jax.sharding import PartitionSpec as P


def collect(sectors, tags, received, width):
    flat_tags = tags.reshape(-1)
    select = (jnp.arange(sectors, dtype=jnp.int32)[:, None] == flat_tags[None, :]).astype(
        jnp.bfloat16
    )
    return jnp.dot(select, received.reshape(-1, width * width), preferred_element_type=jnp.float32)


def on_device(psi_blocks, left_env, right_env, dest_index, dest_slot):
    sectors = psi_blocks.shape[0]
    terms = left_env.shape[0]
    width = psi_blocks.shape[1]
    shards = lax.axis_size("sec")
    pairs = sectors * terms
    capacity = max(2, 3 * pairs // (2 * shards))
    dest = dest_index.reshape(pairs)
    slot = dest_slot.reshape(pairs)
    onehot = (dest[:, None] == jnp.arange(shards, dtype=jnp.int32)[None, :]).astype(jnp.int32)
    rank = jnp.sum(jnp.cumsum(onehot, axis=0) * onehot, axis=1) - 1
    place = dest * capacity + rank
    labels = jnp.full((shards * capacity,), sectors, jnp.int32).at[place].set(slot)
    labels = labels.reshape(shards, capacity)
    half = jnp.einsum(
        "wab,sbc->wsac", left_env, psi_blocks, preferred_element_type=jnp.float32
    ).astype(jnp.bfloat16)
    full = jnp.einsum("wsac,wcd->wsad", half, right_env, preferred_element_type=jnp.float32).astype(
        jnp.bfloat16
    )
    outgoing = (
        jnp.zeros((shards * capacity, width, width), jnp.bfloat16)
        .at[place]
        .set(full.reshape(pairs, width, width))
    )
    outgoing = outgoing.reshape(shards, capacity, width, width)
    received, tags = (
        lax.all_to_all(outgoing, "sec", split_axis=0, concat_axis=0, tiled=True),
        lax.all_to_all(labels, "sec", split_axis=0, concat_axis=0, tiled=True),
    )
    summed = collect(sectors, tags, received, width)
    summed = summed.reshape(sectors, width, width)
    return lax.psum_scatter(summed, "mpo", scatter_dimension=1, tiled=True)


def solution(mesh):
    in_specs = (
        P("sec", None, None),
        P("mpo", None, None),
        P("mpo", None, None),
        P("mpo", "sec", None, None),
        P("mpo", "sec", None),
    )
    out_specs = P("sec", "mpo", None)
    return jax.shard_map(
        on_device, mesh=mesh, in_specs=in_specs, out_specs=out_specs, check_vma=False
    )
```

profile of v0, /device:TPU:1, one launch (start us, length us, event | category | flops | bytes accessed | tf_op | source)
XLA Modules:
  0.0 320.8 jit_solution(11198603474283274258)
XLA Ops:
  6.5 0.0 copy-start
  6.5 0.8 fusion.16
  7.4 0.1 reduce_window_sum.11
  7.4 0.8 select_reduce_fusion
  8.2 0.7 fusion.20
  8.9 0.8 scatter_custom_fusion
  9.7 0.7 all_to_all.9
  10.4 13.7 %all-to-all-start = ((s32[32,1,2]{2,1,0:T(1,128)}), s32[32,1,2]{2,1,0:T(1,128)S(1)}, u32[]{:S(2)}, u32[]{:S(2)}) async-start(s32[32,1,2]{2,1,0:T(1,128)} %bitcast.5), calls=%async_computation | async-start | bytes 32768 | tf_op jit(solution)/shard_map/all_to_all | solution.py:43
  24.2 0.0 copy-done
  24.2 5.9 %fusion.8 = bf16[4,8,256,256]{3,2,1,0:T(8,128)(2,1)} fusion(bf16[8,256,256]{2,1,0:T(8,128)(2,1)S(1)} %copy-done, bf16[4,256,256]{2,1,0:T(8,128)(2,1)} %param.7, bf16[4,256,256]{2,1,0:T(8,128)(2,1)} %param.6), kind=kOutput, calls=%fused_computation.9 | convolution fusion | flops 2151677952 | bytes 6291456 | tf_op jit(solution)/shard_map/wsac,wcd->wsad/dot_general | solution.py:32
  30.1 4.2 %broadcast_in_dim.5 = bf16[64,256,256]{2,1,0:T(8,128)(2,1)} broadcast(bf16[]{:T(256)} %constant.17.clone.1), dimensions={} | broadcast | bytes 8388610 | tf_op jit(solution)/shard_map/broadcast_in_dim | solution.py:36
  34.3 11.4 %scatter_fusion = bf16[64,256,256]{2,1,0:T(8,128)(2,1)} fusion(bf16[64,256,256]{2,1,0:T(8,128)(2,1)} %broadcast_in_dim.5, s32[32]{0:T(128)S(1)} %fusion.20, bf16[32,256,256]{2,1,0:T(8,128)(2,1)} %bitcast.49), kind=kCustom, calls=%fused_computation.1 | custom fusion | bytes 12583040 | tf_op jit(solution)/shard_map/scatter | solution.py:38
  45.7 0.0 all-to-all-done
  45.7 9.4 %all-to-all-start.1 = ((bf16[32,2,256,256]{3,2,1,0:T(8,128)(2,1)}), bf16[32,2,256,256]{3,2,1,0:T(8,128)(2,1)}, u32[]{:S(2)}, u32[]{:S(2)}) async-start(bf16[32,2,256,256]{3,2,1,0:T(8,128)(2,1)} %bitcast.48), calls=%async_computation.1 | async-start | bytes 16777216 | tf_op jit(solution)/shard_map/all_to_all | solution.py:42
  55.0 0.0 reduce-scatter.2.cloned.1.call-start
  55.1 0.5 broadcast.55
  55.6 0.7 reduce.3
  56.3 0.1 eq.35
  56.4 181.9 %all-to-all-done.1 = bf16[32,2,256,256]{3,2,1,0:T(8,128)(2,1)} async-done(((bf16[32,2,256,256]{3,2,1,0:T(8,128)(2,1)}), bf16[32,2,256,256]{3,2,1,0:T(8,128)(2,1)}, u32[]{:S(2)}, u32[]{:S(2)}) %all-to-all-start.1) | async-done | bytes 8388640 | tf_op jit(solution)/shard_map/all_to_all | solution.py:42
  238.3 9.3 %fusion = f32[8,256,256]{2,0,1:T(8,128)} fusion(s32[64]{0:T(128)S(1)} %eq.35, bf16[8,8,256,256]{3,2,1,0:T(8,128)(2,1)} %bitcast.21), kind=kOutput, calls=%fused_computation.2 | convolution fusion | flops 67109376 | bytes 10486016 | tf_op jit(solution)/shard_map/dot_general | solution.py:12
  247.6 0.0 reduce-scatter.2.cloned.1.call-update
  247.6 64.7 %reduce-scatter.2.cloned.1.call-done = f32[8,16,256]{2,0,1:T(8,128)} async-done(((f32[8,256,256]{2,0,1:T(8,128)}), f32[8,16,256]{2,0,1:T(8,128)}) %reduce-scatter.2.cloned.1.call-update) | async-done | bytes 131088 | tf_op jit(solution)/shard_map/reduce_scatter | solution.py:47
  312.3 1.6 copy.13
Async XLA Ops:
  6.5 17.6 %copy-start = (bf16[8,256,256]{2,1,0:T(8,128)(2,1)S(1)}, bf16[8,256,256]{2,1,0:T(8,128)(2,1)}, u32[]{:S(2)}) copy-start(bf16[8,256,256]{2,1,0:T(8,128)(2,1)} %param.5) | copy-start | bytes 3145732
  10.4 35.2 %all-to-all-start = ((s32[32,1,2]{2,1,0:T(1,128)}), s32[32,1,2]{2,1,0:T(1,128)S(1)}, u32[]{:S(2)}, u32[]{:S(2)}) async-start(s32[32,1,2]{2,1,0:T(1,128)} %bitcast.5), calls=%async_computation | async-start | bytes 32768 | tf_op jit(solution)/shard_map/all_to_all | solution.py:43
  45.7 192.7 %all-to-all-start.1 = ((bf16[32,2,256,256]{3,2,1,0:T(8,128)(2,1)}), bf16[32,2,256,256]{3,2,1,0:T(8,128)(2,1)}, u32[]{:S(2)}, u32[]{:S(2)}) async-start(bf16[32,2,256,256]{3,2,1,0:T(8,128)(2,1)} %bitcast.48), calls=%async_computation.1 | async-start | bytes 16777216 | tf_op jit(solution)/shard_map/all_to_all | solution.py:42
  55.0 257.3 %reduce-scatter.2.cloned.1.call-start = ((), (), s32[]{:S(2)}) async-start(), calls=%async_computation.3 | async-start | bytes 2228224 | tf_op jit(solution)/shard_map/reduce_scatter | solution.py:47
Sparse Core Ops, SparseCore 0:
  247.8 64.5 reduce-scatter.1
where the time goes:
time: 322 us; the launch traced here: 321 us
  waiting for transfers between devices  247 us (77%)
  starting transfers between devices  23.1 us (7%)
  local copies, waits for them, and re-layouts  19.3 us (6%)
  matrix products  15.2 us (5%)
  between operations  13.4 us (4%)
    all_to_all x1, waiting for transfers between devices, on_device(): lax.all_to_all(outgoing, 'sec', split_axis=0, concat_axis=0, tiled=True)  182 us
    reduce_scatter x1, waiting for transfers between devices, on_device(): return lax.psum_scatter(summed, 'mpo', scatter_dimension=1, tiled=True)  64.7 us
    all_to_all x1, starting transfers between devices, on_device(): lax.all_to_all(labels, 'sec', split_axis=0, concat_axis=0, tiled=True)  13.7 us
    scatter x1, local copies, waits for them, and re-layouts, on_device(): outgoing = jnp.zeros((shards * capacity, width, width), jnp.bfloat16).at[...  11.4 us
    all_to_all x1, starting transfers between devices, on_device(): lax.all_to_all(outgoing, 'sec', split_axis=0, concat_axis=0, tiled=True)  9.37 us
    dot_general x1, matrix products, collect(): jnp.dot(select, received.reshape(-1, width * width), preferred_element_ty...  9.3 us
  transfers between devices with their start and end apart: 3, of which 2 were waited for; matrix products, arithmetic and copies ran while one was open for 7% of the time, Pallas kernels for 0%

commit v1 on v0

v1 whole, which is shorter than its diff:
```python
import jax
import jax.numpy as jnp
from jax import lax
from jax.sharding import PartitionSpec as P


def on_device(psi_blocks, left_env, right_env, dest_index, dest_slot):
    sectors = psi_blocks.shape[0]
    width = psi_blocks.shape[1]
    shards = lax.axis_size("sec")
    lefts = lax.all_to_all(left_env, "mpo", split_axis=1, concat_axis=0, tiled=True)
    rights = lax.all_gather(right_env, "mpo", axis=0, tiled=True)
    target = dest_index[:, :, :, 0] * sectors + dest_slot
    targets = lax.all_gather(target[0], "mpo", axis=0, tiled=True).reshape(-1)
    half = jnp.einsum("wrb,sbc->wsrc", lefts, psi_blocks, preferred_element_type=jnp.float32)
    half = half.astype(jnp.bfloat16)
    full = jnp.einsum("wsrc,wcd->wsrd", half, rights, preferred_element_type=jnp.float32)
    full = full.astype(jnp.bfloat16)
    rows = full.shape[2]
    select = jnp.arange(shards * sectors, dtype=jnp.int32)[:, None] == targets[None, :]
    partial = jnp.dot(
        select.astype(jnp.bfloat16),
        full.reshape(-1, rows * width),
        preferred_element_type=jnp.float32,
    )
    partial = partial.reshape(shards * sectors, rows, width)
    return lax.psum_scatter(partial, "sec", scatter_dimension=0, tiled=True)


def solution(mesh):
    in_specs = (
        P("sec", None, None),
        P("mpo", None, None),
        P("mpo", None, None),
        P("mpo", "sec", None, None),
        P("mpo", "sec", None),
    )
    out_specs = P("sec", "mpo", None)
    return jax.shard_map(
        on_device, mesh=mesh, in_specs=in_specs, out_specs=out_specs, check_vma=False
    )
```

time: 322 us -> 339 us (1.053); the launches traced: 321 us -> 334 us
  blocking collectives: 0 us -> 26.3 us
  starting transfers between devices: 23.1 us -> 10.3 us
  waiting for transfers between devices: 247 us -> 252 us
    all_to_all x2 -> x1, waiting for transfers between devices: 182 us -> 0.01 us  [on_device(): lax.all_to_all(left_env, 'mpo', split_axis=1, concat_axis=0, tiled=True)]
    reduce_scatter x1, waiting for transfers between devices: 64.7 us -> 224 us  [on_device(): return lax.psum_scatter(partial, 'sec', scatter_dimension=0, tiled=True)]
    all_gather x0 -> x1, waiting for transfers between devices: none -> 28.2 us  [on_device(): rights = lax.all_gather(right_env, 'mpo', axis=0, tiled=True)]
    all_gather x0 -> x1, blocking collectives: none -> 26.3 us  [on_device(): targets = lax.all_gather(target[0], 'mpo', axis=0, tiled=True).reshape(-1)]
    all_to_all x2 -> x1, starting transfers between devices: 23.1 us -> 10.2 us  [on_device(): lax.all_to_all(left_env, 'mpo', split_axis=1, concat_axis=0, tiled=True)]
    scatter x2 -> x0, local copies, waits for them, and re-layouts: 12.2 us -> none  [the longest x1 11.4 us: on_device(): outgoing = jnp.zeros((shards * capacity, width, width), jnp.bfloat16).at[...]
    unnamed x2 -> x4, local copies, waits for them, and re-layouts: 0.01 us -> 8.62 us
    dot_general x0 -> x1, local copies, waits for them, and re-layouts: none -> 6.51 us  [on_device(): jnp.dot(select.astype(jnp.bfloat16), full.reshape(-1, rows * width), pref...]
  transfers between devices with their start and end apart: 3 -> 3, of which waited for: 2 -> 2; matrix products, arithmetic and copies ran while one was open for 7% -> 1% of each run, Pallas kernels for 0% -> 0%
where the time goes in v1:
time: 339 us; the launch traced here: 334 us
  waiting for transfers between devices  252 us (74%)
  blocking collectives  26.3 us (8%)
  local copies, waits for them, and re-layouts  17.4 us (5%)
  between operations  13.4 us (4%)
  matrix products  13.1 us (4%)
  starting transfers between devices  10.3 us (3%)
    reduce_scatter x1, waiting for transfers between devices, on_device(): return lax.psum_scatter(partial, 'sec', scatter_dimension=0, tiled=True)  224 us
    all_gather x1, waiting for transfers between devices, on_device(): rights = lax.all_gather(right_env, 'mpo', axis=0, tiled=True)  28.2 us
    all_gather x1, blocking collectives, on_device(): targets = lax.all_gather(target[0], 'mpo', axis=0, tiled=True).reshape(-1)  26.3 us
    all_to_all x1, starting transfers between devices, on_device(): lax.all_to_all(left_env, 'mpo', split_axis=1, concat_axis=0, tiled=True)  10.2 us
    unnamed x4, local copies, waits for them, and re-layouts  8.62 us
    dot_general x1, matrix products, on_device(): jnp.einsum('wsrc,wcd->wsrd', half, rights, preferred_element_type=jnp.flo...  7.7 us
  transfers between devices with their start and end apart: 3, of which 2 were waited for; matrix products, arithmetic and copies ran while one was open for 1% of the time, Pallas kernels for 0%

profile of v1, /device:TPU:1, one launch (start us, length us, event | category | flops | bytes accessed | tf_op | source)
XLA Modules:
  0.0 334.3 jit_solution(17519727256088023447)
XLA Ops:
  6.5 0.0 copy-start
  6.5 0.0 all-gather.3.cloned.1.call-start
  6.5 0.7 all-gather.3.cloned.1.call-update
  7.3 2.3 copy.13
  9.5 10.2 %all-to-all-start = ((bf16[4,256,256]{2,0,1:T(4,128)(2,1)}), bf16[4,256,256]{2,0,1:T(4,128)(2,1)S(1)}, u32[]{:S(2)}, u32[]{:S(2)}) async-start(bf16[4,256,256]{2,0,1:T(4,128)(2,1)} %copy.13), calls=%async_computation | async-start | bytes 1048576 | tf_op jit(solution)/shard_map/all_to_all | solution.py:11
  19.8 0.0 reduce-scatter.2.cloned.1.call-start
  19.8 0.7 bitcast_add_fusion
  20.5 26.3 %all-gather = s32[16,1,32]{2,1,0:T(1,128)S(1)} all-gather(s32[1,1,32]{2,1,0:T(1,128)S(1)} %bitcast_add_fusion), channel_id=2, replica_groups=mesh['sec'=32,'mpo'=16] {'mpo'}, dimensions={0}, use_global_device_ids=true | all-gather | bytes 2176 | tf_op jit(solution)/shard_map/all_gather | solution.py:14
  46.8 0.5 broadcast.13
  47.3 0.7 reduce.3
  48.0 0.1 eq.16
  48.1 0.0 all-to-all-done
  48.1 0.1 copy.14
  48.2 28.2 %all-gather.3.cloned.1.call-done = bf16[64,256,256]{2,1,0:T(8,128)(2,1)} async-done(((bf16[4,256,256]{2,1,0:T(8,128)(2,1)}), bf16[64,256,256]{2,1,0:T(8,128)(2,1)}) %all-gather.3.cloned.1.call-update) | async-done | bytes 8388624 | tf_op jit(solution)/shard_map/all_gather | solution.py:12
  76.4 0.0 copy-done
  76.4 7.7 %convert_bitcast_fusion = bf16[64,8,16,256]{3,2,1,0:T(8,128)(2,1)} fusion(bf16[64,256,256]{2,1,0:T(8,128)(2,1)} %all-gather.3.cloned.1.call-done, bf16[64,16,256,1]{2,1,3,0:T(8,128)(2,1)S(1)} %bitcast.40, bf16[8,256,256]{2,1,0:T(8,128)(2,1)S(1)} %copy-done), kind=kOutput, calls=%fused_computation.3 | convolution fusion | flops 2151677952 | bytes 14155776 | tf_op jit(solution)/shard_map/wsrc,wcd->wsrd/dot_general | solution.py:17
  84.1 6.3 %copy.20 = bf16[64,8,16,256]{3,1,2,0:T(8,128)(2,1)} copy(bf16[64,8,16,256]{3,2,1,0:T(8,128)(2,1)} %convert_bitcast_fusion) | data formatting | bytes 8388608
  90.4 6.5 %copy.16 = bf16[4096,512]{1,0:T(8,128)(2,1)} copy(bf16[4096,512]{0,1:T(8,128)(2,1)} %bitcast.39) | data formatting | bytes 8388608 | tf_op jit(solution)/shard_map/dot_general | solution.py:21
  96.9 5.4 %fusion.13 = f32[256,16,256]{2,0,1:T(8,128)} fusion(bf16[16,256,512]{2,1,0:T(8,128)(2,1)} %bitcast.38, s32[512]{0:T(512)S(1)} %eq.16), kind=kOutput, calls=%fused_computation.9 | convolution fusion | flops 1073872896 | bytes 8390656 | tf_op jit(solution)/shard_map/dot_general | solution.py:21
  102.3 0.0 reduce-scatter.2.cloned.1.call-update
  102.3 223.6 %reduce-scatter.2.cloned.1.call-done = f32[8,16,256]{2,0,1:T(8,128)} async-done(((f32[256,16,256]{2,0,1:T(8,128)}), f32[8,16,256]{2,0,1:T(8,128)}) %reduce-scatter.2.cloned.1.call-update) | async-done | bytes 131088 | tf_op jit(solution)/shard_map/reduce_scatter | solution.py:27
  325.9 1.6 copy.17
  (1 shorter events, 0.0 us)
Async XLA Ops:
  6.5 69.8 %copy-start = (bf16[8,256,256]{2,1,0:T(8,128)(2,1)S(1)}, bf16[8,256,256]{2,1,0:T(8,128)(2,1)}, u32[]{:S(2)}) copy-start(bf16[8,256,256]{2,1,0:T(8,128)(2,1)} %param.5) | copy-start | bytes 3145732
  6.5 69.8 %all-gather.3.cloned.1.call-start = ((), (), s32[]{:S(2)}) async-start(), calls=%async_computation.2 | async-start | bytes 8912896 | tf_op jit(solution)/shard_map/all_gather | solution.py:12
  9.5 38.5 %all-to-all-start = ((bf16[4,256,256]{2,0,1:T(4,128)(2,1)}), bf16[4,256,256]{2,0,1:T(4,128)(2,1)S(1)}, u32[]{:S(2)}, u32[]{:S(2)}) async-start(bf16[4,256,256]{2,0,1:T(4,128)(2,1)} %copy.13), calls=%async_computation | async-start | bytes 1048576 | tf_op jit(solution)/shard_map/all_to_all | solution.py:11
  19.8 306.1 %reduce-scatter.2.cloned.1.call-start = ((), (), s32[]{:S(2)}) async-start(), calls=%async_computation.3 | async-start | bytes 4325376 | tf_op jit(solution)/shard_map/reduce_scatter | solution.py:27
Sparse Core Ops, SparseCore 0:
  9.5 66.8 all-gather.2
  102.5 223.3 reduce-scatter.1

commit v2 on v1

--- a/solution.py
+++ b/solution.py
@@ -23,8 +23,10 @@
         full.reshape(-1, rows * width),
         preferred_element_type=jnp.float32,
     )
-    partial = partial.reshape(shards * sectors, rows, width)
-    return lax.psum_scatter(partial, "sec", scatter_dimension=0, tiled=True)
+    partial = partial.astype(jnp.bfloat16).reshape(shards * sectors, rows, width)
+    received = lax.all_to_all(partial, "sec", split_axis=0, concat_axis=0, tiled=True)
+    received = received.reshape(shards, sectors, rows, width)
+    return jnp.sum(received.astype(jnp.float32), axis=0)
 
 
 def solution(mesh):

time: 339 us -> 160 us (0.47)
  waiting for transfers between devices: 252 us -> 28.9 us
  blocking collectives: 26.3 us -> 85 us
  local copies, waits for them, and re-layouts: 17.4 us -> 8.03 us
  matrix products: 13.1 us -> 9.02 us
    reduce_scatter x1 -> x0, waiting for transfers between devices: 224 us -> none  [on_device(): return lax.psum_scatter(partial, 'sec', scatter_dimension=0, tiled=True)]
    all_to_all x0 -> x1, blocking collectives: none -> 58.6 us  [on_device(): lax.all_to_all(partial, 'sec', split_axis=0, concat_axis=0, tiled=True)]
    dot_general x1 -> x0, local copies, waits for them, and re-layouts: 6.51 us -> none  [on_device(): jnp.dot(select.astype(jnp.bfloat16), full.reshape(-1, rows * width), pref...]
    dot_general x1, matrix products: 5.42 us -> 1.3 us  [on_device(): jnp.dot(select.astype(jnp.bfloat16), full.reshape(-1, rows * width), pref...]
    unnamed x4 -> x5, local copies, waits for them, and re-layouts: 8.62 us -> 7.33 us
  transfers between devices with their start and end apart: 3 -> 2, of which waited for: 2 -> 1; matrix products, arithmetic and copies ran while one was open for 1% -> 3% of each run, Pallas kernels for 0% -> 0%
where the time goes in v2:
time: 160 us; the launch traced here: 157 us
  blocking collectives  85 us (53%)
  waiting for transfers between devices  28.9 us (18%)
  between operations  13.4 us (8%)
  starting transfers between devices  10.2 us (6%)
  matrix products  9.02 us (6%)
  local copies, waits for them, and re-layouts  8.03 us (5%)
  other arithmetic  2.29 us (1%)
    all_to_all x1, blocking collectives, on_device(): lax.all_to_all(partial, 'sec', split_axis=0, concat_axis=0, tiled=True)  58.6 us
    all_gather x1, waiting for transfers between devices, on_device(): rights = lax.all_gather(right_env, 'mpo', axis=0, tiled=True)  28.2 us
    all_gather x1, blocking collectives, on_device(): targets = lax.all_gather(target[0], 'mpo', axis=0, tiled=True).reshape(-1)  26.4 us
    all_to_all x1, starting transfers between devices, on_device(): lax.all_to_all(left_env, 'mpo', split_axis=1, concat_axis=0, tiled=True)  10.2 us
    dot_general x1, matrix products, on_device(): jnp.einsum('wsrc,wcd->wsrd', half, rights, preferred_element_type=jnp.flo...  7.72 us
    unnamed x5, local copies, waits for them, and re-layouts  7.33 us
  transfers between devices with their start and end apart: 2, of which 1 were waited for; matrix products, arithmetic and copies ran while one was open for 3% of the time, Pallas kernels for 0%

profile of v2, /device:TPU:1, one launch (start us, length us, event | category | flops | bytes accessed | tf_op | source)
XLA Modules:
  0.0 156.9 jit_solution(6751923599840231681)
XLA Ops:
  6.5 0.0 copy-start
  6.5 0.0 all-gather.3.cloned.1.call-start
  6.5 0.7 all-gather.3.cloned.1.call-update
  7.3 2.3 %copy.7 = bf16[4,256,256]{2,0,1:T(4,128)(2,1)} copy(bf16[4,256,256]{2,1,0:T(8,128)(2,1)} %param.6) | data formatting | bytes 1048576 | tf_op args[1]
  9.6 10.2 %all-to-all-start = ((bf16[4,256,256]{2,0,1:T(4,128)(2,1)}), bf16[4,256,256]{2,0,1:T(4,128)(2,1)S(1)}, u32[]{:S(2)}, u32[]{:S(2)}) async-start(bf16[4,256,256]{2,0,1:T(4,128)(2,1)} %copy.7), calls=%async_computation | async-start | bytes 1048576 | tf_op jit(solution)/shard_map/all_to_all | solution.py:11
  19.8 0.7 bitcast_add_fusion
  20.5 26.4 %all-gather = s32[16,1,32]{2,1,0:T(1,128)S(1)} all-gather(s32[1,1,32]{2,1,0:T(1,128)S(1)} %bitcast_add_fusion), channel_id=2, replica_groups=mesh['sec'=32,'mpo'=16] {'mpo'}, dimensions={0}, use_global_device_ids=true | all-gather | bytes 2176 | tf_op jit(solution)/shard_map/all_gather | solution.py:14
  46.8 0.5 broadcast.13
  47.3 0.7 reduce.3
  48.0 0.1 eq.16
  48.1 0.0 all-to-all-done
  48.1 0.1 copy.8
  48.2 28.2 %all-gather.3.cloned.1.call-done = bf16[64,256,256]{2,1,0:T(8,128)(2,1)} async-done(((bf16[4,256,256]{2,1,0:T(8,128)(2,1)}), bf16[64,256,256]{2,1,0:T(8,128)(2,1)}) %all-gather.3.cloned.1.call-update) | async-done | bytes 8388624 | tf_op jit(solution)/shard_map/all_gather | solution.py:12
  76.4 0.0 copy-done
  76.4 7.7 %convert_bitcast_fusion = bf16[64,8,16,256]{3,2,1,0:T(8,128)(2,1)} fusion(bf16[64,256,256]{2,1,0:T(8,128)(2,1)} %all-gather.3.cloned.1.call-done, bf16[64,16,256,1]{2,1,3,0:T(8,128)(2,1)S(1)} %bitcast.39, bf16[8,256,256]{2,1,0:T(8,128)(2,1)S(1)} %copy-done), kind=kOutput, calls=%fused_computation.5 | convolution fusion | flops 2151677952 | bytes 14155776 | tf_op jit(solution)/shard_map/wsrc,wcd->wsrd/dot_general | solution.py:17
  84.1 4.4 %copy.12 = bf16[64,8,16,256]{3,1,2,0:T(8,128)(2,1)S(1)} copy(bf16[64,8,16,256]{3,2,1,0:T(8,128)(2,1)} %convert_bitcast_fusion) | data formatting | bytes 8388608
  88.5 1.3 convolution_convert_fusion
  89.8 0.6 copy.13
  90.4 58.6 %all_to_all.23 = bf16[256,16,256]{2,1,0:T(8,128)(2,1)S(1)} all-to-all(bf16[256,16,256]{2,1,0:T(8,128)(2,1)S(1)} %bitcast.36), channel_id=1, replica_groups=mesh['sec'=32,'mpo'=16] {'sec'}, dimensions={0} | all-to-all | bytes 4194304 | tf_op jit(solution)/shard_map/all_to_all | solution.py:27
  149.1 0.9 convert_reduce_fusion
  (1 shorter events, 0.0 us)
Async XLA Ops:
  6.5 69.8 %copy-start = (bf16[8,256,256]{2,1,0:T(8,128)(2,1)S(1)}, bf16[8,256,256]{2,1,0:T(8,128)(2,1)}, u32[]{:S(2)}) copy-start(bf16[8,256,256]{2,1,0:T(8,128)(2,1)} %param.5) | copy-start | bytes 3145732
  6.5 69.8 %all-gather.3.cloned.1.call-start = ((), (), s32[]{:S(2)}) async-start(), calls=%async_computation.2 | async-start | bytes 8912896 | tf_op jit(solution)/shard_map/all_gather | solution.py:12
  9.6 38.5 %all-to-all-start = ((bf16[4,256,256]{2,0,1:T(4,128)(2,1)}), bf16[4,256,256]{2,0,1:T(4,128)(2,1)S(1)}, u32[]{:S(2)}, u32[]{:S(2)}) async-start(bf16[4,256,256]{2,0,1:T(4,128)(2,1)} %copy.7), calls=%async_computation | async-start | bytes 1048576 | tf_op jit(solution)/shard_map/all_to_all | solution.py:11
Sparse Core Ops, SparseCore 0:
  9.5 66.8 all-gather.2

commit v3 on v1

v3 whole, which is shorter than its diff:
```python
import jax
import jax.numpy as jnp
from jax import lax
from jax.experimental import pallas as pl
from jax.experimental.pallas import tpu as pltpu
from jax.sharding import Mesh
from jax.sharding import PartitionSpec as P

X, Z, Y, C = 4, 8, 8, 2
SEC, MPO = ("x", "z"), ("y", "c")
BF16, F32 = jnp.bfloat16, jnp.float32
TAG_ROWS = 16
CAP = 2


def half_kernel(packet_ref, psi_ref, half_ref):
    shards, _, width = packet_ref.shape
    terms, _, rows, _ = half_ref.shape
    lefts = packet_ref[:, : terms // shards * rows, :].reshape(terms * rows, width)
    out = jnp.dot(lefts, psi_ref[0], preferred_element_type=F32).astype(BF16)
    half_ref[:, 0] = out.reshape(terms, rows, width)


def halves(packet, psi, terms, rows):
    count, width = psi.shape[:2]
    return pl.pallas_call(
        half_kernel,
        grid=(count,),
        in_specs=[
            pl.BlockSpec(packet.shape, lambda s: (0, 0, 0)),
            pl.BlockSpec((1, width, width), lambda s: (s, 0, 0)),
        ],
        out_specs=pl.BlockSpec((terms, 1, rows, width), lambda s: (0, s, 0, 0)),
        out_shape=jax.ShapeDtypeStruct((terms, count, rows, width), BF16),
        compiler_params=pltpu.CompilerParams(vmem_limit_bytes=32 << 20),
        cost_estimate=pl.CostEstimate(
            flops=2 * terms * rows * width * width * count,
            bytes_accessed=2 * count * width * (width + terms * rows),
            transcendentals=0,
        ),
        name="halves",
    )(packet, psi)


def sums_kernel(pair_ref, slot_ref, *refs):
    half_refs, (right_ref, out_ref, full_ref, total_ref) = refs[:-4], refs[-4:]
    step = pl.program_id(0)
    terms = right_ref.shape[0]
    rows, width = out_ref.shape[1:]
    sectors = full_ref.shape[0] // terms
    limit = pair_ref.shape[1]

    @pl.when(step == 0)
    def _():
        total_ref[...] = jnp.zeros_like(total_ref)

    for w in range(terms):
        at = w * sectors
        for half_ref in half_refs:
            count = half_ref.shape[1]
            lhs = half_ref[w].reshape(count * rows, width)
            full = jnp.dot(lhs, right_ref[w], preferred_element_type=F32).astype(BF16)
            full_ref[at : at + count] = full.astype(F32).reshape(count, rows, width)
            at += count
    for i in range(limit):
        total_ref[slot_ref[step, i]] += full_ref[pair_ref[step, i]]

    @pl.when(step == pl.num_programs(0) - 1)
    def _():
        out_ref[...] = total_ref[: out_ref.shape[0]].astype(BF16)


def sums(pairs, slots, halves_of, rights, shards, count):
    terms, _, rows, width = halves_of[0].shape
    each = terms // shards
    sectors = sum(h.shape[1] for h in halves_of)
    return pl.pallas_call(
        sums_kernel,
        grid_spec=pltpu.PrefetchScalarGridSpec(
            num_scalar_prefetch=2,
            grid=(shards,),
            in_specs=[
                pl.BlockSpec((each, h.shape[1], rows, width), lambda i, *_: (i, 0, 0, 0))
                for h in halves_of
            ]
            + [pl.BlockSpec((each, width, width), lambda i, *_: (i, 0, 0))],
            out_specs=pl.BlockSpec((count, rows, width), lambda i, *_: (0, 0, 0)),
            scratch_shapes=[
                pltpu.VMEM((each * sectors, rows, width), F32),
                pltpu.VMEM((count + 1, rows, width), F32),
            ],
        ),
        out_shape=jax.ShapeDtypeStruct((count, rows, width), BF16),
        compiler_params=pltpu.CompilerParams(vmem_limit_bytes=48 << 20),
        cost_estimate=pl.CostEstimate(
            flops=2 * terms * sectors * rows * width * width,
            bytes_accessed=2 * terms * width * (sectors * rows + width),
            transcendentals=0,
        ),
        name="sums",
    )(pairs, slots, *halves_of, rights)


def moved(block, axis, size, by):
    return lax.ppermute(block, axis, [(i, (i + by) % size) for i in range(size)])


def both_ways(block, axis, size, by):
    pairs = []
    for i in range(size):
        pairs.append((i * C, (i + by) % size * C))
        pairs.append((i * C + 1, (i - by) % size * C + 1))
    return lax.ppermute(block, (axis, "c"), pairs)


def added(parts):
    total = parts[0].astype(F32)
    for i in range(1, parts.shape[0]):
        total = total + parts[i].astype(F32)
    return total


def ending_here(targets, first, count, limit):
    number = targets.shape[1]
    here = (targets >= first) & (targets < first + count)
    before = jnp.arange(number)[:, None] < jnp.arange(number)[None, :]
    rank = jnp.dot(
        here.astype(BF16), before.astype(BF16), preferred_element_type=F32
    ).astype(jnp.int32)
    rank = jnp.where(here, rank, limit)
    chosen = rank[:, None, :] == jnp.arange(limit, dtype=jnp.int32)[None, :, None]
    pairs = jnp.sum(jnp.where(chosen, jnp.arange(number, dtype=jnp.int32), 0), axis=2)
    slots = jnp.sum(jnp.where(chosen, (targets - first - count)[:, None, :], 0), axis=2) + count
    return pairs, slots


def on_device(psi_blocks, left_env, right_env, dest_index, dest_slot):
    sectors, width = psi_blocks.shape[:2]
    terms = left_env.shape[0]
    shards = Y * C
    rows = width // shards
    part = sectors // C
    x, core = lax.axis_index("x"), lax.axis_index("c")
    rights = lax.all_gather(right_env, MPO, axis=0, tiled=True)
    psi_next = both_ways(psi_blocks, "x", X, 1)
    psi_far = both_ways(lax.dynamic_slice_in_dim(psi_blocks, core * part, part, 0), "x", X, 2)
    psi_a = jnp.concatenate([psi_next, psi_far])
    psi_b = moved(psi_a, "c", C, 1)
    target = (dest_index[0, 0, :, 0] * sectors + dest_slot[0, 0])[None]
    tags = [target] + [moved(target, "x", X, by) for by in (1, 2, -1)]
    tags = jnp.concatenate(tags, axis=1).astype(BF16)
    tags = jnp.pad(tags, ((0, TAG_ROWS - 1), (0, width - tags.shape[1])))
    left = left_env.reshape(terms, shards, rows, width).transpose(1, 0, 2, 3)
    packet = jnp.concatenate(
        [
            left.reshape(shards, terms * rows, width),
            jnp.broadcast_to(tags[None], (shards, TAG_ROWS, width)),
        ],
        axis=1,
    )
    packet = lax.all_to_all(packet, MPO, split_axis=0, concat_axis=0, tiled=True)
    tags = packet[:, terms * rows, : X * terms * sectors].astype(jnp.int32)
    own, behind, far, ahead = (
        tags.reshape(shards, X, terms, sectors)[:, i] for i in range(X)
    )
    first = core == 0
    tags = jnp.concatenate(
        [
            own,
            jnp.where(first, behind, ahead),
            jnp.where(first, far[..., :part], far[..., part:]),
            jnp.where(first, ahead, behind),
            jnp.where(first, far[..., part:], far[..., :part]),
        ],
        axis=2,
    ).reshape(shards, terms * X * sectors)
    count = Z * sectors
    pairs, slots = ending_here(tags, x * count, count, X * Z * CAP)
    held = [halves(packet, p, shards * terms, rows) for p in (psi_blocks, psi_a, psi_b)]
    partial = sums(pairs, slots, held, rights, shards, count)
    partial = partial.reshape(Z, sectors, rows, width)
    partial = lax.all_to_all(partial, "z", split_axis=0, concat_axis=0, tiled=True)
    return added(partial)


def solution(mesh):
    chips = Mesh(mesh.devices.reshape(X, Z, Y, C), (*SEC, *MPO))
    in_specs = (
        P(SEC, None, None),
        P(MPO, None, None),
        P(MPO, None, None),
        P(MPO, SEC, None, None),
        P(MPO, SEC, None),
    )
    out_specs = P(SEC, MPO, None)
    return jax.shard_map(
        on_device, mesh=chips, in_specs=in_specs, out_specs=out_specs, check_vma=False
    )
```

time: 339 us -> 142 us (0.42); the launches traced: 334 us -> 141 us
  waiting for transfers between devices: 252 us -> 21 us
  Pallas kernels: 0 us -> 33.9 us
  starting transfers between devices: 10.3 us -> 30.2 us
  matrix products: 13.1 us -> 0.18 us
    reduce_scatter x1 -> x0, waiting for transfers between devices: 224 us -> none  [on_device(): return lax.psum_scatter(partial, 'sec', scatter_dimension=0, tiled=True)]
    pallas_call x0 -> x4, Pallas kernels: none -> 33.9 us  [the longest x1 19.3 us: sums(): pl.pallas_call(sums_kernel, grid_spec=pltpu.PrefetchScalarGridSpec(num_sc...]
    all_gather x1 -> x0, blocking collectives: 26.3 us -> none  [on_device(): targets = lax.all_gather(target[0], 'mpo', axis=0, tiled=True).reshape(-1)]
    all_to_all x0 -> x1, blocking collectives: none -> 24.3 us  [on_device(): lax.all_to_all(partial, 'z', split_axis=0, concat_axis=0, tiled=True)]
    all_gather x1, waiting for transfers between devices: 28.2 us -> 5.22 us  [on_device(): rights = lax.all_gather(right_env, MPO, axis=0, tiled=True)]
    ppermute x0 -> x6, starting transfers between devices: none -> 21 us  [the longest x4 15.9 us: moved(): lax.ppermute(block, axis, [(i, (i + by) % size) for i in range(size)])]
    ppermute x0 -> x6, waiting for transfers between devices: none -> 13.3 us  [the longest x2 13.3 us: both_ways(): return lax.ppermute(block, (axis, 'c'), pairs)]
    dot_general x2 -> x1, matrix products: 13.1 us -> 0.18 us  [ending_here(): jnp.dot(here.astype(BF16), before.astype(BF16), preferred_element_type=F32)]
  transfers between devices with their start and end apart: 3 -> 8, of which waited for: 2 -> 3; matrix products, arithmetic and copies ran while one was open for 1% -> 6% of each run, Pallas kernels for 0% -> 10%
where the time goes in v3:
time: 142 us; the launch traced here: 141 us
  Pallas kernels  33.9 us (24%)
  starting transfers between devices  30.2 us (21%)
  blocking collectives  24.3 us (17%)
  waiting for transfers between devices  21 us (15%)
  local copies, waits for them, and re-layouts  14.1 us (10%)
  between operations  13.6 us (10%)
  other arithmetic  3.75 us (3%)
    all_to_all x1, blocking collectives, on_device(): lax.all_to_all(partial, 'z', split_axis=0, concat_axis=0, tiled=True)  24.3 us
    pallas_call x1, Pallas kernels, sums(): pl.pallas_call(sums_kernel, grid_spec=pltpu.PrefetchScalarGridSpec(num_sc...  19.3 us
    ppermute x4, starting transfers between devices, moved(): lax.ppermute(block, axis, [(i, (i + by) % size) for i in range(size)])  15.9 us
    pallas_call x3, Pallas kernels, halves(): pl.pallas_call(half_kernel, grid=(count,), in_specs=[pl.BlockSpec(packet....  14.6 us
    ppermute x2, waiting for transfers between devices, both_ways(): return lax.ppermute(block, (axis, 'c'), pairs)  13.3 us
    unnamed x11, local copies, waits for them, and re-layouts  10.7 us
    all_to_all x1, starting transfers between devices, on_device(): lax.all_to_all(packet, MPO, split_axis=0, concat_axis=0, tiled=True)  9.21 us
    all_gather x1, waiting for transfers between devices, on_device(): rights = lax.all_gather(right_env, MPO, axis=0, tiled=True)  5.22 us
  transfers between devices with their start and end apart: 8, of which 3 were waited for; matrix products, arithmetic and copies ran while one was open for 6% of the time, Pallas kernels for 10%

profile of v3, /device:TPU:1, one launch (start us, length us, event | category | flops | bytes accessed | tf_op | source)
XLA Modules:
  0.0 141.1 jit_solution(8384290063869470820)
XLA Ops:
  6.5 0.7 all-gather.2.cloned.1.call-update
  7.3 0.7 bitcast_add_fusion
  7.9 3.9 %collective-permute-start = (s32[1,32]{1,0:T(1,128)S(1)}, s32[1,32]{1,0:T(1,128)S(1)}, u32[]{:S(2)}, u32[]{:S(2)}) collective-permute-start(s32[1,32]{1,0:T(1,128)S(1)} %bitcast_add_fusion), channel_id=1, source_target_pairs={{0,128},{128,256},{256,384},{384,0},{1,129},{129,257},{257,385},{3... | collective-permute-start | bytes 392 | tf_op jit(solution)/shard_map/ppermute | solution.py:105
  11.9 4.4 %collective-permute-start.1 = (s32[1,32]{1,0:T(1,128)S(1)}, s32[1,32]{1,0:T(1,128)S(1)}, u32[]{:S(2)}, u32[]{:S(2)}) collective-permute-start(s32[1,32]{1,0:T(1,128)S(1)} %bitcast_add_fusion), channel_id=1, source_target_pairs={{0,256},{128,384},{256,0},{384,128},{1,257},{129,385},{257,1},{385... | collective-permute-start | bytes 392 | tf_op jit(solution)/shard_map/ppermute | solution.py:105
  16.2 3.1 %collective-permute-start.2 = (s32[1,32]{1,0:T(1,128)S(1)}, s32[1,32]{1,0:T(1,128)S(1)}, u32[]{:S(2)}, u32[]{:S(2)}) collective-permute-start(s32[1,32]{1,0:T(1,128)S(1)} %bitcast_add_fusion), channel_id=1, source_target_pairs={{0,384},{128,0},{256,128},{384,256},{1,385},{129,1},{257,129},{385... | collective-permute-start | bytes 392 | tf_op jit(solution)/shard_map/ppermute | solution.py:105
  19.3 1.9 %collective-permute-start.3 = (bf16[8,256,256]{2,1,0:T(8,128)(2,1)}, bf16[8,256,256]{2,1,0:T(8,128)(2,1)}, u32[]{:S(2)}, u32[]{:S(2)}) collective-permute-start(bf16[8,256,256]{2,1,0:T(8,128)(2,1)} %psi_ref.1), channel_id=1, source_target_pairs={{0,128},{1,385},{128,256},{129,1},{256,384},{257,129},{384,0},{385... | collective-permute-start | bytes 3145736 | tf_op jit(solution)/shard_map/ppermute | solution.py:113
  21.2 0.7 fusion.14
  21.9 1.1 copy.24
  23.2 0.9 pad_maximum_fusion
  24.1 9.2 %all-to-all-start = ((bf16[16,80,256]{2,1,0:T(8,128)(2,1)}), bf16[16,80,256]{2,1,0:T(8,128)(2,1)S(1)}, u32[]{:S(2)}, u32[]{:S(2)}) async-start(bf16[16,80,256]{2,1,0:T(8,128)(2,1)} %pad_maximum_fusion), calls=%async_computation | async-start | bytes 1310720 | tf_op jit(solution)/shard_map/all_to_all | solution.py:161
  33.3 0.9 constant_dynamic-slice_fusion
  34.1 3.2 %collective-permute-start.4 = (bf16[4,256,256]{2,1,0:T(8,128)(2,1)}, bf16[4,256,256]{2,1,0:T(8,128)(2,1)}, u32[]{:S(2)}, u32[]{:S(2)}) collective-permute-start(bf16[4,256,256]{2,1,0:T(8,128)(2,1)} %constant_dynamic-slice_fusion), channel_id=1, source_target_pairs={{0,256},{1,257},{128,384},{129,385},{256,0},{257,1},{384,128},{385... | collective-permute-start | bytes 1572872 | tf_op jit(solution)/shard_map/ppermute | solution.py:113
  37.4 1.3 constant_dynamic-update-slice_fusion.1
  38.7 13.3 %collective-permute-done.4 = bf16[4,256,256]{2,1,0:T(8,128)(2,1)} collective-permute-done((bf16[4,256,256]{2,1,0:T(8,128)(2,1)}, bf16[4,256,256]{2,1,0:T(8,128)(2,1)}, u32[]{:S(2)}, u32[]{:S(2)}) %collective-permute-start.4) | collective-permute-done | bytes 524320 | tf_op jit(solution)/shard_map/ppermute | solution.py:113
  51.9 1.1 constant_dynamic-update-slice_fusion.psi_ref
  53.0 4.5 %collective-permute-start.5 = (bf16[12,256,256]{2,1,0:T(8,128)(2,1)S(1)}, bf16[12,256,256]{2,1,0:T(8,128)(2,1)}, u32[]{:S(2)}, u32[]{:S(2)}) collective-permute-start(bf16[12,256,256]{2,1,0:T(8,128)(2,1)S(1)} %constant_dynamic-update-slice_fusion.psi_ref), channel_id=1, source_target_pairs={{0,1},{1,0},{2,3},{3,2},{4,5},{5,4},{6,7},{7,6},{8,9},{9,8},{10,11... | collective-permute-start | bytes 4718600 | tf_op jit(solution)/shard_map/ppermute | solution.py:105
  57.6 1.8 %all-to-all-done.packet_ref = bf16[16,80,256]{2,1,0:T(8,128)(2,1)S(1)} async-done(((bf16[16,80,256]{2,1,0:T(8,128)(2,1)}), bf16[16,80,256]{2,1,0:T(8,128)(2,1)S(1)}, u32[]{:S(2)}, u32[]{:S(2)}) %all-to-all-start) | async-done | bytes 655392 | tf_op jit(solution)/shard_map/all_to_all | solution.py:161
  59.4 0.1 copy.25
  59.5 0.1 concatenate.26
  59.8 2.7 %halves.3.refs_0_ = bf16[64,8,16,256]{3,2,1,0:T(8,128)(2,1)S(1)} custom-call(bf16[16,80,256]{2,1,0:T(8,128)(2,1)S(1)} %all-to-all-done.packet_ref, bf16[8,256,256]{2,1,0:T(8,128)(2,1)S(1)} %copy-done.4), custom_call_target="tpu_custom_call" | custom-call | flops 1073741824 | bytes 5242880 | tf_op jit(solution)/shard_map/halves/pallas_call | solution.py:26
  62.5 2.0 %copy-done.2 = bf16[64,8,16,256]{3,2,1,0:T(8,128)(2,1)} copy-done((bf16[64,8,16,256]{3,2,1,0:T(8,128)(2,1)}, bf16[64,8,16,256]{3,2,1,0:T(8,128)(2,1)S(1)}, u32[]{:S(2)}) %copy-start.2) | copy-done | bytes 4194328
  64.5 0.2 fusion
  64.7 0.6 select_reduce_fusion
  65.3 4.0 %halves.4.refs_1_ = bf16[64,12,16,256]{3,2,1,0:T(8,128)(2,1)S(1)} custom-call(bf16[16,80,256]{2,1,0:T(8,128)(2,1)S(1)} %all-to-all-done.packet_ref, bf16[12,256,256]{2,1,0:T(8,128)(2,1)S(1)} %constant_dynamic-update-slice_fusion.psi_ref), custom_call_target="tpu_custom_call" | custom-call | flops 1610612736 | bytes 7864320 | tf_op jit(solution)/shard_map/halves/pallas_call | solution.py:26
  69.3 2.7 %copy-done = bf16[64,12,16,256]{3,2,1,0:T(8,128)(2,1)} copy-done((bf16[64,12,16,256]{3,2,1,0:T(8,128)(2,1)}, bf16[64,12,16,256]{3,2,1,0:T(8,128)(2,1)S(1)}, u32[]{:S(2)}) %copy-start) | copy-done | bytes 6291480
  72.0 7.9 %halves.5.refs_2_ = bf16[64,12,16,256]{3,2,1,0:T(8,128)(2,1)S(1)} custom-call(bf16[16,80,256]{2,1,0:T(8,128)(2,1)S(1)} %all-to-all-done.packet_ref, bf16[12,256,256]{2,1,0:T(8,128)(2,1)} %collective-permute-done.5.psi_ref), custom_call_target="tpu_custom_call" | custom-call | flops 1610612736 | bytes 7864320 | tf_op jit(solution)/shard_map/halves/pallas_call | solution.py:26
  79.9 2.6 %copy-done.1 = bf16[64,12,16,256]{3,2,1,0:T(8,128)(2,1)} copy-done((bf16[64,12,16,256]{3,2,1,0:T(8,128)(2,1)}, bf16[64,12,16,256]{3,2,1,0:T(8,128)(2,1)S(1)}, u32[]{:S(2)}) %copy-start.1) | copy-done | bytes 6291480
  82.5 5.2 %all-gather.2.cloned.1.call-done.refs_3_ = bf16[64,256,256]{2,1,0:T(8,128)(2,1)} async-done(((bf16[4,256,256]{2,1,0:T(8,128)(2,1)}), bf16[64,256,256]{2,1,0:T(8,128)(2,1)}) %all-gather.2.cloned.1.call-update) | async-done | bytes 8388624 | tf_op jit(solution)/shard_map/all_gather | solution.py:144
  87.7 2.2 %copy-done.3 = bf16[64,8,16,256]{3,2,1,0:T(8,128)(2,1)S(1)} copy-done((bf16[64,8,16,256]{3,2,1,0:T(8,128)(2,1)S(1)}, bf16[64,8,16,256]{3,2,1,0:T(8,128)(2,1)}, u32[]{:S(2)}) %copy-start.3) | copy-done | bytes 4194328
  89.9 19.3 %sums.1 = bf16[64,16,256]{2,1,0:T(8,128)(2,1)S(1)} custom-call(s32[16,64]{1,0:T(8,128)S(1)} %get-tuple-element.6.pair_ref, s32[16,64]{1,0:T(8,128)S(1)} %broadcast_add_fusion.slot_ref, bf16[64,8,16,256]{3,2,1,0:T(8,128)(2,1)S(1)} %copy-done.3, bf16[64,12,16,256]{3,2,1,0:T(8,128)(2,1)} %copy-done, bf16[64,12,16,256]{3,2,1,0:T(8,128)(2,1)} %copy-done.1, ...), custom_call_target="tpu_custom_call" | custom-call | flops 4294967296 | bytes 25165824 | tf_op jit(solution)/shard_map/sums/pallas_call | solution.py:77
  109.2 24.3 %all_to_all.10 = bf16[8,8,16,256]{3,2,1,0:T(8,128)(2,1)S(1)} all-to-all(bf16[8,8,16,256]{3,2,1,0:T(8,128)(2,1)S(1)} %bitcast.33), channel_id=1, replica_groups=mesh['x'=4,'z'=8,'y'=8,'c'=2] {'z'}, dimensions={0} | all-to-all | bytes 1048576 | tf_op jit(solution)/shard_map/all_to_all | solution.py:182
  133.5 0.7 add_bitcast_fusion
  (25 shorter events, 0.3 us)
Async XLA Ops:
  6.5 81.1 %all-gather.2.cloned.1.call-start = ((), (), s32[]{:S(2)}) async-start(), calls=%async_computation.2 | async-start | bytes 8912896 | tf_op jit(solution)/shard_map/all_gather | solution.py:144
  7.9 15.1 %collective-permute-start = (s32[1,32]{1,0:T(1,128)S(1)}, s32[1,32]{1,0:T(1,128)S(1)}, u32[]{:S(2)}, u32[]{:S(2)}) collective-permute-start(s32[1,32]{1,0:T(1,128)S(1)} %bitcast_add_fusion), channel_id=1, source_target_pairs={{0,128},{128,256},{256,384},{384,0},{1,129},{129,257},{257,385},{3... | collective-permute-start | bytes 392 | tf_op jit(solution)/shard_map/ppermute | solution.py:105
  11.9 11.2 %collective-permute-start.1 = (s32[1,32]{1,0:T(1,128)S(1)}, s32[1,32]{1,0:T(1,128)S(1)}, u32[]{:S(2)}, u32[]{:S(2)}) collective-permute-start(s32[1,32]{1,0:T(1,128)S(1)} %bitcast_add_fusion), channel_id=1, source_target_pairs={{0,256},{128,384},{256,0},{384,128},{1,257},{129,385},{257,1},{385... | collective-permute-start | bytes 392 | tf_op jit(solution)/shard_map/ppermute | solution.py:105
  16.2 6.8 %collective-permute-start.2 = (s32[1,32]{1,0:T(1,128)S(1)}, s32[1,32]{1,0:T(1,128)S(1)}, u32[]{:S(2)}, u32[]{:S(2)}) collective-permute-start(s32[1,32]{1,0:T(1,128)S(1)} %bitcast_add_fusion), channel_id=1, source_target_pairs={{0,384},{128,0},{256,128},{384,256},{1,385},{129,1},{257,129},{385... | collective-permute-start | bytes 392 | tf_op jit(solution)/shard_map/ppermute | solution.py:105
  19.3 18.0 %collective-permute-start.3 = (bf16[8,256,256]{2,1,0:T(8,128)(2,1)}, bf16[8,256,256]{2,1,0:T(8,128)(2,1)}, u32[]{:S(2)}, u32[]{:S(2)}) collective-permute-start(bf16[8,256,256]{2,1,0:T(8,128)(2,1)} %psi_ref.1), channel_id=1, source_target_pairs={{0,128},{1,385},{128,256},{129,1},{256,384},{257,129},{384,0},{385... | collective-permute-start | bytes 3145736 | tf_op jit(solution)/shard_map/ppermute | solution.py:113
  23.0 10.3 %copy-start.4 = (bf16[8,256,256]{2,1,0:T(8,128)(2,1)S(1)}, bf16[8,256,256]{2,1,0:T(8,128)(2,1)}, u32[]{:S(2)}) copy-start(bf16[8,256,256]{2,1,0:T(8,128)(2,1)} %psi_ref.1) | copy-start | bytes 3145732
  24.1 35.3 %all-to-all-start = ((bf16[16,80,256]{2,1,0:T(8,128)(2,1)}), bf16[16,80,256]{2,1,0:T(8,128)(2,1)S(1)}, u32[]{:S(2)}, u32[]{:S(2)}) async-start(bf16[16,80,256]{2,1,0:T(8,128)(2,1)} %pad_maximum_fusion), calls=%async_computation | async-start | bytes 1310720 | tf_op jit(solution)/shard_map/all_to_all | solution.py:161
  34.1 17.8 %collective-permute-start.4 = (bf16[4,256,256]{2,1,0:T(8,128)(2,1)}, bf16[4,256,256]{2,1,0:T(8,128)(2,1)}, u32[]{:S(2)}, u32[]{:S(2)}) collective-permute-start(bf16[4,256,256]{2,1,0:T(8,128)(2,1)} %constant_dynamic-slice_fusion), channel_id=1, source_target_pairs={{0,256},{1,257},{128,384},{129,385},{256,0},{257,1},{384,128},{385... | collective-permute-start | bytes 1572872 | tf_op jit(solution)/shard_map/ppermute | solution.py:113
  53.0 19.0 %collective-permute-start.5 = (bf16[12,256,256]{2,1,0:T(8,128)(2,1)S(1)}, bf16[12,256,256]{2,1,0:T(8,128)(2,1)}, u32[]{:S(2)}, u32[]{:S(2)}) collective-permute-start(bf16[12,256,256]{2,1,0:T(8,128)(2,1)S(1)} %constant_dynamic-update-slice_fusion.psi_ref), channel_id=1, source_target_pairs={{0,1},{1,0},{2,3},{3,2},{4,5},{5,4},{6,7},{7,6},{8,9},{9,8},{10,11... | collective-permute-start | bytes 4718600 | tf_op jit(solution)/shard_map/ppermute | solution.py:105
  62.5 2.0 %copy-start.2 = (bf16[64,8,16,256]{3,2,1,0:T(8,128)(2,1)}, bf16[64,8,16,256]{3,2,1,0:T(8,128)(2,1)S(1)}, u32[]{:S(2)}) copy-start(bf16[64,8,16,256]{3,2,1,0:T(8,128)(2,1)S(1)} %halves.3.refs_0_) | copy-start | bytes 12582916
  69.3 2.7 %copy-start = (bf16[64,12,16,256]{3,2,1,0:T(8,128)(2,1)}, bf16[64,12,16,256]{3,2,1,0:T(8,128)(2,1)S(1)}, u32[]{:S(2)}) copy-start(bf16[64,12,16,256]{3,2,1,0:T(8,128)(2,1)S(1)} %halves.4.refs_1_) | copy-start | bytes 18874372
  79.9 2.6 %copy-start.1 = (bf16[64,12,16,256]{3,2,1,0:T(8,128)(2,1)}, bf16[64,12,16,256]{3,2,1,0:T(8,128)(2,1)S(1)}, u32[]{:S(2)}) copy-start(bf16[64,12,16,256]{3,2,1,0:T(8,128)(2,1)S(1)} %halves.5.refs_2_) | copy-start | bytes 18874372
  87.7 2.2 %copy-start.3 = (bf16[64,8,16,256]{3,2,1,0:T(8,128)(2,1)S(1)}, bf16[64,8,16,256]{3,2,1,0:T(8,128)(2,1)}, u32[]{:S(2)}) copy-start(bf16[64,8,16,256]{3,2,1,0:T(8,128)(2,1)} %copy-done.2) | copy-start | bytes 12582916
Sparse Core Ops, SparseCore 0:
  9.5 78.1 all-gather.1

commit v4 on v3

v4 whole, which is shorter than its diff:
```python
import jax
import jax.numpy as jnp
from jax import lax
from jax.experimental import pallas as pl
from jax.experimental.pallas import tpu as pltpu
from jax.sharding import Mesh
from jax.sharding import PartitionSpec as P

XB, XA, Z, Y, C = 2, 2, 8, 8, 2
X = XB * XA
AXIS_X, SEC, MPO = ("xb", "xa"), ("xb", "xa", "z"), ("y", "c")
BF16, F32 = jnp.bfloat16, jnp.float32
TAG_ROWS = 16


def half_kernel(packet_ref, psi_ref, *refs):
    half_ref = refs[-1]
    shards, _, width = packet_ref.shape
    terms, _, rows, _ = half_ref.shape
    lefts = packet_ref[:, : terms // shards * rows, :].reshape(terms * rows, width)
    out = jnp.dot(lefts, psi_ref[0], preferred_element_type=F32).astype(BF16)
    half_ref[:, 0] = out.reshape(terms, rows, width)


def halves(packet, psi, into, at, shape):
    terms, _, rows, width = shape
    count = psi.shape[0]
    before = [] if into is None else [into]
    return pl.pallas_call(
        half_kernel,
        grid=(count,),
        in_specs=[
            pl.BlockSpec(packet.shape, lambda s: (0, 0, 0)),
            pl.BlockSpec((1, width, width), lambda s: (s, 0, 0)),
        ]
        + [pl.BlockSpec(memory_space=pl.ANY) for _ in before],
        out_specs=pl.BlockSpec((terms, 1, rows, width), lambda s: (0, s + at, 0, 0)),
        out_shape=jax.ShapeDtypeStruct(shape, BF16),
        input_output_aliases={2: 0} if before else {},
        compiler_params=pltpu.CompilerParams(vmem_limit_bytes=56 << 20),
        cost_estimate=pl.CostEstimate(
            flops=2 * terms * rows * width * width * count,
            bytes_accessed=2 * count * width * (width + terms * rows),
            transcendentals=0,
        ),
        name="halves",
    )(packet, psi, *before)


def sums_kernel(place_ref, tag_ref, half_ref, right_ref, out_ref, total_ref):
    step = pl.program_id(0)
    terms, sectors, rows, width = half_ref.shape
    xb, core = place_ref[0], place_ref[1]
    count = out_ref.shape[0]
    each = sectors // X
    part = each // C
    near, away = 1 + 2 * core, 3 - 2 * core
    runs = (
        (each, 0, 0),
        (each, near, 0),
        (part, 2, core * part),
        (each, away, 0),
        (part, 2, (1 - core) * part),
    )

    @pl.when(step == 0)
    def _():
        total_ref[...] = jnp.zeros_like(total_ref)

    for w in range(terms):
        lhs = half_ref[w].reshape(sectors * rows, width)
        full = jnp.dot(lhs, right_ref[w], preferred_element_type=F32).astype(BF16)
        full = full.astype(F32).reshape(sectors, rows, width)
        s = 0
        for length, shard, first in runs:
            for k in range(length):
                t = tag_ref[step, (shard * terms + w) * each + first + k] - xb * count
                total_ref[jnp.where((t >= 0) & (t < count), t, count)] += full[s]
                s += 1

    @pl.when(step == pl.num_programs(0) - 1)
    def _():
        out_ref[...] = total_ref[:count].astype(BF16)


def sums(place, tags, half, rights, count):
    terms, sectors, rows, width = half.shape
    steps = tags.shape[0]
    each = terms // steps
    return pl.pallas_call(
        sums_kernel,
        grid_spec=pltpu.PrefetchScalarGridSpec(
            num_scalar_prefetch=2,
            grid=(steps,),
            in_specs=[
                pl.BlockSpec((each, sectors, rows, width), lambda i, *_: (i, 0, 0, 0)),
                pl.BlockSpec((each, width, width), lambda i, *_: (i, 0, 0)),
            ],
            out_specs=pl.BlockSpec((count, rows, width), lambda i, *_: (0, 0, 0)),
            scratch_shapes=[pltpu.VMEM((count + 1, rows, width), F32)],
        ),
        out_shape=jax.ShapeDtypeStruct((count, rows, width), BF16),
        compiler_params=pltpu.CompilerParams(vmem_limit_bytes=56 << 20),
        cost_estimate=pl.CostEstimate(
            flops=2 * terms * sectors * rows * width * width,
            bytes_accessed=2 * terms * width * (sectors * rows + width),
            transcendentals=0,
        ),
        name="sums",
    )(place, tags, half, rights)


def moved(block, axis, size, by):
    return lax.ppermute(block, axis, [(i, (i + by) % size) for i in range(size)])


def both_ways(block, by):
    pairs = []
    for i in range(X):
        pairs.append((i * C, (i + by) % X * C))
        pairs.append((i * C + 1, (i - by) % X * C + 1))
    return lax.ppermute(block, (*AXIS_X, "c"), pairs)


def added(parts):
    total = parts[0].astype(F32)
    for i in range(1, parts.shape[0]):
        total = total + parts[i].astype(F32)
    return total


def on_device(psi_blocks, left_env, right_env, dest_index, dest_slot):
    sectors, width = psi_blocks.shape[:2]
    terms = left_env.shape[0] // XA
    shards = Y * C
    rows = width // shards
    part = sectors // C
    xb, xa, core = lax.axis_index("xb"), lax.axis_index("xa"), lax.axis_index("c")
    right = lax.dynamic_slice_in_dim(right_env, xa * terms, terms, 0)
    rights = lax.all_gather(right, MPO, axis=0, tiled=True)
    psi_next = both_ways(psi_blocks, 1)
    psi_far = both_ways(lax.dynamic_slice_in_dim(psi_blocks, core * part, part, 0), 2)
    psi_a = jnp.concatenate([psi_next, psi_far])
    psi_b = moved(psi_a, "c", C, 1)
    target = (dest_index[0, 0, :, 0] * sectors + dest_slot[0, 0])[None]
    same = lax.dynamic_slice_in_dim(target, xa * terms * sectors, terms * sectors, 1)
    other = lax.dynamic_slice_in_dim(target, (1 - xa) * terms * sectors, terms * sectors, 1)
    tags = [
        same,
        moved(other, AXIS_X, X, 1),
        moved(same, AXIS_X, X, 2),
        moved(other, AXIS_X, X, -1),
    ]
    tags = jnp.concatenate(tags, axis=1).astype(BF16)
    tags = jnp.pad(tags, ((0, TAG_ROWS - 1), (0, width - tags.shape[1])))
    left = lax.dynamic_slice_in_dim(left_env, xa * terms, terms, 0)
    left = left.reshape(terms, shards, rows, width).transpose(1, 0, 2, 3)
    packet = jnp.concatenate(
        [
            left.reshape(shards, terms * rows, width),
            jnp.broadcast_to(tags[None], (shards, TAG_ROWS, width)),
        ],
        axis=1,
    )
    packet = lax.all_to_all(packet, MPO, split_axis=0, concat_axis=0, tiled=True)
    tags = packet[:, terms * rows, : X * terms * sectors].astype(jnp.int32)
    place = jnp.stack([xb, core]).astype(jnp.int32)
    count = XA * Z * sectors
    shape = (shards * terms, X * sectors, rows, width)
    half, at = None, 0
    for psi in (psi_blocks, psi_a, psi_b):
        half = halves(packet, psi, half, at, shape)
        at += psi.shape[0]
    partial = sums(place, tags, half, rights, count)
    partial = partial.reshape(XA * Z, sectors, rows, width)
    partial = lax.all_to_all(partial, ("xa", "z"), split_axis=0, concat_axis=0, tiled=True)
    return added(partial)


def solution(mesh):
    chips = Mesh(mesh.devices.reshape(XB, XA, Z, Y, C), (*SEC, *MPO))
    in_specs = (
        P(SEC, None, None),
        P(MPO, None, None),
        P(MPO, None, None),
        P(MPO, SEC, None, None),
        P(MPO, SEC, None),
    )
    out_specs = P(SEC, MPO, None)
    return jax.shard_map(
        on_device, mesh=chips, in_specs=in_specs, out_specs=out_specs, check_vma=False
    )
```

time: 142 us -> 167 us (1.18)
  waiting for transfers between devices: 21 us -> 36.4 us
  blocking collectives: 24.3 us -> 37 us
  local copies, waits for them, and re-layouts: 14.1 us -> 4.71 us
  Pallas kernels: 33.9 us -> 40.6 us
    all_to_all x1, blocking collectives: 24.3 us -> 37 us  [on_device(): lax.all_to_all(partial, ('xa', 'z'), split_axis=0, concat_axis=0, tiled=T...]
    all_to_all x1, waiting for transfers between devices: 1.81 us -> 13.9 us  [on_device(): lax.all_to_all(packet, MPO, split_axis=0, concat_axis=0, tiled=True)]
    pallas_call x3, Pallas kernels: 14.6 us -> 24.3 us  [halves(): pl.pallas_call(half_kernel, grid=(count,), in_specs=[pl.BlockSpec(packet....]
    unnamed x11, local copies, waits for them, and re-layouts: 10.7 us -> 1.86 us
    ppermute x2, waiting for transfers between devices: 13.3 us -> 19.7 us  [both_ways(): return lax.ppermute(block, (*AXIS_X, 'c'), pairs)]
    all_gather x1, waiting for transfers between devices: 5.22 us -> 0.01 us  [on_device(): rights = lax.all_gather(right, MPO, axis=0, tiled=True)]
    all_to_all x1, starting transfers between devices: 9.21 us -> 5.06 us  [on_device(): lax.all_to_all(packet, MPO, split_axis=0, concat_axis=0, tiled=True)]
    pallas_call x1, Pallas kernels: 19.3 us -> 16.3 us  [sums(): pl.pallas_call(sums_kernel, grid_spec=pltpu.PrefetchScalarGridSpec(num_sc...]
  transfers between devices with their start and end apart: 8 -> 8, of which waited for: 3 -> 3; matrix products, arithmetic and copies ran while one was open for 6% -> 3% of each run, Pallas kernels for 10% -> 15%
where the time goes in v4:
time: 167 us; the launch traced here: 166 us
  Pallas kernels  40.6 us (24%)
  blocking collectives  37 us (22%)
  waiting for transfers between devices  36.4 us (22%)
  starting transfers between devices  30.3 us (18%)
  between operations  13.6 us (8%)
  local copies, waits for them, and re-layouts  4.71 us (3%)
  other arithmetic  3.02 us (2%)
    all_to_all x1, blocking collectives, on_device(): lax.all_to_all(partial, ('xa', 'z'), split_axis=0, concat_axis=0, tiled=T...  37 us
    pallas_call x3, Pallas kernels, halves(): pl.pallas_call(half_kernel, grid=(count,), in_specs=[pl.BlockSpec(packet....  24.3 us
    ppermute x2, waiting for transfers between devices, both_ways(): return lax.ppermute(block, (*AXIS_X, 'c'), pairs)  19.7 us
    ppermute x4, starting transfers between devices, moved(): lax.ppermute(block, axis, [(i, (i + by) % size) for i in range(size)])  17.6 us
    pallas_call x1, Pallas kernels, sums(): pl.pallas_call(sums_kernel, grid_spec=pltpu.PrefetchScalarGridSpec(num_sc...  16.3 us
    all_to_all x1, waiting for transfers between devices, on_device(): lax.all_to_all(packet, MPO, split_axis=0, concat_axis=0, tiled=True)  13.9 us
    ppermute x2, starting transfers between devices, both_ways(): return lax.ppermute(block, (*AXIS_X, 'c'), pairs)  7.65 us
    all_to_all x1, starting transfers between devices, on_device(): lax.all_to_all(packet, MPO, split_axis=0, concat_axis=0, tiled=True)  5.06 us
  transfers between devices with their start and end apart: 8, of which 3 were waited for; matrix products, arithmetic and copies ran while one was open for 3% of the time, Pallas kernels for 15%

profile of v4, /device:TPU:1, one launch (start us, length us, event | category | flops | bytes accessed | tf_op | source)
XLA Modules:
  0.0 165.7 jit_solution(934020469165833890)
XLA Ops:
  6.5 1.0 copy-done
  7.6 0.7 constant_dynamic-slice_fusion
  8.3 0.0 all-gather.2.cloned.1.call-update
  8.3 5.2 %collective-permute-start.3 = (bf16[8,256,256]{2,1,0:T(8,128)(2,1)}, bf16[8,256,256]{2,1,0:T(8,128)(2,1)S(1)}, u32[]{:S(2)}, u32[]{:S(2)}) collective-permute-start(bf16[8,256,256]{2,1,0:T(8,128)(2,1)} %psi_ref.1), channel_id=1, source_target_pairs={{0,128},{1,385},{128,256},{129,1},{256,384},{257,129},{384,0},{385... | collective-permute-start | bytes 3145736 | tf_op jit(solution)/shard_map/ppermute | solution.py:122
  13.5 1.1 constant_dynamic-slice_fusion.1
  14.6 0.0 copy-start.3
  14.6 0.0 copy-start.4
  14.7 2.4 %collective-permute-start.4 = (bf16[4,256,256]{2,1,0:T(8,128)(2,1)S(1)}, bf16[4,256,256]{2,1,0:T(8,128)(2,1)S(1)}, u32[]{:S(2)}, u32[]{:S(2)}) collective-permute-start(bf16[4,256,256]{2,1,0:T(8,128)(2,1)S(1)} %constant_dynamic-slice_fusion.1), channel_id=1, source_target_pairs={{0,256},{1,257},{128,384},{129,385},{256,0},{257,1},{384,128},{385... | collective-permute-start | bytes 1572872 | tf_op jit(solution)/shard_map/ppermute | solution.py:122
  17.1 19.7 %collective-permute-done.3 = bf16[8,256,256]{2,1,0:T(8,128)(2,1)S(1)} collective-permute-done((bf16[8,256,256]{2,1,0:T(8,128)(2,1)}, bf16[8,256,256]{2,1,0:T(8,128)(2,1)S(1)}, u32[]{:S(2)}, u32[]{:S(2)}) %collective-permute-start.3) | collective-permute-done | bytes 1048608 | tf_op jit(solution)/shard_map/ppermute | solution.py:122
  36.8 0.1 constant_dynamic-update-slice_fusion.1
  36.9 0.0 collective-permute-done.4
  36.9 9.2 %collective-permute-start.5 = (bf16[12,256,256]{2,1,0:T(8,128)(2,1)S(1)}, bf16[12,256,256]{2,1,0:T(8,128)(2,1)}, u32[]{:S(2)}, u32[]{:S(2)}) collective-permute-start(bf16[12,256,256]{2,1,0:T(8,128)(2,1)S(1)} %constant_dynamic-update-slice_fusion.psi_ref), channel_id=1, source_target_pairs={{0,1},{1,0},{2,3},{3,2},{4,5},{5,4},{6,7},{7,6},{8,9},{9,8},{10,11... | collective-permute-start | bytes 4718600 | tf_op jit(solution)/shard_map/ppermute | solution.py:114
  46.2 0.1 fusion.13
  46.3 1.9 %collective-permute-start = (s32[1,16]{1,0:T(1,128)S(1)}, s32[1,16]{1,0:T(1,128)S(1)}, u32[]{:S(2)}, u32[]{:S(2)}) collective-permute-start(s32[1,16]{1,0:T(1,128)S(1)} %get-tuple-element.7), channel_id=1, source_target_pairs={{0,128},{128,256},{256,384},{384,0},{1,129},{129,257},{257,385},{3... | collective-permute-start | bytes 200 | tf_op jit(solution)/shard_map/ppermute | solution.py:114
  48.2 4.6 %collective-permute-start.2 = (s32[1,16]{1,0:T(1,128)S(1)}, s32[1,16]{1,0:T(1,128)S(1)}, u32[]{:S(2)}, u32[]{:S(2)}) collective-permute-start(s32[1,16]{1,0:T(1,128)S(1)} %get-tuple-element.7), channel_id=1, source_target_pairs={{0,384},{128,0},{256,128},{384,256},{1,385},{129,1},{257,129},{385... | collective-permute-start | bytes 200 | tf_op jit(solution)/shard_map/ppermute | solution.py:114
  52.8 1.9 %collective-permute-start.1 = (s32[1,16]{1,0:T(1,128)S(1)}, s32[1,16]{1,0:T(1,128)S(1)}, u32[]{:S(2)}, u32[]{:S(2)}) collective-permute-start(s32[1,16]{1,0:T(1,128)S(1)} %get-tuple-element.6), channel_id=1, source_target_pairs={{0,256},{128,384},{256,0},{384,128},{1,257},{129,385},{257,1},{385... | collective-permute-start | bytes 200 | tf_op jit(solution)/shard_map/ppermute | solution.py:114
  54.7 1.0 constant_dynamic-slice_fusion.2
  55.7 0.0 collective-permute-done
  55.8 2.8 %collective-permute-done.1 = s32[1,16]{1,0:T(1,128)S(1)} collective-permute-done((s32[1,16]{1,0:T(1,128)S(1)}, s32[1,16]{1,0:T(1,128)S(1)}, u32[]{:S(2)}, u32[]{:S(2)}) %collective-permute-start.1) | collective-permute-done | bytes 96 | tf_op jit(solution)/shard_map/ppermute | solution.py:114
  58.6 0.1 fusion.8
  58.7 0.8 pad_maximum_fusion
  59.5 5.1 %all-to-all-start = ((bf16[16,48,256]{2,1,0:T(8,128)(2,1)}), bf16[16,48,256]{2,1,0:T(8,128)(2,1)S(1)}, u32[]{:S(2)}, u32[]{:S(2)}) async-start(bf16[16,48,256]{2,1,0:T(8,128)(2,1)} %pad_maximum_fusion), calls=%async_computation | async-start | bytes 786432 | tf_op jit(solution)/shard_map/all_to_all | solution.py:165
  64.5 0.7 pad_add_fusion.place_ref
  65.2 13.9 %all-to-all-done.packet_ref = bf16[16,48,256]{2,1,0:T(8,128)(2,1)S(1)} async-done(((bf16[16,48,256]{2,1,0:T(8,128)(2,1)}), bf16[16,48,256]{2,1,0:T(8,128)(2,1)S(1)}, u32[]{:S(2)}, u32[]{:S(2)}) %all-to-all-start) | async-done | bytes 393248 | tf_op jit(solution)/shard_map/all_to_all | solution.py:165
  79.1 0.7 copy-done.1
  79.8 6.4 %halves.3.refs_0_ = bf16[32,32,16,256]{3,2,1,0:T(8,128)(2,1)} custom-call(bf16[16,48,256]{2,1,0:T(8,128)(2,1)} %copy-done.1, bf16[8,256,256]{2,1,0:T(8,128)(2,1)} %psi_ref.1), custom_call_target="tpu_custom_call" | custom-call | flops 536870912 | bytes 3145728 | tf_op jit(solution)/shard_map/halves/pallas_call | solution.py:29
  86.2 0.6 fusion.12.tag_ref
  86.8 8.9 %halves.4.refs_0_ = bf16[32,32,16,256]{3,2,1,0:T(8,128)(2,1)} custom-call(bf16[16,48,256]{2,1,0:T(8,128)(2,1)} %copy-done.1, bf16[12,256,256]{2,1,0:T(8,128)(2,1)} %copy-done.2, bf16[32,32,16,256]{3,2,1,0:T(8,128)(2,1)} %halves.3.refs_0_), custom_call_target="tpu_custom_call", output_to_operand_aliasing={{}: (2, {})} | custom-call | flops 805306368 | bytes 4718592 | tf_op jit(solution)/shard_map/halves/pallas_call | solution.py:29
  95.7 9.0 %halves.5.half_ref = bf16[32,32,16,256]{3,2,1,0:T(8,128)(2,1)} custom-call(bf16[16,48,256]{2,1,0:T(8,128)(2,1)} %copy-done.1, bf16[12,256,256]{2,1,0:T(8,128)(2,1)} %collective-permute-done.5.psi_ref, bf16[32,32,16,256]{3,2,1,0:T(8,128)(2,1)} %halves.4.refs_0_), custom_call_target="tpu_custom_call", output_to_operand_aliasing={{}: (2, {})} | custom-call | flops 805306368 | bytes 4718592 | tf_op jit(solution)/shard_map/halves/pallas_call | solution.py:29
  104.7 16.3 %sums.1 = bf16[128,16,256]{2,1,0:T(8,128)(2,1)} custom-call(s32[2]{0:T(128)} %pad_add_fusion.place_ref, s32[16,64]{1,0:T(8,128)} %fusion.12.tag_ref, bf16[32,32,16,256]{3,2,1,0:T(8,128)(2,1)} %halves.5.half_ref, bf16[32,256,256]{2,1,0:T(8,128)(2,1)} %all-gather.2.cloned.1.call-done.right_ref), custom_call_target="tpu_custom_call" | custom-call | flops 2147483648 | bytes 12582912 | tf_op jit(solution)/shard_map/sums/pallas_call | solution.py:90
  121.0 37.0 %all_to_all.10 = bf16[16,8,16,256]{3,2,1,0:T(8,128)(2,1)S(1)} all-to-all(bf16[16,8,16,256]{3,2,1,0:T(8,128)(2,1)} %bitcast.28), channel_id=1, replica_groups=mesh['xb'=2,'xa'=2,'z'=8,'y'=8,'c'=2] {'xa','z'}, dimensions={0} | all-to-all | bytes 2097152 | tf_op jit(solution)/shard_map/all_to_all | solution.py:176
  158.0 0.8 convert_add_fusion
  (18 shorter events, 0.1 us)
Async XLA Ops:
  6.5 1.0 copy-start
  6.5 98.2 %all-gather.2.cloned.1.call-start = ((), (), s32[]{:S(2)}) async-start(), calls=%async_computation.2 | async-start | bytes 4456448 | tf_op jit(solution)/shard_map/all_gather | solution.py:140
  8.3 28.5 %collective-permute-start.3 = (bf16[8,256,256]{2,1,0:T(8,128)(2,1)}, bf16[8,256,256]{2,1,0:T(8,128)(2,1)S(1)}, u32[]{:S(2)}, u32[]{:S(2)}) collective-permute-start(bf16[8,256,256]{2,1,0:T(8,128)(2,1)} %psi_ref.1), channel_id=1, source_target_pairs={{0,128},{1,385},{128,256},{129,1},{256,384},{257,129},{384,0},{385... | collective-permute-start | bytes 3145736 | tf_op jit(solution)/shard_map/ppermute | solution.py:122
  14.6 31.5 %copy-start.3 = (s32[1,1,32]{2,1,0:T(1,128)S(1)}, s32[1,1,32]{2,1,0:T(1,128)}, u32[]{:S(2)}) copy-start(s32[1,1,32]{2,1,0:T(1,128)} %param.9) | copy-start | bytes 388
  14.6 31.5 %copy-start.4 = (s32[1,1,32,1]{2,3,1,0:T(1,128)S(1)}, s32[1,1,32,1]{2,3,1,0:T(1,128)}, u32[]{:S(2)}) copy-start(s32[1,1,32,1]{2,3,1,0:T(1,128)} %param.8) | copy-start | bytes 388
  14.7 22.2 %collective-permute-start.4 = (bf16[4,256,256]{2,1,0:T(8,128)(2,1)S(1)}, bf16[4,256,256]{2,1,0:T(8,128)(2,1)S(1)}, u32[]{:S(2)}, u32[]{:S(2)}) collective-permute-start(bf16[4,256,256]{2,1,0:T(8,128)(2,1)S(1)} %constant_dynamic-slice_fusion.1), channel_id=1, source_target_pairs={{0,256},{1,257},{128,384},{129,385},{256,0},{257,1},{384,128},{385... | collective-permute-start | bytes 1572872 | tf_op jit(solution)/shard_map/ppermute | solution.py:122
  36.9 49.3 %copy-start.2 = (bf16[12,256,256]{2,1,0:T(8,128)(2,1)}, bf16[12,256,256]{2,1,0:T(8,128)(2,1)S(1)}, u32[]{:S(2)}) copy-start(bf16[12,256,256]{2,1,0:T(8,128)(2,1)S(1)} %constant_dynamic-update-slice_fusion.psi_ref) | copy-start | bytes 4718596
  36.9 58.8 %collective-permute-start.5 = (bf16[12,256,256]{2,1,0:T(8,128)(2,1)S(1)}, bf16[12,256,256]{2,1,0:T(8,128)(2,1)}, u32[]{:S(2)}, u32[]{:S(2)}) collective-permute-start(bf16[12,256,256]{2,1,0:T(8,128)(2,1)S(1)} %constant_dynamic-update-slice_fusion.psi_ref), channel_id=1, source_target_pairs={{0,1},{1,0},{2,3},{3,2},{4,5},{5,4},{6,7},{7,6},{8,9},{9,8},{10,11... | collective-permute-start | bytes 4718600 | tf_op jit(solution)/shard_map/ppermute | solution.py:114
  46.3 9.4 %collective-permute-start = (s32[1,16]{1,0:T(1,128)S(1)}, s32[1,16]{1,0:T(1,128)S(1)}, u32[]{:S(2)}, u32[]{:S(2)}) collective-permute-start(s32[1,16]{1,0:T(1,128)S(1)} %get-tuple-element.7), channel_id=1, source_target_pairs={{0,128},{128,256},{256,384},{384,0},{1,129},{129,257},{257,385},{3... | collective-permute-start | bytes 200 | tf_op jit(solution)/shard_map/ppermute | solution.py:114
  48.2 7.5 %collective-permute-start.2 = (s32[1,16]{1,0:T(1,128)S(1)}, s32[1,16]{1,0:T(1,128)S(1)}, u32[]{:S(2)}, u32[]{:S(2)}) collective-permute-start(s32[1,16]{1,0:T(1,128)S(1)} %get-tuple-element.7), channel_id=1, source_target_pairs={{0,384},{128,0},{256,128},{384,256},{1,385},{129,1},{257,129},{385... | collective-permute-start | bytes 200 | tf_op jit(solution)/shard_map/ppermute | solution.py:114
  52.8 5.8 %collective-permute-start.1 = (s32[1,16]{1,0:T(1,128)S(1)}, s32[1,16]{1,0:T(1,128)S(1)}, u32[]{:S(2)}, u32[]{:S(2)}) collective-permute-start(s32[1,16]{1,0:T(1,128)S(1)} %get-tuple-element.6), channel_id=1, source_target_pairs={{0,256},{128,384},{256,0},{384,128},{1,257},{129,385},{257,1},{385... | collective-permute-start | bytes 200 | tf_op jit(solution)/shard_map/ppermute | solution.py:114
  59.5 19.6 %all-to-all-start = ((bf16[16,48,256]{2,1,0:T(8,128)(2,1)}), bf16[16,48,256]{2,1,0:T(8,128)(2,1)S(1)}, u32[]{:S(2)}, u32[]{:S(2)}) async-start(bf16[16,48,256]{2,1,0:T(8,128)(2,1)} %pad_maximum_fusion), calls=%async_computation | async-start | bytes 786432 | tf_op jit(solution)/shard_map/all_to_all | solution.py:165
  79.1 0.7 copy-start.1
Sparse Core Ops, SparseCore 0:
  9.5 50.4 all-gather.1

commit v5 on v4

v5 whole, which is shorter than its diff:
```python
import jax
import jax.numpy as jnp
from jax import lax
from jax.experimental import pallas as pl
from jax.experimental.pallas import tpu as pltpu
from jax.sharding import Mesh
from jax.sharding import PartitionSpec as P

XB, XA, Z, Y, C = 2, 2, 8, 8, 2
X = XB * XA
AXIS_X, SEC, MPO = ("xb", "xa"), ("xb", "xa", "z"), ("y", "c")
BF16, F32 = jnp.bfloat16, jnp.float32
TAG_ROWS = 16
STEPS = 4


def half_kernel(packet_ref, *refs):
    half_ref = refs[-1]
    shards, _, width = packet_ref.shape
    terms, _, rows, _ = half_ref.shape
    lefts = packet_ref[:, : terms // shards * rows, :].reshape(terms * rows, width)
    at = 0
    for psi_ref in refs[:-1]:
        for k in range(psi_ref.shape[0]):
            out = jnp.dot(lefts, psi_ref[k], preferred_element_type=F32).astype(BF16)
            half_ref[:, at] = out.reshape(terms, rows, width)
            at += 1


def halves(packet, pieces, terms, rows):
    count = sum(p.shape[0] for p in pieces)
    width = packet.shape[2]
    return pl.pallas_call(
        half_kernel,
        out_shape=jax.ShapeDtypeStruct((terms, count, rows, width), BF16),
        compiler_params=pltpu.CompilerParams(vmem_limit_bytes=32 << 20),
        cost_estimate=pl.CostEstimate(
            flops=2 * terms * rows * width * width * count,
            bytes_accessed=2 * count * width * (width + terms * rows),
            transcendentals=0,
        ),
        name="halves",
    )(packet, *pieces)


def sums_kernel(place_ref, tag_ref, half_a, half_b, right_ref, out_ref, *total_refs):
    step = pl.program_id(0)
    terms, sectors_a, rows, width = half_a.shape
    sectors_b = half_b.shape[1]
    xb, core = place_ref[0], place_ref[1]
    count = out_ref.shape[0]
    each = (sectors_a + sectors_b) // X
    part = each // C
    near, away = 1 + 2 * core, 3 - 2 * core
    runs = (
        ((each, 0, 0), (each, near, 0), (part, 2, core * part)),
        ((each, away, 0), (part, 2, (1 - core) * part)),
    )
    own = tag_ref.shape[1] // (X * each)

    @pl.when(step == 0)
    def _():
        for total_ref in total_refs:
            total_ref[...] = jnp.zeros_like(total_ref)

    turn = 0
    for w in range(terms):
        row = step * (terms // own) + w // own
        for half_ref, some in zip((half_a, half_b), runs, strict=True):
            number = half_ref.shape[1]
            lhs = half_ref[w].reshape(number * rows, width)
            full = jnp.dot(lhs, right_ref[w], preferred_element_type=F32).astype(BF16)
            full = full.astype(F32).reshape(number, rows, width)
            s = 0
            for length, shard, first in some:
                for k in range(length):
                    t = tag_ref[row, (shard * own + w % own) * each + first + k] - xb * count
                    t = jnp.where((t >= 0) & (t < count), t, count)
                    total_ref = total_refs[turn % len(total_refs)]
                    total_ref[t] += full[s]
                    s += 1
                    turn += 1

    @pl.when(step == pl.num_programs(0) - 1)
    def _():
        total = total_refs[0][:count]
        for total_ref in total_refs[1:]:
            total = total + total_ref[:count]
        out_ref[...] = total.astype(BF16)


def sums(place, tags, half_a, half_b, rights, count, steps):
    terms, _, rows, width = half_a.shape
    each = terms // steps
    pairs = terms * (half_a.shape[1] + half_b.shape[1])
    return pl.pallas_call(
        sums_kernel,
        grid_spec=pltpu.PrefetchScalarGridSpec(
            num_scalar_prefetch=2,
            grid=(steps,),
            in_specs=[
                pl.BlockSpec((each, h.shape[1], rows, width), lambda i, *_: (i, 0, 0, 0))
                for h in (half_a, half_b)
            ]
            + [pl.BlockSpec((each, width, width), lambda i, *_: (i, 0, 0))],
            out_specs=pl.BlockSpec((count, rows, width), lambda i, *_: (0, 0, 0)),
            scratch_shapes=[pltpu.VMEM((count + 1, rows, width), F32)] * 2,
        ),
        out_shape=jax.ShapeDtypeStruct((count, rows, width), BF16),
        compiler_params=pltpu.CompilerParams(vmem_limit_bytes=56 << 20),
        cost_estimate=pl.CostEstimate(
            flops=2 * pairs * rows * width * width,
            bytes_accessed=2 * width * (pairs * rows + terms * width),
            transcendentals=0,
        ),
        name="sums",
    )(place, tags, half_a, half_b, rights)


def moved(block, axis, size, by):
    return lax.ppermute(block, axis, [(i, (i + by) % size) for i in range(size)])


def both_ways(block, by):
    pairs = []
    for i in range(X):
        pairs.append((i * C, (i + by) % X * C))
        pairs.append((i * C + 1, (i - by) % X * C + 1))
    return lax.ppermute(block, (*AXIS_X, "c"), pairs)


def added(parts):
    total = parts[0].astype(F32)
    for i in range(1, parts.shape[0]):
        total = total + parts[i].astype(F32)
    return total


def on_device(psi_blocks, left_env, right_env, dest_index, dest_slot):
    sectors, width = psi_blocks.shape[:2]
    terms = left_env.shape[0] // XA
    shards = Y * C
    rows = width // shards
    part = sectors // C
    xb, xa, core = lax.axis_index("xb"), lax.axis_index("xa"), lax.axis_index("c")
    right = lax.dynamic_slice_in_dim(right_env, xa * terms, terms, 0)
    rights = lax.all_gather(right, MPO, axis=0, tiled=True)
    psi_next = both_ways(psi_blocks, 1)
    psi_far = both_ways(lax.dynamic_slice_in_dim(psi_blocks, core * part, part, 0), 2)
    target = (dest_index[0, 0, :, 0] * sectors + dest_slot[0, 0])[None]
    same = lax.dynamic_slice_in_dim(target, xa * terms * sectors, terms * sectors, 1)
    other = lax.dynamic_slice_in_dim(target, (1 - xa) * terms * sectors, terms * sectors, 1)
    tags = [
        same,
        moved(other, AXIS_X, X, 1),
        moved(same, AXIS_X, X, 2),
        moved(other, AXIS_X, X, -1),
    ]
    tags = jnp.concatenate(tags, axis=1).astype(BF16)
    tags = jnp.pad(tags, ((0, TAG_ROWS - 1), (0, width - tags.shape[1])))
    left = lax.dynamic_slice_in_dim(left_env, xa * terms, terms, 0)
    left = left.reshape(terms, shards, rows, width).transpose(1, 0, 2, 3)
    packet = jnp.concatenate(
        [
            left.reshape(shards, terms * rows, width),
            jnp.broadcast_to(tags[None], (shards, TAG_ROWS, width)),
        ],
        axis=1,
    )
    psi_next, psi_far, _ = lax.optimization_barrier((psi_next, psi_far, packet))
    packet = lax.all_to_all(packet, MPO, split_axis=0, concat_axis=0, tiled=True)
    tags = packet[:, terms * rows, : X * terms * sectors].astype(jnp.int32)
    place = jnp.stack([xb, core]).astype(jnp.int32)
    half_a = halves(packet, [psi_blocks, psi_next, psi_far], shards * terms, rows)
    theirs = [moved(psi_next, "c", C, 1), moved(psi_far, "c", C, 1)]
    half_b = halves(packet, theirs, shards * terms, rows)
    partial = sums(place, tags, half_a, half_b, rights, XA * Z * sectors, STEPS)
    partial = partial.reshape(XA * Z, sectors, rows, width)
    partial = lax.all_to_all(partial, ("xa", "z"), split_axis=0, concat_axis=0, tiled=True)
    return added(partial)


def solution(mesh):
    chips = Mesh(mesh.devices.reshape(XB, XA, Z, Y, C), (*SEC, *MPO))
    in_specs = (
        P(SEC, None, None),
        P(MPO, None, None),
        P(MPO, None, None),
        P(MPO, SEC, None, None),
        P(MPO, SEC, None),
    )
    out_specs = P(SEC, MPO, None)
    return jax.shard_map(
        on_device, mesh=chips, in_specs=in_specs, out_specs=out_specs, check_vma=False
    )
```

time: 167 us -> 126 us (0.75)
  Pallas kernels: 40.6 us -> 14.7 us
  waiting for transfers between devices: 36.4 us -> 19.5 us
  blocking collectives: 37 us -> 33.2 us
  local copies, waits for them, and re-layouts: 4.71 us -> 7.83 us
  starting transfers between devices: 30.3 us -> 32.4 us
    ppermute x2, waiting for transfers between devices: 19.7 us -> 0.01 us  [both_ways(): return lax.ppermute(block, (*AXIS_X, 'c'), pairs)]
    pallas_call x3 -> x2, Pallas kernels: 24.3 us -> 4.78 us  [halves(): pl.pallas_call(half_kernel, out_shape=jax.ShapeDtypeStruct((terms, count,...]
    pallas_call x1, Pallas kernels: 16.3 us -> 9.9 us  [sums(): pl.pallas_call(sums_kernel, grid_spec=pltpu.PrefetchScalarGridSpec(num_sc...]
    all_to_all x1, starting transfers between devices: 5.06 us -> 10.8 us  [on_device(): lax.all_to_all(packet, MPO, split_axis=0, concat_axis=0, tiled=True)]
    ppermute x4 -> x5, waiting for transfers between devices: 2.81 us -> 8.34 us  [moved(): lax.ppermute(block, axis, [(i, (i + by) % size) for i in range(size)])]
    all_to_all x1, blocking collectives: 37 us -> 33.2 us  [on_device(): lax.all_to_all(partial, ('xa', 'z'), split_axis=0, concat_axis=0, tiled=T...]
    ppermute x4 -> x5, starting transfers between devices: 17.6 us -> 14 us  [moved(): lax.ppermute(block, axis, [(i, (i + by) % size) for i in range(size)])]
    unnamed x11 -> x8, local copies, waits for them, and re-layouts: 1.86 us -> 4.99 us
  transfers between devices with their start and end apart: 8 -> 9, of which waited for: 3 -> 2; matrix products, arithmetic and copies ran while one was open for 3% -> 4% of each run, Pallas kernels for 15% -> 4%
where the time goes in v5:
time: 126 us; the launch traced here: 125 us
  blocking collectives  33.2 us (26%)
  starting transfers between devices  32.4 us (26%)
  waiting for transfers between devices  19.5 us (15%)
  Pallas kernels  14.7 us (12%)
  between operations  13.5 us (11%)
  local copies, waits for them, and re-layouts  7.83 us (6%)
  other arithmetic  3.59 us (3%)
    all_to_all x1, blocking collectives, on_device(): lax.all_to_all(partial, ('xa', 'z'), split_axis=0, concat_axis=0, tiled=T...  33.2 us
    ppermute x5, starting transfers between devices, moved(): lax.ppermute(block, axis, [(i, (i + by) % size) for i in range(size)])  14 us
    all_to_all x1, waiting for transfers between devices, on_device(): lax.all_to_all(packet, MPO, split_axis=0, concat_axis=0, tiled=True)  11.1 us
    all_to_all x1, starting transfers between devices, on_device(): lax.all_to_all(packet, MPO, split_axis=0, concat_axis=0, tiled=True)  10.8 us
    pallas_call x1, Pallas kernels, sums(): pl.pallas_call(sums_kernel, grid_spec=pltpu.PrefetchScalarGridSpec(num_sc...  9.9 us
    ppermute x5, waiting for transfers between devices, moved(): lax.ppermute(block, axis, [(i, (i + by) % size) for i in range(size)])  8.34 us
    ppermute x2, starting transfers between devices, both_ways(): return lax.ppermute(block, (*AXIS_X, 'c'), pairs)  7.65 us
    unnamed x8, local copies, waits for them, and re-layouts  4.99 us
  transfers between devices with their start and end apart: 9, of which 2 were waited for; matrix products, arithmetic and copies ran while one was open for 4% of the time, Pallas kernels for 4%

profile of v5, /device:TPU:1, one launch (start us, length us, event | category | flops | bytes accessed | tf_op | source)
XLA Modules:
  0.0 124.7 jit_solution(17000839292063587352)
XLA Ops:
  6.5 1.0 copy-done
  7.6 0.7 constant_dynamic-slice_fusion
  8.3 0.0 all-gather.2.cloned.1.call-update
  8.3 5.2 %collective-permute-start.3 = (bf16[8,256,256]{2,1,0:T(8,128)(2,1)}, bf16[8,256,256]{2,1,0:T(8,128)(2,1)}, u32[]{:S(2)}, u32[]{:S(2)}) collective-permute-start(bf16[8,256,256]{2,1,0:T(8,128)(2,1)} %refs_0_.1), channel_id=1, source_target_pairs={{0,128},{1,385},{128,256},{129,1},{256,384},{257,129},{384,0},{385... | collective-permute-start | bytes 3145736 | tf_op jit(solution)/shard_map/ppermute | solution.py:129
  13.6 1.1 constant_dynamic-slice_fusion.1
  14.7 2.4 %collective-permute-start.4 = (bf16[4,256,256]{2,1,0:T(8,128)(2,1)S(1)}, bf16[4,256,256]{2,1,0:T(8,128)(2,1)S(1)}, u32[]{:S(2)}, u32[]{:S(2)}) collective-permute-start(bf16[4,256,256]{2,1,0:T(8,128)(2,1)S(1)} %constant_dynamic-slice_fusion.1), channel_id=1, source_target_pairs={{0,256},{1,257},{128,384},{129,385},{256,0},{257,1},{384,128},{385... | collective-permute-start | bytes 1572872 | tf_op jit(solution)/shard_map/ppermute | solution.py:129
  17.1 0.7 bitcast_add_fusion
  17.8 0.1 fusion.13
  17.9 2.5 %collective-permute-start = (s32[1,16]{1,0:T(1,128)S(1)}, s32[1,16]{1,0:T(1,128)S(1)}, u32[]{:S(2)}, u32[]{:S(2)}) collective-permute-start(s32[1,16]{1,0:T(1,128)S(1)} %get-tuple-element.11), channel_id=1, source_target_pairs={{0,128},{128,256},{256,384},{384,0},{1,129},{129,257},{257,385},{3... | collective-permute-start | bytes 200 | tf_op jit(solution)/shard_map/ppermute | solution.py:121
  20.4 4.0 %collective-permute-start.2 = (s32[1,16]{1,0:T(1,128)S(1)}, s32[1,16]{1,0:T(1,128)S(1)}, u32[]{:S(2)}, u32[]{:S(2)}) collective-permute-start(s32[1,16]{1,0:T(1,128)S(1)} %get-tuple-element.11), channel_id=1, source_target_pairs={{0,384},{128,0},{256,128},{384,256},{1,385},{129,1},{257,129},{385... | collective-permute-start | bytes 200 | tf_op jit(solution)/shard_map/ppermute | solution.py:121
  24.4 3.1 %collective-permute-start.1 = (s32[1,16]{1,0:T(1,128)S(1)}, s32[1,16]{1,0:T(1,128)S(1)}, u32[]{:S(2)}, u32[]{:S(2)}) collective-permute-start(s32[1,16]{1,0:T(1,128)S(1)} %get-tuple-element.10), channel_id=1, source_target_pairs={{0,256},{128,384},{256,0},{384,128},{1,257},{129,385},{257,1},{385... | collective-permute-start | bytes 200 | tf_op jit(solution)/shard_map/ppermute | solution.py:121
  27.5 1.0 constant_dynamic-slice_fusion.2
  28.5 0.0 collective-permute-done
  28.5 8.3 %collective-permute-done.2 = s32[1,16]{1,0:T(1,128)S(1)} collective-permute-done((s32[1,16]{1,0:T(1,128)S(1)}, s32[1,16]{1,0:T(1,128)S(1)}, u32[]{:S(2)}, u32[]{:S(2)}) %collective-permute-start.2) | collective-permute-done | bytes 96 | tf_op jit(solution)/shard_map/ppermute | solution.py:121
  36.9 0.0 collective-permute-done.1
  36.9 0.1 fusion.8
  37.0 0.8 pad_maximum_fusion
  37.8 10.8 %all-to-all-start = ((bf16[16,48,256]{2,1,0:T(8,128)(2,1)}), bf16[16,48,256]{2,1,0:T(8,128)(2,1)S(1)}, u32[]{:S(2)}, u32[]{:S(2)}) async-start(bf16[16,48,256]{2,1,0:T(8,128)(2,1)} %pad_maximum_fusion), calls=%async_computation | async-start | bytes 786432 | tf_op jit(solution)/shard_map/all_to_all | solution.py:171
  48.5 0.0 collective-permute-done.3.refs_1_
  48.5 2.1 %collective-permute-start.5 = (bf16[8,256,256]{2,1,0:T(8,128)(2,1)}, bf16[8,256,256]{2,1,0:T(8,128)(2,1)S(1)}, u32[]{:S(2)}, u32[]{:S(2)}) collective-permute-start(bf16[8,256,256]{2,1,0:T(8,128)(2,1)} %collective-permute-done.3.refs_1_), channel_id=1, source_target_pairs={{0,1},{1,0},{2,3},{3,2},{4,5},{5,4},{6,7},{7,6},{8,9},{9,8},{10,11... | collective-permute-start | bytes 3145736 | tf_op jit(solution)/shard_map/ppermute | solution.py:121
  50.7 2.2 %collective-permute-start.6 = (bf16[4,256,256]{2,1,0:T(8,128)(2,1)S(1)}, bf16[4,256,256]{2,1,0:T(8,128)(2,1)}, u32[]{:S(2)}, u32[]{:S(2)}) collective-permute-start(bf16[4,256,256]{2,1,0:T(8,128)(2,1)S(1)} %collective-permute-done.4.refs_2_), channel_id=1, source_target_pairs={{0,1},{1,0},{2,3},{3,2},{4,5},{5,4},{6,7},{7,6},{8,9},{9,8},{10,11... | collective-permute-start | bytes 1572872 | tf_op jit(solution)/shard_map/ppermute | solution.py:121
  52.9 0.6 pad_add_fusion.place_ref
  53.4 11.1 %all-to-all-done.packet_ref = bf16[16,48,256]{2,1,0:T(8,128)(2,1)S(1)} async-done(((bf16[16,48,256]{2,1,0:T(8,128)(2,1)}), bf16[16,48,256]{2,1,0:T(8,128)(2,1)S(1)}, u32[]{:S(2)}, u32[]{:S(2)}) %all-to-all-start) | async-done | bytes 393248 | tf_op jit(solution)/shard_map/all_to_all | solution.py:171
  64.6 0.6 fusion.12.tag_ref
  65.2 2.8 %halves.2.half_a = bf16[32,20,16,256]{3,2,1,0:T(8,128)(2,1)S(1)} custom-call(bf16[16,48,256]{2,1,0:T(8,128)(2,1)S(1)} %all-to-all-done.packet_ref, bf16[8,256,256]{2,1,0:T(8,128)(2,1)S(1)} %copy-done.3, bf16[8,256,256]{2,1,0:T(8,128)(2,1)} %collective-permute-done.3.refs_1_, bf16[4,256,256]{2,1,0:T(8,128)(2,1)S(1)} %collective-permute-done.4.refs_2_), custom_call_target="tpu_custom_call" | custom-call | flops 1342177280 | bytes 7864320 | tf_op jit(solution)/shard_map/halves/pallas_call | solution.py:33
  68.0 2.3 %copy-done.1 = bf16[32,20,16,256]{3,2,1,0:T(8,128)(2,1)} copy-done((bf16[32,20,16,256]{3,2,1,0:T(8,128)(2,1)}, bf16[32,20,16,256]{3,2,1,0:T(8,128)(2,1)S(1)}, u32[]{:S(2)}) %copy-start.1) | copy-done | bytes 5242904
  70.3 0.0 collective-permute-done.6.refs_1_
  70.3 2.0 %halves.3.half_b = bf16[32,12,16,256]{3,2,1,0:T(8,128)(2,1)S(1)} custom-call(bf16[16,48,256]{2,1,0:T(8,128)(2,1)S(1)} %all-to-all-done.packet_ref, bf16[8,256,256]{2,1,0:T(8,128)(2,1)S(1)} %collective-permute-done.5.refs_0_, bf16[4,256,256]{2,1,0:T(8,128)(2,1)} %collective-permute-done.6.refs_1_), custom_call_target="tpu_custom_call" | custom-call | flops 805306368 | bytes 4718592 | tf_op jit(solution)/shard_map/halves/pallas_call | solution.py:33
  72.3 1.7 %copy-done.2 = bf16[32,12,16,256]{3,2,1,0:T(8,128)(2,1)} copy-done((bf16[32,12,16,256]{3,2,1,0:T(8,128)(2,1)}, bf16[32,12,16,256]{3,2,1,0:T(8,128)(2,1)S(1)}, u32[]{:S(2)}) %copy-start.2) | copy-done | bytes 3145752
  74.0 9.9 %sums.1 = bf16[128,16,256]{2,1,0:T(8,128)(2,1)} custom-call(s32[2]{0:T(128)} %pad_add_fusion.place_ref, s32[16,64]{1,0:T(8,128)} %fusion.12.tag_ref, bf16[32,20,16,256]{3,2,1,0:T(8,128)(2,1)} %copy-done.1, bf16[32,12,16,256]{3,2,1,0:T(8,128)(2,1)} %copy-done.2, bf16[32,256,256]{2,1,0:T(8,128)(2,1)} %all-gather.2.cloned.1.call-done.right_ref), custom_call_target="tpu_custom_call" | custom-call | flops 2147483648 | bytes 12582912 | tf_op jit(solution)/shard_map/sums/pallas_call | solution.py:96
  83.9 33.2 %all_to_all.10 = bf16[16,8,16,256]{3,2,1,0:T(8,128)(2,1)S(1)} all-to-all(bf16[16,8,16,256]{3,2,1,0:T(8,128)(2,1)} %bitcast.28), channel_id=1, replica_groups=mesh['xb'=2,'xa'=2,'z'=8,'y'=8,'c'=2] {'xa','z'}, dimensions={0} | all-to-all | bytes 2097152 | tf_op jit(solution)/shard_map/all_to_all | solution.py:179
  117.0 0.8 convert_add_fusion
  (15 shorter events, 0.1 us)
Async XLA Ops:
  6.5 1.0 copy-start
  6.5 58.7 %copy-start.3 = (bf16[8,256,256]{2,1,0:T(8,128)(2,1)S(1)}, bf16[8,256,256]{2,1,0:T(8,128)(2,1)}, u32[]{:S(2)}) copy-start(bf16[8,256,256]{2,1,0:T(8,128)(2,1)} %refs_0_.1) | copy-start | bytes 3145732
  6.5 67.4 %all-gather.2.cloned.1.call-start = ((), (), s32[]{:S(2)}) async-start(), calls=%async_computation.2 | async-start | bytes 4456448 | tf_op jit(solution)/shard_map/all_gather | solution.py:147
  8.3 40.2 %collective-permute-start.3 = (bf16[8,256,256]{2,1,0:T(8,128)(2,1)}, bf16[8,256,256]{2,1,0:T(8,128)(2,1)}, u32[]{:S(2)}, u32[]{:S(2)}) collective-permute-start(bf16[8,256,256]{2,1,0:T(8,128)(2,1)} %refs_0_.1), channel_id=1, source_target_pairs={{0,128},{1,385},{128,256},{129,1},{256,384},{257,129},{384,0},{385... | collective-permute-start | bytes 3145736 | tf_op jit(solution)/shard_map/ppermute | solution.py:129
  14.7 33.9 %collective-permute-start.4 = (bf16[4,256,256]{2,1,0:T(8,128)(2,1)S(1)}, bf16[4,256,256]{2,1,0:T(8,128)(2,1)S(1)}, u32[]{:S(2)}, u32[]{:S(2)}) collective-permute-start(bf16[4,256,256]{2,1,0:T(8,128)(2,1)S(1)} %constant_dynamic-slice_fusion.1), channel_id=1, source_target_pairs={{0,256},{1,257},{128,384},{129,385},{256,0},{257,1},{384,128},{385... | collective-permute-start | bytes 1572872 | tf_op jit(solution)/shard_map/ppermute | solution.py:129
  17.9 10.7 %collective-permute-start = (s32[1,16]{1,0:T(1,128)S(1)}, s32[1,16]{1,0:T(1,128)S(1)}, u32[]{:S(2)}, u32[]{:S(2)}) collective-permute-start(s32[1,16]{1,0:T(1,128)S(1)} %get-tuple-element.11), channel_id=1, source_target_pairs={{0,128},{128,256},{256,384},{384,0},{1,129},{129,257},{257,385},{3... | collective-permute-start | bytes 200 | tf_op jit(solution)/shard_map/ppermute | solution.py:121
  20.4 16.5 %collective-permute-start.2 = (s32[1,16]{1,0:T(1,128)S(1)}, s32[1,16]{1,0:T(1,128)S(1)}, u32[]{:S(2)}, u32[]{:S(2)}) collective-permute-start(s32[1,16]{1,0:T(1,128)S(1)} %get-tuple-element.11), channel_id=1, source_target_pairs={{0,384},{128,0},{256,128},{384,256},{1,385},{129,1},{257,129},{385... | collective-permute-start | bytes 200 | tf_op jit(solution)/shard_map/ppermute | solution.py:121
  24.4 12.5 %collective-permute-start.1 = (s32[1,16]{1,0:T(1,128)S(1)}, s32[1,16]{1,0:T(1,128)S(1)}, u32[]{:S(2)}, u32[]{:S(2)}) collective-permute-start(s32[1,16]{1,0:T(1,128)S(1)} %get-tuple-element.10), channel_id=1, source_target_pairs={{0,256},{128,384},{256,0},{384,128},{1,257},{129,385},{257,1},{385... | collective-permute-start | bytes 200 | tf_op jit(solution)/shard_map/ppermute | solution.py:121
  37.8 26.8 %all-to-all-start = ((bf16[16,48,256]{2,1,0:T(8,128)(2,1)}), bf16[16,48,256]{2,1,0:T(8,128)(2,1)S(1)}, u32[]{:S(2)}, u32[]{:S(2)}) async-start(bf16[16,48,256]{2,1,0:T(8,128)(2,1)} %pad_maximum_fusion), calls=%async_computation | async-start | bytes 786432 | tf_op jit(solution)/shard_map/all_to_all | solution.py:171
  48.5 21.7 %collective-permute-start.5 = (bf16[8,256,256]{2,1,0:T(8,128)(2,1)}, bf16[8,256,256]{2,1,0:T(8,128)(2,1)S(1)}, u32[]{:S(2)}, u32[]{:S(2)}) collective-permute-start(bf16[8,256,256]{2,1,0:T(8,128)(2,1)} %collective-permute-done.3.refs_1_), channel_id=1, source_target_pairs={{0,1},{1,0},{2,3},{3,2},{4,5},{5,4},{6,7},{7,6},{8,9},{9,8},{10,11... | collective-permute-start | bytes 3145736 | tf_op jit(solution)/shard_map/ppermute | solution.py:121
  50.7 19.6 %collective-permute-start.6 = (bf16[4,256,256]{2,1,0:T(8,128)(2,1)S(1)}, bf16[4,256,256]{2,1,0:T(8,128)(2,1)}, u32[]{:S(2)}, u32[]{:S(2)}) collective-permute-start(bf16[4,256,256]{2,1,0:T(8,128)(2,1)S(1)} %collective-permute-done.4.refs_2_), channel_id=1, source_target_pairs={{0,1},{1,0},{2,3},{3,2},{4,5},{5,4},{6,7},{7,6},{8,9},{9,8},{10,11... | collective-permute-start | bytes 1572872 | tf_op jit(solution)/shard_map/ppermute | solution.py:121
  68.0 2.3 %copy-start.1 = (bf16[32,20,16,256]{3,2,1,0:T(8,128)(2,1)}, bf16[32,20,16,256]{3,2,1,0:T(8,128)(2,1)S(1)}, u32[]{:S(2)}) copy-start(bf16[32,20,16,256]{3,2,1,0:T(8,128)(2,1)S(1)} %halves.2.half_a) | copy-start | bytes 15728644
  72.3 1.7 %copy-start.2 = (bf16[32,12,16,256]{3,2,1,0:T(8,128)(2,1)}, bf16[32,12,16,256]{3,2,1,0:T(8,128)(2,1)S(1)}, u32[]{:S(2)}) copy-start(bf16[32,12,16,256]{3,2,1,0:T(8,128)(2,1)S(1)} %halves.3.half_b) | copy-start | bytes 9437188
Sparse Core Ops, SparseCore 0:
  9.5 57.2 all-gather.1

commit v6 on v5

--- a/solution.py
+++ b/solution.py
@@ -33,7 +33,7 @@
     return pl.pallas_call(
         half_kernel,
         out_shape=jax.ShapeDtypeStruct((terms, count, rows, width), BF16),
-        compiler_params=pltpu.CompilerParams(vmem_limit_bytes=32 << 20),
+        compiler_params=pltpu.CompilerParams(vmem_limit_bytes=16 << 20),
         cost_estimate=pl.CostEstimate(
             flops=2 * terms * rows * width * width * count,
             bytes_accessed=2 * count * width * (width + terms * rows),
@@ -145,8 +145,6 @@
     xb, xa, core = lax.axis_index("xb"), lax.axis_index("xa"), lax.axis_index("c")
     right = lax.dynamic_slice_in_dim(right_env, xa * terms, terms, 0)
     rights = lax.all_gather(right, MPO, axis=0, tiled=True)
-    psi_next = both_ways(psi_blocks, 1)
-    psi_far = both_ways(lax.dynamic_slice_in_dim(psi_blocks, core * part, part, 0), 2)
     target = (dest_index[0, 0, :, 0] * sectors + dest_slot[0, 0])[None]
     same = lax.dynamic_slice_in_dim(target, xa * terms * sectors, terms * sectors, 1)
     other = lax.dynamic_slice_in_dim(target, (1 - xa) * terms * sectors, terms * sectors, 1)
@@ -158,6 +156,9 @@
     ]
     tags = jnp.concatenate(tags, axis=1).astype(BF16)
     tags = jnp.pad(tags, ((0, TAG_ROWS - 1), (0, width - tags.shape[1])))
+    sent, _ = lax.optimization_barrier((psi_blocks, tags))
+    psi_next = both_ways(sent, 1)
+    psi_far = both_ways(lax.dynamic_slice_in_dim(sent, core * part, part, 0), 2)
     left = lax.dynamic_slice_in_dim(left_env, xa * terms, terms, 0)
     left = left.reshape(terms, shards, rows, width).transpose(1, 0, 2, 3)
     packet = jnp.concatenate(

time: 126 us -> 124 us (0.984)
  waiting for transfers between devices: 19.5 us -> 2.15 us
  starting transfers between devices: 32.4 us -> 46 us
    ppermute x5, starting transfers between devices: 14 us -> 29.4 us  [moved(): lax.ppermute(block, axis, [(i, (i + by) % size) for i in range(size)])]
    all_to_all x1, waiting for transfers between devices: 11.1 us -> 0.01 us  [on_device(): lax.all_to_all(packet, MPO, split_axis=0, concat_axis=0, tiled=True)]
    ppermute x5, waiting for transfers between devices: 8.34 us -> 2.12 us  [moved(): lax.ppermute(block, axis, [(i, (i + by) % size) for i in range(size)])]
    ppermute x2, starting transfers between devices: 7.65 us -> 5.78 us  [both_ways(): return lax.ppermute(block, (*AXIS_X, 'c'), pairs)]
  transfers between devices with their start and end apart: 9 -> 9, of which waited for: 2 -> 1; matrix products, arithmetic and copies ran while one was open for 4% -> 4% of each run, Pallas kernels for 4% -> 4%
where the time goes in v6:
time: 124 us; the launch traced here: 122 us
  starting transfers between devices  46 us (37%)
  blocking collectives  34 us (27%)
  Pallas kernels  14.7 us (12%)
  between operations  13.6 us (11%)
  local copies, waits for them, and re-layouts  7.82 us (6%)
  other arithmetic  3.59 us (3%)
  waiting for transfers between devices  2.15 us (2%)
    all_to_all x1, blocking collectives, on_device(): lax.all_to_all(partial, ('xa', 'z'), split_axis=0, concat_axis=0, tiled=T...  34 us
    ppermute x5, starting transfers between devices, moved(): lax.ppermute(block, axis, [(i, (i + by) % size) for i in range(size)])  29.4 us
    all_to_all x1, starting transfers between devices, on_device(): lax.all_to_all(packet, MPO, split_axis=0, concat_axis=0, tiled=True)  10.8 us
    pallas_call x1, Pallas kernels, sums(): pl.pallas_call(sums_kernel, grid_spec=pltpu.PrefetchScalarGridSpec(num_sc...  9.9 us
    ppermute x2, starting transfers between devices, both_ways(): return lax.ppermute(block, (*AXIS_X, 'c'), pairs)  5.78 us
    unnamed x8, local copies, waits for them, and re-layouts  4.99 us
    pallas_call x2, Pallas kernels, halves(): pl.pallas_call(half_kernel, out_shape=jax.ShapeDtypeStruct((terms, count,...  4.78 us
  transfers between devices with their start and end apart: 9, of which 1 were waited for; matrix products, arithmetic and copies ran while one was open for 4% of the time, Pallas kernels for 4%

profile of v6, /device:TPU:1, one launch (start us, length us, event | category | flops | bytes accessed | tf_op | source)
XLA Modules:
  0.0 121.8 jit_solution(2343401931392384618)
XLA Ops:
  6.5 1.0 copy-done
  7.6 0.7 constant_dynamic-slice_fusion
  8.3 0.0 all-gather.2.cloned.1.call-update
  8.3 0.7 bitcast_add_fusion
  9.0 0.1 fusion.13
  9.1 3.9 %collective-permute-start = (s32[1,16]{1,0:T(1,128)S(1)}, s32[1,16]{1,0:T(1,128)S(1)}, u32[]{:S(2)}, u32[]{:S(2)}) collective-permute-start(s32[1,16]{1,0:T(1,128)S(1)} %get-tuple-element.13), channel_id=1, source_target_pairs={{0,128},{128,256},{256,384},{384,0},{1,129},{129,257},{257,385},{3... | collective-permute-start | bytes 200 | tf_op jit(solution)/shard_map/ppermute | solution.py:121
  13.1 3.2 %collective-permute-start.2 = (s32[1,16]{1,0:T(1,128)S(1)}, s32[1,16]{1,0:T(1,128)S(1)}, u32[]{:S(2)}, u32[]{:S(2)}) collective-permute-start(s32[1,16]{1,0:T(1,128)S(1)} %get-tuple-element.13), channel_id=1, source_target_pairs={{0,384},{128,0},{256,128},{384,256},{1,385},{129,1},{257,129},{385... | collective-permute-start | bytes 200 | tf_op jit(solution)/shard_map/ppermute | solution.py:121
  16.2 3.6 %collective-permute-start.1 = (s32[1,16]{1,0:T(1,128)S(1)}, s32[1,16]{1,0:T(1,128)S(1)}, u32[]{:S(2)}, u32[]{:S(2)}) collective-permute-start(s32[1,16]{1,0:T(1,128)S(1)} %get-tuple-element.12), channel_id=1, source_target_pairs={{0,256},{128,384},{256,0},{384,128},{1,257},{129,385},{257,1},{385... | collective-permute-start | bytes 200 | tf_op jit(solution)/shard_map/ppermute | solution.py:121
  19.9 0.0 collective-permute-done
  19.9 0.0 collective-permute-done.2
  19.9 2.1 %collective-permute-done.1 = s32[1,16]{1,0:T(1,128)S(1)} collective-permute-done((s32[1,16]{1,0:T(1,128)S(1)}, s32[1,16]{1,0:T(1,128)S(1)}, u32[]{:S(2)}, u32[]{:S(2)}) %collective-permute-start.1) | collective-permute-done | bytes 96 | tf_op jit(solution)/shard_map/ppermute | solution.py:121
  22.0 0.1 fusion.8
  22.1 3.4 %collective-permute-start.3 = (bf16[8,256,256]{2,1,0:T(8,128)(2,1)}, bf16[8,256,256]{2,1,0:T(8,128)(2,1)}, u32[]{:S(2)}, u32[]{:S(2)}) collective-permute-start(bf16[8,256,256]{2,1,0:T(8,128)(2,1)} %refs_0_.1), channel_id=1, source_target_pairs={{0,128},{1,385},{128,256},{129,1},{256,384},{257,129},{384,0},{385... | collective-permute-start | bytes 3145736 | tf_op jit(solution)/shard_map/ppermute | solution.py:129
  25.5 1.1 constant_dynamic-slice_fusion.1
  26.6 2.4 %collective-permute-start.4 = (bf16[4,256,256]{2,1,0:T(8,128)(2,1)S(1)}, bf16[4,256,256]{2,1,0:T(8,128)(2,1)S(1)}, u32[]{:S(2)}, u32[]{:S(2)}) collective-permute-start(bf16[4,256,256]{2,1,0:T(8,128)(2,1)S(1)} %constant_dynamic-slice_fusion.1), channel_id=1, source_target_pairs={{0,256},{1,257},{128,384},{129,385},{256,0},{257,1},{384,128},{385... | collective-permute-start | bytes 1572872 | tf_op jit(solution)/shard_map/ppermute | solution.py:129
  29.0 1.0 constant_dynamic-slice_fusion.2
  30.0 0.8 pad_maximum_fusion
  30.8 10.8 %all-to-all-start = ((bf16[16,48,256]{2,1,0:T(8,128)(2,1)}), bf16[16,48,256]{2,1,0:T(8,128)(2,1)S(1)}, u32[]{:S(2)}, u32[]{:S(2)}) async-start(bf16[16,48,256]{2,1,0:T(8,128)(2,1)} %pad_maximum_fusion), calls=%async_computation | async-start | bytes 786432 | tf_op jit(solution)/shard_map/all_to_all | solution.py:172
  41.6 0.0 collective-permute-done.4.refs_2_
  41.6 16.8 %collective-permute-start.5 = (bf16[8,256,256]{2,1,0:T(8,128)(2,1)}, bf16[8,256,256]{2,1,0:T(8,128)(2,1)S(1)}, u32[]{:S(2)}, u32[]{:S(2)}) collective-permute-start(bf16[8,256,256]{2,1,0:T(8,128)(2,1)} %collective-permute-done.3.refs_1_), channel_id=1, source_target_pairs={{0,1},{1,0},{2,3},{3,2},{4,5},{5,4},{6,7},{7,6},{8,9},{9,8},{10,11... | collective-permute-start | bytes 3145736 | tf_op jit(solution)/shard_map/ppermute | solution.py:121
  58.4 1.9 %collective-permute-start.6 = (bf16[4,256,256]{2,1,0:T(8,128)(2,1)S(1)}, bf16[4,256,256]{2,1,0:T(8,128)(2,1)}, u32[]{:S(2)}, u32[]{:S(2)}) collective-permute-start(bf16[4,256,256]{2,1,0:T(8,128)(2,1)S(1)} %collective-permute-done.4.refs_2_), channel_id=1, source_target_pairs={{0,1},{1,0},{2,3},{3,2},{4,5},{5,4},{6,7},{7,6},{8,9},{9,8},{10,11... | collective-permute-start | bytes 1572872 | tf_op jit(solution)/shard_map/ppermute | solution.py:121
  60.3 0.6 pad_add_fusion.place_ref
  60.9 0.6 fusion.12.tag_ref
  61.5 2.8 %halves.2.half_a = bf16[32,20,16,256]{3,2,1,0:T(8,128)(2,1)S(1)} custom-call(bf16[16,48,256]{2,1,0:T(8,128)(2,1)S(1)} %all-to-all-done.packet_ref, bf16[8,256,256]{2,1,0:T(8,128)(2,1)S(1)} %copy-done.3, bf16[8,256,256]{2,1,0:T(8,128)(2,1)} %collective-permute-done.3.refs_1_, bf16[4,256,256]{2,1,0:T(8,128)(2,1)S(1)} %collective-permute-done.4.refs_2_), custom_call_target="tpu_custom_call" | custom-call | flops 1342177280 | bytes 7864320 | tf_op jit(solution)/shard_map/halves/pallas_call | solution.py:33
  64.3 2.3 %copy-done.1 = bf16[32,20,16,256]{3,2,1,0:T(8,128)(2,1)} copy-done((bf16[32,20,16,256]{3,2,1,0:T(8,128)(2,1)}, bf16[32,20,16,256]{3,2,1,0:T(8,128)(2,1)S(1)}, u32[]{:S(2)}) %copy-start.1) | copy-done | bytes 5242904
  66.6 0.0 collective-permute-done.6.refs_1_
  66.6 0.0 collective-permute-done.5.refs_0_
  66.6 2.0 %halves.3.half_b = bf16[32,12,16,256]{3,2,1,0:T(8,128)(2,1)S(1)} custom-call(bf16[16,48,256]{2,1,0:T(8,128)(2,1)S(1)} %all-to-all-done.packet_ref, bf16[8,256,256]{2,1,0:T(8,128)(2,1)S(1)} %collective-permute-done.5.refs_0_, bf16[4,256,256]{2,1,0:T(8,128)(2,1)} %collective-permute-done.6.refs_1_), custom_call_target="tpu_custom_call" | custom-call | flops 805306368 | bytes 4718592 | tf_op jit(solution)/shard_map/halves/pallas_call | solution.py:33
  68.6 1.7 %copy-done.2 = bf16[32,12,16,256]{3,2,1,0:T(8,128)(2,1)} copy-done((bf16[32,12,16,256]{3,2,1,0:T(8,128)(2,1)}, bf16[32,12,16,256]{3,2,1,0:T(8,128)(2,1)S(1)}, u32[]{:S(2)}) %copy-start.2) | copy-done | bytes 3145752
  70.3 9.9 %sums.1 = bf16[128,16,256]{2,1,0:T(8,128)(2,1)} custom-call(s32[2]{0:T(128)} %pad_add_fusion.place_ref, s32[16,64]{1,0:T(8,128)} %fusion.12.tag_ref, bf16[32,20,16,256]{3,2,1,0:T(8,128)(2,1)} %copy-done.1, bf16[32,12,16,256]{3,2,1,0:T(8,128)(2,1)} %copy-done.2, bf16[32,256,256]{2,1,0:T(8,128)(2,1)} %all-gather.2.cloned.1.call-done.right_ref), custom_call_target="tpu_custom_call" | custom-call | flops 2147483648 | bytes 12582912 | tf_op jit(solution)/shard_map/sums/pallas_call | solution.py:96
  80.2 34.0 %all_to_all.10 = bf16[16,8,16,256]{3,2,1,0:T(8,128)(2,1)S(1)} all-to-all(bf16[16,8,16,256]{3,2,1,0:T(8,128)(2,1)} %bitcast.28), channel_id=1, replica_groups=mesh['xb'=2,'xa'=2,'z'=8,'y'=8,'c'=2] {'xa','z'}, dimensions={0} | all-to-all | bytes 2097152 | tf_op jit(solution)/shard_map/all_to_all | solution.py:180
  114.2 0.8 convert_add_fusion
  (15 shorter events, 0.1 us)
Async XLA Ops:
  6.5 1.0 copy-start
  6.5 55.0 %copy-start.3 = (bf16[8,256,256]{2,1,0:T(8,128)(2,1)S(1)}, bf16[8,256,256]{2,1,0:T(8,128)(2,1)}, u32[]{:S(2)}) copy-start(bf16[8,256,256]{2,1,0:T(8,128)(2,1)} %refs_0_.1) | copy-start | bytes 3145732
  6.5 63.7 %all-gather.2.cloned.1.call-start = ((), (), s32[]{:S(2)}) async-start(), calls=%async_computation.2 | async-start | bytes 4456448 | tf_op jit(solution)/shard_map/all_gather | solution.py:147
  9.1 10.8 %collective-permute-start = (s32[1,16]{1,0:T(1,128)S(1)}, s32[1,16]{1,0:T(1,128)S(1)}, u32[]{:S(2)}, u32[]{:S(2)}) collective-permute-start(s32[1,16]{1,0:T(1,128)S(1)} %get-tuple-element.13), channel_id=1, source_target_pairs={{0,128},{128,256},{256,384},{384,0},{1,129},{129,257},{257,385},{3... | collective-permute-start | bytes 200 | tf_op jit(solution)/shard_map/ppermute | solution.py:121
  13.1 6.9 %collective-permute-start.2 = (s32[1,16]{1,0:T(1,128)S(1)}, s32[1,16]{1,0:T(1,128)S(1)}, u32[]{:S(2)}, u32[]{:S(2)}) collective-permute-start(s32[1,16]{1,0:T(1,128)S(1)} %get-tuple-element.13), channel_id=1, source_target_pairs={{0,384},{128,0},{256,128},{384,256},{1,385},{129,1},{257,129},{385... | collective-permute-start | bytes 200 | tf_op jit(solution)/shard_map/ppermute | solution.py:121
  16.2 5.8 %collective-permute-start.1 = (s32[1,16]{1,0:T(1,128)S(1)}, s32[1,16]{1,0:T(1,128)S(1)}, u32[]{:S(2)}, u32[]{:S(2)}) collective-permute-start(s32[1,16]{1,0:T(1,128)S(1)} %get-tuple-element.12), channel_id=1, source_target_pairs={{0,256},{128,384},{256,0},{384,128},{1,257},{129,385},{257,1},{385... | collective-permute-start | bytes 200 | tf_op jit(solution)/shard_map/ppermute | solution.py:121
  22.1 19.5 %collective-permute-start.3 = (bf16[8,256,256]{2,1,0:T(8,128)(2,1)}, bf16[8,256,256]{2,1,0:T(8,128)(2,1)}, u32[]{:S(2)}, u32[]{:S(2)}) collective-permute-start(bf16[8,256,256]{2,1,0:T(8,128)(2,1)} %refs_0_.1), channel_id=1, source_target_pairs={{0,128},{1,385},{128,256},{129,1},{256,384},{257,129},{384,0},{385... | collective-permute-start | bytes 3145736 | tf_op jit(solution)/shard_map/ppermute | solution.py:129
  26.6 15.0 %collective-permute-start.4 = (bf16[4,256,256]{2,1,0:T(8,128)(2,1)S(1)}, bf16[4,256,256]{2,1,0:T(8,128)(2,1)S(1)}, u32[]{:S(2)}, u32[]{:S(2)}) collective-permute-start(bf16[4,256,256]{2,1,0:T(8,128)(2,1)S(1)} %constant_dynamic-slice_fusion.1), channel_id=1, source_target_pairs={{0,256},{1,257},{128,384},{129,385},{256,0},{257,1},{384,128},{385... | collective-permute-start | bytes 1572872 | tf_op jit(solution)/shard_map/ppermute | solution.py:129
  30.8 30.1 %all-to-all-start = ((bf16[16,48,256]{2,1,0:T(8,128)(2,1)}), bf16[16,48,256]{2,1,0:T(8,128)(2,1)S(1)}, u32[]{:S(2)}, u32[]{:S(2)}) async-start(bf16[16,48,256]{2,1,0:T(8,128)(2,1)} %pad_maximum_fusion), calls=%async_computation | async-start | bytes 786432 | tf_op jit(solution)/shard_map/all_to_all | solution.py:172
  41.6 25.0 %collective-permute-start.5 = (bf16[8,256,256]{2,1,0:T(8,128)(2,1)}, bf16[8,256,256]{2,1,0:T(8,128)(2,1)S(1)}, u32[]{:S(2)}, u32[]{:S(2)}) collective-permute-start(bf16[8,256,256]{2,1,0:T(8,128)(2,1)} %collective-permute-done.3.refs_1_), channel_id=1, source_target_pairs={{0,1},{1,0},{2,3},{3,2},{4,5},{5,4},{6,7},{7,6},{8,9},{9,8},{10,11... | collective-permute-start | bytes 3145736 | tf_op jit(solution)/shard_map/ppermute | solution.py:121
  58.4 8.2 %collective-permute-start.6 = (bf16[4,256,256]{2,1,0:T(8,128)(2,1)S(1)}, bf16[4,256,256]{2,1,0:T(8,128)(2,1)}, u32[]{:S(2)}, u32[]{:S(2)}) collective-permute-start(bf16[4,256,256]{2,1,0:T(8,128)(2,1)S(1)} %collective-permute-done.4.refs_2_), channel_id=1, source_target_pairs={{0,1},{1,0},{2,3},{3,2},{4,5},{5,4},{6,7},{7,6},{8,9},{9,8},{10,11... | collective-permute-start | bytes 1572872 | tf_op jit(solution)/shard_map/ppermute | solution.py:121
  64.3 2.3 %copy-start.1 = (bf16[32,20,16,256]{3,2,1,0:T(8,128)(2,1)}, bf16[32,20,16,256]{3,2,1,0:T(8,128)(2,1)S(1)}, u32[]{:S(2)}) copy-start(bf16[32,20,16,256]{3,2,1,0:T(8,128)(2,1)S(1)} %halves.2.half_a) | copy-start | bytes 15728644
  68.6 1.7 %copy-start.2 = (bf16[32,12,16,256]{3,2,1,0:T(8,128)(2,1)}, bf16[32,12,16,256]{3,2,1,0:T(8,128)(2,1)S(1)}, u32[]{:S(2)}) copy-start(bf16[32,12,16,256]{3,2,1,0:T(8,128)(2,1)S(1)} %halves.3.half_b) | copy-start | bytes 9437188
Sparse Core Ops, SparseCore 0:
  9.5 58.1 all-gather.1

commit v7 on v6

--- a/solution.py
+++ b/solution.py
@@ -10,8 +10,8 @@
 X = XB * XA
 AXIS_X, SEC, MPO = ("xb", "xa"), ("xb", "xa", "z"), ("y", "c")
 BF16, F32 = jnp.bfloat16, jnp.float32
-TAG_ROWS = 16
-STEPS = 4
+TAG_ROWS = 8
+STEPS = 2
 
 
 def half_kernel(packet_ref, *refs):
@@ -53,8 +53,8 @@
     part = each // C
     near, away = 1 + 2 * core, 3 - 2 * core
     runs = (
-        ((each, 0, 0), (each, near, 0), (part, 2, core * part)),
-        ((each, away, 0), (part, 2, (1 - core) * part)),
+        ((each, 0, 0), (each, near, 0)),
+        ((part, 2, core * part), (each, away, 0), (part, 2, (1 - core) * part)),
     )
     own = tag_ref.shape[1] // (X * each)
 
@@ -156,9 +156,7 @@
     ]
     tags = jnp.concatenate(tags, axis=1).astype(BF16)
     tags = jnp.pad(tags, ((0, TAG_ROWS - 1), (0, width - tags.shape[1])))
-    sent, _ = lax.optimization_barrier((psi_blocks, tags))
-    psi_next = both_ways(sent, 1)
-    psi_far = both_ways(lax.dynamic_slice_in_dim(sent, core * part, part, 0), 2)
+    psi_next = both_ways(psi_blocks, 1)
     left = lax.dynamic_slice_in_dim(left_env, xa * terms, terms, 0)
     left = left.reshape(terms, shards, rows, width).transpose(1, 0, 2, 3)
     packet = jnp.concatenate(
@@ -168,13 +166,14 @@
         ],
         axis=1,
     )
-    psi_next, psi_far, _ = lax.optimization_barrier((psi_next, psi_far, packet))
+    psi_next, _ = lax.optimization_barrier((psi_next, packet))
+    psi_far = both_ways(lax.dynamic_slice_in_dim(psi_next, core * part, part, 0), 1)
     packet = lax.all_to_all(packet, MPO, split_axis=0, concat_axis=0, tiled=True)
     tags = packet[:, terms * rows, : X * terms * sectors].astype(jnp.int32)
     place = jnp.stack([xb, core]).astype(jnp.int32)
-    half_a = halves(packet, [psi_blocks, psi_next, psi_far], shards * terms, rows)
-    theirs = [moved(psi_next, "c", C, 1), moved(psi_far, "c", C, 1)]
-    half_b = halves(packet, theirs, shards * terms, rows)
+    half_a = halves(packet, [psi_blocks, psi_next], shards * terms, rows)
+    rest = [psi_far, moved(psi_next, "c", C, 1), moved(psi_far, "c", C, 1)]
+    half_b = halves(packet, rest, shards * terms, rows)
     partial = sums(place, tags, half_a, half_b, rights, XA * Z * sectors, STEPS)
     partial = partial.reshape(XA * Z, sectors, rows, width)
     partial = lax.all_to_all(partial, ("xa", "z"), split_axis=0, concat_axis=0, tiled=True)

time: 124 us -> 121 us (0.976)
  the two profiles are of different devices: /device:TPU:1 before, /device:TPU:4 now
where the time goes in v7:
time: 121 us
  blocking collectives  38.7 us (32%)
  starting transfers between devices  27.8 us (23%)
  waiting for transfers between devices  16.3 us (13%)
  between operations  13.6 us (11%)
  Pallas kernels  13.5 us (11%)
  local copies, waits for them, and re-layouts  7.57 us (6%)
  other arithmetic  3.57 us (3%)
    all_to_all x1, blocking collectives, on_device(): lax.all_to_all(partial, ('xa', 'z'), split_axis=0, concat_axis=0, tiled=T...  38.7 us
    ppermute x5, starting transfers between devices, moved(): lax.ppermute(block, axis, [(i, (i + by) % size) for i in range(size)])  17.5 us
    all_to_all x1, waiting for transfers between devices, on_device(): lax.all_to_all(packet, MPO, split_axis=0, concat_axis=0, tiled=True)  11.3 us
    pallas_call x1, Pallas kernels, sums(): pl.pallas_call(sums_kernel, grid_spec=pltpu.PrefetchScalarGridSpec(num_sc...  9.59 us
    ppermute x2, starting transfers between devices, both_ways(): return lax.ppermute(block, (*AXIS_X, 'c'), pairs)  6.76 us
    unnamed x8, local copies, waits for them, and re-layouts  4.98 us
    pallas_call x2, Pallas kernels, halves(): pl.pallas_call(half_kernel, out_shape=jax.ShapeDtypeStruct((terms, count,...  3.89 us
    all_to_all x1, starting transfers between devices, on_device(): lax.all_to_all(packet, MPO, split_axis=0, concat_axis=0, tiled=True)  3.55 us
  transfers between devices with their start and end apart: 9, of which 4 were waited for; matrix products, arithmetic and copies ran while one was open for 4% of the time, Pallas kernels for 3%

profile of v7, /device:TPU:4, one launch (start us, length us, event | category | flops | bytes accessed | tf_op | source)
XLA Modules:
  0.0 120.9 jit_solution(6187357975810804538)
XLA Ops:
  6.5 1.0 copy-done
  7.6 0.7 constant_dynamic-slice_fusion
  8.3 0.0 all-gather.2.cloned.1.call-update
  8.3 3.1 %collective-permute-start.3 = (bf16[8,256,256]{2,1,0:T(8,128)(2,1)}, bf16[8,256,256]{2,1,0:T(8,128)(2,1)S(1)}, u32[]{:S(2)}, u32[]{:S(2)}) collective-permute-start(bf16[8,256,256]{2,1,0:T(8,128)(2,1)} %refs_0_.1), channel_id=1, source_target_pairs={{0,128},{1,385},{128,256},{129,1},{256,384},{257,129},{384,0},{385... | collective-permute-start | bytes 3145736 | tf_op jit(solution)/shard_map/ppermute | solution.py:129
  11.5 0.7 bitcast_add_fusion
  12.1 0.1 fusion.13
  12.2 7.7 %collective-permute-start = (s32[1,16]{1,0:T(1,128)S(1)}, s32[1,16]{1,0:T(1,128)S(1)}, u32[]{:S(2)}, u32[]{:S(2)}) collective-permute-start(s32[1,16]{1,0:T(1,128)S(1)} %get-tuple-element.9), channel_id=1, source_target_pairs={{0,128},{128,256},{256,384},{384,0},{1,129},{129,257},{257,385},{3... | collective-permute-start | bytes 200 | tf_op jit(solution)/shard_map/ppermute | solution.py:121
  20.0 1.9 %collective-permute-start.2 = (s32[1,16]{1,0:T(1,128)S(1)}, s32[1,16]{1,0:T(1,128)S(1)}, u32[]{:S(2)}, u32[]{:S(2)}) collective-permute-start(s32[1,16]{1,0:T(1,128)S(1)} %get-tuple-element.9), channel_id=1, source_target_pairs={{0,384},{128,0},{256,128},{384,256},{1,385},{129,1},{257,129},{385... | collective-permute-start | bytes 200 | tf_op jit(solution)/shard_map/ppermute | solution.py:121
  21.9 4.0 %collective-permute-start.1 = (s32[1,16]{1,0:T(1,128)S(1)}, s32[1,16]{1,0:T(1,128)S(1)}, u32[]{:S(2)}, u32[]{:S(2)}) collective-permute-start(s32[1,16]{1,0:T(1,128)S(1)} %get-tuple-element.8), channel_id=1, source_target_pairs={{0,256},{128,384},{256,0},{384,128},{1,257},{129,385},{257,1},{385... | collective-permute-start | bytes 200 | tf_op jit(solution)/shard_map/ppermute | solution.py:121
  25.9 1.0 constant_dynamic-slice_fusion.2
  26.9 0.0 collective-permute-done.2
  26.9 2.2 %collective-permute-done.1 = s32[1,16]{1,0:T(1,128)S(1)} collective-permute-done((s32[1,16]{1,0:T(1,128)S(1)}, s32[1,16]{1,0:T(1,128)S(1)}, u32[]{:S(2)}, u32[]{:S(2)}) %collective-permute-start.1) | collective-permute-done | bytes 96 | tf_op jit(solution)/shard_map/ppermute | solution.py:121
  29.1 0.1 fusion.8
  29.2 0.8 pad_maximum_fusion
  30.0 0.0 collective-permute-done.3.refs_1_
  30.0 0.8 constant_dynamic-slice_fusion.1
  30.8 3.6 %collective-permute-start.4 = (bf16[4,256,256]{2,1,0:T(8,128)(2,1)}, bf16[4,256,256]{2,1,0:T(8,128)(2,1)S(1)}, u32[]{:S(2)}, u32[]{:S(2)}) collective-permute-start(bf16[4,256,256]{2,1,0:T(8,128)(2,1)} %constant_dynamic-slice_fusion.1), channel_id=1, source_target_pairs={{0,128},{1,385},{128,256},{129,1},{256,384},{257,129},{384,0},{385... | collective-permute-start | bytes 1572872 | tf_op jit(solution)/shard_map/ppermute | solution.py:129
  34.5 1.9 %collective-permute-start.5 = (bf16[8,256,256]{2,1,0:T(8,128)(2,1)S(1)}, bf16[8,256,256]{2,1,0:T(8,128)(2,1)}, u32[]{:S(2)}, u32[]{:S(2)}) collective-permute-start(bf16[8,256,256]{2,1,0:T(8,128)(2,1)S(1)} %collective-permute-done.3.refs_1_), channel_id=1, source_target_pairs={{0,1},{1,0},{2,3},{3,2},{4,5},{5,4},{6,7},{7,6},{8,9},{9,8},{10,11... | collective-permute-start | bytes 3145736 | tf_op jit(solution)/shard_map/ppermute | solution.py:121
  36.4 3.6 %all-to-all-start = ((bf16[16,40,256]{2,1,0:T(8,128)(2,1)}), bf16[16,40,256]{2,1,0:T(8,128)(2,1)S(1)}, u32[]{:S(2)}, u32[]{:S(2)}) async-start(bf16[16,40,256]{2,1,0:T(8,128)(2,1)} %pad_maximum_fusion), calls=%async_computation | async-start | bytes 655360 | tf_op jit(solution)/shard_map/all_to_all | solution.py:171
  40.0 2.1 %collective-permute-done.4.refs_0_ = bf16[4,256,256]{2,1,0:T(8,128)(2,1)S(1)} collective-permute-done((bf16[4,256,256]{2,1,0:T(8,128)(2,1)}, bf16[4,256,256]{2,1,0:T(8,128)(2,1)S(1)}, u32[]{:S(2)}, u32[]{:S(2)}) %collective-permute-start.4) | collective-permute-done | bytes 524320 | tf_op jit(solution)/shard_map/ppermute | solution.py:129
  42.1 1.9 %collective-permute-start.6 = (bf16[4,256,256]{2,1,0:T(8,128)(2,1)S(1)}, bf16[4,256,256]{2,1,0:T(8,128)(2,1)}, u32[]{:S(2)}, u32[]{:S(2)}) collective-permute-start(bf16[4,256,256]{2,1,0:T(8,128)(2,1)S(1)} %collective-permute-done.4.refs_0_), channel_id=1, source_target_pairs={{0,1},{1,0},{2,3},{3,2},{4,5},{5,4},{6,7},{7,6},{8,9},{9,8},{10,11... | collective-permute-start | bytes 1572872 | tf_op jit(solution)/shard_map/ppermute | solution.py:121
  44.0 0.6 pad_add_fusion.place_ref
  44.6 11.3 %all-to-all-done.packet_ref = bf16[16,40,256]{2,1,0:T(8,128)(2,1)S(1)} async-done(((bf16[16,40,256]{2,1,0:T(8,128)(2,1)}), bf16[16,40,256]{2,1,0:T(8,128)(2,1)S(1)}, u32[]{:S(2)}, u32[]{:S(2)}) %all-to-all-start) | async-done | bytes 327712 | tf_op jit(solution)/shard_map/all_to_all | solution.py:171
  55.8 0.6 fusion.12.tag_ref
  56.4 1.3 %halves.2.half_a = bf16[32,16,16,256]{3,2,1,0:T(8,128)(2,1)S(1)} custom-call(bf16[16,40,256]{2,1,0:T(8,128)(2,1)S(1)} %all-to-all-done.packet_ref, bf16[8,256,256]{2,1,0:T(8,128)(2,1)S(1)} %copy-done.3, bf16[8,256,256]{2,1,0:T(8,128)(2,1)S(1)} %collective-permute-done.3.refs_1_), custom_call_target="tpu_custom_call" | custom-call | flops 1073741824 | bytes 6291456 | tf_op jit(solution)/shard_map/halves/pallas_call | solution.py:33
  57.7 2.0 %copy-done.1 = bf16[32,16,16,256]{3,2,1,0:T(8,128)(2,1)} copy-done((bf16[32,16,16,256]{3,2,1,0:T(8,128)(2,1)}, bf16[32,16,16,256]{3,2,1,0:T(8,128)(2,1)S(1)}, u32[]{:S(2)}) %copy-start.1) | copy-done | bytes 4194328
  59.7 2.6 %halves.3.half_b = bf16[32,16,16,256]{3,2,1,0:T(8,128)(2,1)S(1)} custom-call(bf16[16,40,256]{2,1,0:T(8,128)(2,1)S(1)} %all-to-all-done.packet_ref, bf16[4,256,256]{2,1,0:T(8,128)(2,1)S(1)} %collective-permute-done.4.refs_0_, bf16[8,256,256]{2,1,0:T(8,128)(2,1)} %collective-permute-done.5.refs_1_, bf16[4,256,256]{2,1,0:T(8,128)(2,1)} %collective-permute-done.6.refs_2_), custom_call_target="tpu_custom_call" | custom-call | flops 1073741824 | bytes 6291456 | tf_op jit(solution)/shard_map/halves/pallas_call | solution.py:33
  62.3 2.0 %copy-done.2 = bf16[32,16,16,256]{3,2,1,0:T(8,128)(2,1)} copy-done((bf16[32,16,16,256]{3,2,1,0:T(8,128)(2,1)}, bf16[32,16,16,256]{3,2,1,0:T(8,128)(2,1)S(1)}, u32[]{:S(2)}) %copy-start.2) | copy-done | bytes 4194328
  64.3 0.7 all-gather.2.cloned.1.call-done.right_ref
  65.0 9.6 %sums.1 = bf16[128,16,256]{2,1,0:T(8,128)(2,1)} custom-call(s32[2]{0:T(128)} %pad_add_fusion.place_ref, s32[16,64]{1,0:T(8,128)} %fusion.12.tag_ref, bf16[32,16,16,256]{3,2,1,0:T(8,128)(2,1)} %copy-done.1, bf16[32,16,16,256]{3,2,1,0:T(8,128)(2,1)} %copy-done.2, bf16[32,256,256]{2,1,0:T(8,128)(2,1)} %all-gather.2.cloned.1.call-done.right_ref), custom_call_target="tpu_custom_call" | custom-call | flops 2147483648 | bytes 12582912 | tf_op jit(solution)/shard_map/sums/pallas_call | solution.py:96
  74.6 38.7 %all_to_all.10 = bf16[16,8,16,256]{3,2,1,0:T(8,128)(2,1)S(1)} all-to-all(bf16[16,8,16,256]{3,2,1,0:T(8,128)(2,1)} %bitcast.28), channel_id=1, replica_groups=mesh['xb'=2,'xa'=2,'z'=8,'y'=8,'c'=2] {'xa','z'}, dimensions={0} | all-to-all | bytes 2097152 | tf_op jit(solution)/shard_map/all_to_all | solution.py:179
  113.3 0.8 convert_add_fusion
  (15 shorter events, 0.1 us)
Async XLA Ops:
  6.5 1.0 copy-start
  6.5 49.9 %copy-start.3 = (bf16[8,256,256]{2,1,0:T(8,128)(2,1)S(1)}, bf16[8,256,256]{2,1,0:T(8,128)(2,1)}, u32[]{:S(2)}) copy-start(bf16[8,256,256]{2,1,0:T(8,128)(2,1)} %refs_0_.1) | copy-start | bytes 3145732
  6.5 58.4 %all-gather.2.cloned.1.call-start = ((), (), s32[]{:S(2)}) async-start(), calls=%async_computation.2 | async-start | bytes 4456448 | tf_op jit(solution)/shard_map/all_gather | solution.py:147
  8.3 21.6 %collective-permute-start.3 = (bf16[8,256,256]{2,1,0:T(8,128)(2,1)}, bf16[8,256,256]{2,1,0:T(8,128)(2,1)S(1)}, u32[]{:S(2)}, u32[]{:S(2)}) collective-permute-start(bf16[8,256,256]{2,1,0:T(8,128)(2,1)} %refs_0_.1), channel_id=1, source_target_pairs={{0,128},{1,385},{128,256},{129,1},{256,384},{257,129},{384,0},{385... | collective-permute-start | bytes 3145736 | tf_op jit(solution)/shard_map/ppermute | solution.py:129
  12.2 14.7 %collective-permute-start = (s32[1,16]{1,0:T(1,128)S(1)}, s32[1,16]{1,0:T(1,128)S(1)}, u32[]{:S(2)}, u32[]{:S(2)}) collective-permute-start(s32[1,16]{1,0:T(1,128)S(1)} %get-tuple-element.9), channel_id=1, source_target_pairs={{0,128},{128,256},{256,384},{384,0},{1,129},{129,257},{257,385},{3... | collective-permute-start | bytes 200 | tf_op jit(solution)/shard_map/ppermute | solution.py:121
  20.0 6.9 %collective-permute-start.2 = (s32[1,16]{1,0:T(1,128)S(1)}, s32[1,16]{1,0:T(1,128)S(1)}, u32[]{:S(2)}, u32[]{:S(2)}) collective-permute-start(s32[1,16]{1,0:T(1,128)S(1)} %get-tuple-element.9), channel_id=1, source_target_pairs={{0,384},{128,0},{256,128},{384,256},{1,385},{129,1},{257,129},{385... | collective-permute-start | bytes 200 | tf_op jit(solution)/shard_map/ppermute | solution.py:121
  21.9 7.2 %collective-permute-start.1 = (s32[1,16]{1,0:T(1,128)S(1)}, s32[1,16]{1,0:T(1,128)S(1)}, u32[]{:S(2)}, u32[]{:S(2)}) collective-permute-start(s32[1,16]{1,0:T(1,128)S(1)} %get-tuple-element.8), channel_id=1, source_target_pairs={{0,256},{128,384},{256,0},{384,128},{1,257},{129,385},{257,1},{385... | collective-permute-start | bytes 200 | tf_op jit(solution)/shard_map/ppermute | solution.py:121
  30.8 11.3 %collective-permute-start.4 = (bf16[4,256,256]{2,1,0:T(8,128)(2,1)}, bf16[4,256,256]{2,1,0:T(8,128)(2,1)S(1)}, u32[]{:S(2)}, u32[]{:S(2)}) collective-permute-start(bf16[4,256,256]{2,1,0:T(8,128)(2,1)} %constant_dynamic-slice_fusion.1), channel_id=1, source_target_pairs={{0,128},{1,385},{128,256},{129,1},{256,384},{257,129},{384,0},{385... | collective-permute-start | bytes 1572872 | tf_op jit(solution)/shard_map/ppermute | solution.py:129
  34.5 25.2 %collective-permute-start.5 = (bf16[8,256,256]{2,1,0:T(8,128)(2,1)S(1)}, bf16[8,256,256]{2,1,0:T(8,128)(2,1)}, u32[]{:S(2)}, u32[]{:S(2)}) collective-permute-start(bf16[8,256,256]{2,1,0:T(8,128)(2,1)S(1)} %collective-permute-done.3.refs_1_), channel_id=1, source_target_pairs={{0,1},{1,0},{2,3},{3,2},{4,5},{5,4},{6,7},{7,6},{8,9},{9,8},{10,11... | collective-permute-start | bytes 3145736 | tf_op jit(solution)/shard_map/ppermute | solution.py:121
  36.4 19.4 %all-to-all-start = ((bf16[16,40,256]{2,1,0:T(8,128)(2,1)}), bf16[16,40,256]{2,1,0:T(8,128)(2,1)S(1)}, u32[]{:S(2)}, u32[]{:S(2)}) async-start(bf16[16,40,256]{2,1,0:T(8,128)(2,1)} %pad_maximum_fusion), calls=%async_computation | async-start | bytes 655360 | tf_op jit(solution)/shard_map/all_to_all | solution.py:171
  42.1 17.6 %collective-permute-start.6 = (bf16[4,256,256]{2,1,0:T(8,128)(2,1)S(1)}, bf16[4,256,256]{2,1,0:T(8,128)(2,1)}, u32[]{:S(2)}, u32[]{:S(2)}) collective-permute-start(bf16[4,256,256]{2,1,0:T(8,128)(2,1)S(1)} %collective-permute-done.4.refs_0_), channel_id=1, source_target_pairs={{0,1},{1,0},{2,3},{3,2},{4,5},{5,4},{6,7},{7,6},{8,9},{9,8},{10,11... | collective-permute-start | bytes 1572872 | tf_op jit(solution)/shard_map/ppermute | solution.py:121
  57.7 2.0 %copy-start.1 = (bf16[32,16,16,256]{3,2,1,0:T(8,128)(2,1)}, bf16[32,16,16,256]{3,2,1,0:T(8,128)(2,1)S(1)}, u32[]{:S(2)}) copy-start(bf16[32,16,16,256]{3,2,1,0:T(8,128)(2,1)S(1)} %halves.2.half_a) | copy-start | bytes 12582916
  62.3 2.0 %copy-start.2 = (bf16[32,16,16,256]{3,2,1,0:T(8,128)(2,1)}, bf16[32,16,16,256]{3,2,1,0:T(8,128)(2,1)S(1)}, u32[]{:S(2)}) copy-start(bf16[32,16,16,256]{3,2,1,0:T(8,128)(2,1)S(1)} %halves.3.half_b) | copy-start | bytes 12582916
Sparse Core Ops, SparseCore 0:
  9.5 55.4 all-gather.1

commit v8 on v7

--- a/solution.py
+++ b/solution.py
@@ -10,15 +10,13 @@
 X = XB * XA
 AXIS_X, SEC, MPO = ("xb", "xa"), ("xb", "xa", "z"), ("y", "c")
 BF16, F32 = jnp.bfloat16, jnp.float32
-TAG_ROWS = 8
 STEPS = 2
 
 
-def half_kernel(packet_ref, *refs):
+def half_kernel(left_ref, *refs):
     half_ref = refs[-1]
-    shards, _, width = packet_ref.shape
-    terms, _, rows, _ = half_ref.shape
-    lefts = packet_ref[:, : terms // shards * rows, :].reshape(terms * rows, width)
+    terms, _, rows, width = half_ref.shape
+    lefts = left_ref[...]
     at = 0
     for psi_ref in refs[:-1]:
         for k in range(psi_ref.shape[0]):
@@ -27,9 +25,10 @@
             at += 1
 
 
-def halves(packet, pieces, terms, rows):
+def halves(lefts, pieces, terms):
     count = sum(p.shape[0] for p in pieces)
-    width = packet.shape[2]
+    width = lefts.shape[1]
+    rows = lefts.shape[0] // terms
     return pl.pallas_call(
         half_kernel,
         out_shape=jax.ShapeDtypeStruct((terms, count, rows, width), BF16),
@@ -40,23 +39,25 @@
             transcendentals=0,
         ),
         name="halves",
-    )(packet, *pieces)
+    )(lefts, *pieces)
 
 
 def sums_kernel(place_ref, tag_ref, half_a, half_b, right_ref, out_ref, *total_refs):
     step = pl.program_id(0)
     terms, sectors_a, rows, width = half_a.shape
     sectors_b = half_b.shape[1]
-    xb, core = place_ref[0], place_ref[1]
+    x, core = place_ref[0], place_ref[1]
+    xb = x // XA
     count = out_ref.shape[0]
     each = (sectors_a + sectors_b) // X
     part = each // C
-    near, away = 1 + 2 * core, 3 - 2 * core
+    near, far, away = (x + X - 1 + 2 * core) % X, (x + 2) % X, (x + 1 + 2 * core) % X
     runs = (
-        ((each, 0, 0), (each, near, 0)),
-        ((part, 2, core * part), (each, away, 0), (part, 2, (1 - core) * part)),
+        ((each, x, 0), (each, near, 0)),
+        ((part, far, core * part), (each, away, 0), (part, far, (1 - core) * part)),
     )
-    own = tag_ref.shape[1] // (X * each)
+    own = tag_ref.shape[1] // each
+    shards = tag_ref.shape[0] // X
 
     @pl.when(step == 0)
     def _():
@@ -74,7 +75,7 @@
             s = 0
             for length, shard, first in some:
                 for k in range(length):
-                    t = tag_ref[row, (shard * own + w % own) * each + first + k] - xb * count
+                    t = tag_ref[shard * shards + row, w % own * each + first + k] - xb * count
                     t = jnp.where((t >= 0) & (t < count), t, count)
                     total_ref = total_refs[turn % len(total_refs)]
                     total_ref[t] += full[s]
@@ -145,35 +146,25 @@
     xb, xa, core = lax.axis_index("xb"), lax.axis_index("xa"), lax.axis_index("c")
     right = lax.dynamic_slice_in_dim(right_env, xa * terms, terms, 0)
     rights = lax.all_gather(right, MPO, axis=0, tiled=True)
-    target = (dest_index[0, 0, :, 0] * sectors + dest_slot[0, 0])[None]
-    same = lax.dynamic_slice_in_dim(target, xa * terms * sectors, terms * sectors, 1)
-    other = lax.dynamic_slice_in_dim(target, (1 - xa) * terms * sectors, terms * sectors, 1)
-    tags = [
-        same,
-        moved(other, AXIS_X, X, 1),
-        moved(same, AXIS_X, X, 2),
-        moved(other, AXIS_X, X, -1),
-    ]
-    tags = jnp.concatenate(tags, axis=1).astype(BF16)
-    tags = jnp.pad(tags, ((0, TAG_ROWS - 1), (0, width - tags.shape[1])))
-    psi_next = both_ways(psi_blocks, 1)
     left = lax.dynamic_slice_in_dim(left_env, xa * terms, terms, 0)
     left = left.reshape(terms, shards, rows, width).transpose(1, 0, 2, 3)
-    packet = jnp.concatenate(
-        [
-            left.reshape(shards, terms * rows, width),
-            jnp.broadcast_to(tags[None], (shards, TAG_ROWS, width)),
-        ],
-        axis=1,
+    left = left.reshape(shards, terms * rows, width)
+    lefts = lax.all_to_all(left, MPO, split_axis=0, concat_axis=0, tiled=True)
+    psi_next = both_ways(psi_blocks, 1)
+    target = dest_index[0, 0, :, 0] * sectors + dest_slot[0, 0]
+    lefts, psi_next, target = lax.optimization_barrier((lefts, psi_next, target))
+    psi_far = both_ways(lax.dynamic_slice_in_dim(psi_next, core * part, part, 0), 1)
+    target = jnp.broadcast_to(
+        target.reshape(1, XA, 1, terms * sectors), (XB, XA, shards, terms * sectors)
     )
-    psi_next, _ = lax.optimization_barrier((psi_next, packet))
-    psi_far = both_ways(lax.dynamic_slice_in_dim(psi_next, core * part, part, 0), 1)
-    packet = lax.all_to_all(packet, MPO, split_axis=0, concat_axis=0, tiled=True)
-    tags = packet[:, terms * rows, : X * terms * sectors].astype(jnp.int32)
-    place = jnp.stack([xb, core]).astype(jnp.int32)
-    half_a = halves(packet, [psi_blocks, psi_next], shards * terms, rows)
+    tags = lax.all_to_all(
+        target.reshape(X * shards, -1), (*AXIS_X, *MPO), split_axis=0, concat_axis=0, tiled=True
+    )
+    place = jnp.stack([xb * XA + xa, core]).astype(jnp.int32)
+    lefts = lefts.reshape(shards * terms * rows, width)
+    half_a = halves(lefts, [psi_blocks, psi_next], shards * terms)
     rest = [psi_far, moved(psi_next, "c", C, 1), moved(psi_far, "c", C, 1)]
-    half_b = halves(packet, rest, shards * terms, rows)
+    half_b = halves(lefts, rest, shards * terms)
     partial = sums(place, tags, half_a, half_b, rights, XA * Z * sectors, STEPS)
     partial = partial.reshape(XA * Z, sectors, rows, width)
     partial = lax.all_to_all(partial, ("xa", "z"), split_axis=0, concat_axis=0, tiled=True)

time: 121 us -> 120 us (level)
  the two profiles are of different devices: /device:TPU:4 before, /device:TPU:1 now
where the time goes in v8:
time: 120 us; the launch traced here: 118 us
  blocking collectives  36.4 us (30%)
  starting transfers between devices  27.6 us (23%)
  waiting for transfers between devices  16.6 us (14%)
  Pallas kernels  13.5 us (11%)
  between operations  13.5 us (11%)
  local copies, waits for them, and re-layouts  8.73 us (7%)
  other arithmetic  2.07 us (2%)
    all_to_all x1, blocking collectives, on_device(): lax.all_to_all(partial, ('xa', 'z'), split_axis=0, concat_axis=0, tiled=T...  36.4 us
    all_to_all x1, waiting for transfers between devices, on_device(): lefts = lax.all_to_all(left, MPO, split_axis=0, concat_axis=0, tiled=True)  11.1 us
    ppermute x2, starting transfers between devices, both_ways(): return lax.ppermute(block, (*AXIS_X, 'c'), pairs)  9.93 us
    pallas_call x1, Pallas kernels, sums(): pl.pallas_call(sums_kernel, grid_spec=pltpu.PrefetchScalarGridSpec(num_sc...  9.58 us
    all_to_all x1, starting transfers between devices, on_device(): lefts = lax.all_to_all(left, MPO, split_axis=0, concat_axis=0, tiled=True)  7.23 us
    all_to_all x1, starting transfers between devices, on_device(): lax.all_to_all(target.reshape(X * shards, -1), (*AXIS_X, *MPO), split_axi...  5.6 us
    unnamed x10, local copies, waits for them, and re-layouts  5.56 us
    ppermute x2, starting transfers between devices, moved(): lax.ppermute(block, axis, [(i, (i + by) % size) for i in range(size)])  4.84 us
  transfers between devices with their start and end apart: 7, of which 3 were waited for; matrix products, arithmetic and copies ran while one was open for 3% of the time, Pallas kernels for 3%

profile of v8, /device:TPU:1, one launch (start us, length us, event | category | flops | bytes accessed | tf_op | source)
XLA Modules:
  0.0 118.4 jit_solution(12624473970870257167)
XLA Ops:
  6.5 0.0 copy-start
  6.5 0.0 all-gather.2.cloned.1.call-start
  6.5 1.0 copy-done
  7.6 0.7 constant_dynamic-slice_fusion
  8.3 0.0 all-gather.2.cloned.1.call-update
  8.3 5.2 %collective-permute-start = (bf16[8,256,256]{2,1,0:T(8,128)(2,1)}, bf16[8,256,256]{2,1,0:T(8,128)(2,1)S(1)}, u32[]{:S(2)}, u32[]{:S(2)}) collective-permute-start(bf16[8,256,256]{2,1,0:T(8,128)(2,1)} %refs_0_.1), channel_id=1, source_target_pairs={{0,128},{1,385},{128,256},{129,1},{256,384},{257,129},{384,0},{385... | collective-permute-start | bytes 3145736 | tf_op jit(solution)/shard_map/ppermute | solution.py:130
  13.6 1.0 constant_dynamic-slice_fusion.2
  14.5 0.7 copy.7
  15.3 7.2 %all-to-all-start = ((bf16[16,32,256]{2,1,0:T(8,128)(2,1)}), bf16[16,32,256]{2,1,0:T(8,128)(2,1)S(1)}, u32[]{:S(2)}, u32[]{:S(2)}) async-start(bf16[16,32,256]{2,1,0:T(8,128)(2,1)} %bitcast.4), calls=%async_computation | async-start | bytes 524288 | tf_op jit(solution)/shard_map/all_to_all | solution.py:152
  22.5 0.7 bitcast_add_fusion
  23.2 11.1 %all-to-all-done = bf16[16,32,256]{2,1,0:T(8,128)(2,1)S(1)} async-done(((bf16[16,32,256]{2,1,0:T(8,128)(2,1)}), bf16[16,32,256]{2,1,0:T(8,128)(2,1)S(1)}, u32[]{:S(2)}, u32[]{:S(2)}) %all-to-all-start) | async-done | bytes 262176 | tf_op jit(solution)/shard_map/all_to_all | solution.py:152
  34.2 0.0 collective-permute-done.refs_1_
  34.3 4.7 %collective-permute-start.1 = (bf16[4,256,256]{2,1,0:T(8,128)(2,1)S(1)}, bf16[4,256,256]{2,1,0:T(8,128)(2,1)S(1)}, u32[]{:S(2)}, u32[]{:S(2)}) collective-permute-start(bf16[4,256,256]{2,1,0:T(8,128)(2,1)S(1)} %constant_dynamic-slice_fusion.1), channel_id=1, source_target_pairs={{0,128},{1,385},{128,256},{129,1},{256,384},{257,129},{384,0},{385... | collective-permute-start | bytes 1572872 | tf_op jit(solution)/shard_map/ppermute | solution.py:130
  39.0 1.9 %collective-permute-start.2 = (bf16[8,256,256]{2,1,0:T(8,128)(2,1)S(1)}, bf16[8,256,256]{2,1,0:T(8,128)(2,1)}, u32[]{:S(2)}, u32[]{:S(2)}) collective-permute-start(bf16[8,256,256]{2,1,0:T(8,128)(2,1)S(1)} %collective-permute-done.refs_1_), channel_id=1, source_target_pairs={{0,1},{1,0},{2,3},{3,2},{4,5},{5,4},{6,7},{7,6},{8,9},{9,8},{10,11... | collective-permute-start | bytes 3145736 | tf_op jit(solution)/shard_map/ppermute | solution.py:122
  40.9 4.2 %collective-permute-done.1.refs_0_ = bf16[4,256,256]{2,1,0:T(8,128)(2,1)S(1)} collective-permute-done((bf16[4,256,256]{2,1,0:T(8,128)(2,1)S(1)}, bf16[4,256,256]{2,1,0:T(8,128)(2,1)S(1)}, u32[]{:S(2)}, u32[]{:S(2)}) %collective-permute-start.1) | collective-permute-done | bytes 524320 | tf_op jit(solution)/shard_map/ppermute | solution.py:130
  45.1 2.9 %collective-permute-start.3 = (bf16[4,256,256]{2,1,0:T(8,128)(2,1)S(1)}, bf16[4,256,256]{2,1,0:T(8,128)(2,1)}, u32[]{:S(2)}, u32[]{:S(2)}) collective-permute-start(bf16[4,256,256]{2,1,0:T(8,128)(2,1)S(1)} %collective-permute-done.1.refs_0_), channel_id=1, source_target_pairs={{0,1},{1,0},{2,3},{3,2},{4,5},{5,4},{6,7},{7,6},{8,9},{9,8},{10,11... | collective-permute-start | bytes 1572872 | tf_op jit(solution)/shard_map/ppermute | solution.py:122
  48.0 0.6 pad_add_fusion.place_ref
  48.6 0.1 broadcast_in_dim.7
  48.7 0.6 broadcast_in_dim.8
  49.3 5.6 %all-to-all-start.1 = ((s32[64,1,16]{2,1,0:T(1,128)}), s32[64,1,16]{2,1,0:T(1,128)S(1)}, u32[]{:S(2)}, u32[]{:S(2)}) async-start(s32[64,1,16]{2,1,0:T(1,128)} %bitcast.7), calls=%async_computation.1 | async-start | bytes 65536 | tf_op jit(solution)/shard_map/all_to_all | solution.py:160
  54.9 0.0 copy-done.3
  54.9 1.3 %halves.2.half_a = bf16[32,16,16,256]{3,2,1,0:T(8,128)(2,1)S(1)} custom-call(bf16[512,256]{1,0:T(8,128)(2,1)S(1)} %bitcast.21, bf16[8,256,256]{2,1,0:T(8,128)(2,1)S(1)} %copy-done.3, bf16[8,256,256]{2,1,0:T(8,128)(2,1)S(1)} %collective-permute-done.refs_1_), custom_call_target="tpu_custom_call" | custom-call | flops 1073741824 | bytes 6291456 | tf_op jit(solution)/shard_map/halves/pallas_call | solution.py:32
  56.2 2.0 %copy-done.1 = bf16[32,16,16,256]{3,2,1,0:T(8,128)(2,1)} copy-done((bf16[32,16,16,256]{3,2,1,0:T(8,128)(2,1)}, bf16[32,16,16,256]{3,2,1,0:T(8,128)(2,1)S(1)}, u32[]{:S(2)}) %copy-start.1) | copy-done | bytes 4194328
  58.2 0.0 collective-permute-done.3.refs_2_
  58.2 0.0 collective-permute-done.2.refs_1_
  58.2 2.6 %halves.3.half_b = bf16[32,16,16,256]{3,2,1,0:T(8,128)(2,1)S(1)} custom-call(bf16[512,256]{1,0:T(8,128)(2,1)S(1)} %bitcast.22, bf16[4,256,256]{2,1,0:T(8,128)(2,1)S(1)} %collective-permute-done.1.refs_0_, bf16[8,256,256]{2,1,0:T(8,128)(2,1)} %collective-permute-done.2.refs_1_, bf16[4,256,256]{2,1,0:T(8,128)(2,1)} %collective-permute-done.3.refs_2_), custom_call_target="tpu_custom_call" | custom-call | flops 1073741824 | bytes 6291456 | tf_op jit(solution)/shard_map/halves/pallas_call | solution.py:32
  60.8 2.0 %copy-done.2 = bf16[32,16,16,256]{3,2,1,0:T(8,128)(2,1)} copy-done((bf16[32,16,16,256]{3,2,1,0:T(8,128)(2,1)}, bf16[32,16,16,256]{3,2,1,0:T(8,128)(2,1)S(1)}, u32[]{:S(2)}) %copy-start.2) | copy-done | bytes 4194328
  62.7 1.4 %all-to-all-done.1 = s32[64,1,16]{2,1,0:T(1,128)S(1)} async-done(((s32[64,1,16]{2,1,0:T(1,128)}), s32[64,1,16]{2,1,0:T(1,128)S(1)}, u32[]{:S(2)}, u32[]{:S(2)}) %all-to-all-start.1) | async-done | bytes 4128 | tf_op jit(solution)/shard_map/all_to_all | solution.py:160
  64.1 0.6 copy-done.4
  64.7 9.6 %sums.1 = bf16[128,16,256]{2,1,0:T(8,128)(2,1)} custom-call(s32[2]{0:T(128)} %pad_add_fusion.place_ref, s32[64,16]{1,0:T(8,128)} %bitcast.25, bf16[32,16,16,256]{3,2,1,0:T(8,128)(2,1)} %copy-done.1, bf16[32,16,16,256]{3,2,1,0:T(8,128)(2,1)} %copy-done.2, bf16[32,256,256]{2,1,0:T(8,128)(2,1)} %all-gather.2.cloned.1.call-done.right_ref), custom_call_target="tpu_custom_call" | custom-call | flops 2147483648 | bytes 12582912 | tf_op jit(solution)/shard_map/sums/pallas_call | solution.py:97
  74.3 36.4 %all_to_all.21 = bf16[16,8,16,256]{3,2,1,0:T(8,128)(2,1)S(1)} all-to-all(bf16[16,8,16,256]{3,2,1,0:T(8,128)(2,1)} %bitcast.23), channel_id=1, replica_groups=mesh['xb'=2,'xa'=2,'z'=8,'y'=8,'c'=2] {'xa','z'}, dimensions={0} | all-to-all | bytes 2097152 | tf_op jit(solution)/shard_map/all_to_all | solution.py:170
  110.7 0.8 convert_add_fusion
  (6 shorter events, 0.0 us)
Async XLA Ops:
  6.5 1.0 copy-start
  6.5 48.4 %copy-start.3 = (bf16[8,256,256]{2,1,0:T(8,128)(2,1)S(1)}, bf16[8,256,256]{2,1,0:T(8,128)(2,1)}, u32[]{:S(2)}) copy-start(bf16[8,256,256]{2,1,0:T(8,128)(2,1)} %refs_0_.1) | copy-start | bytes 3145732
  6.5 57.6 %all-gather.2.cloned.1.call-start = ((), (), s32[]{:S(2)}) async-start(), calls=%async_computation.3 | async-start | bytes 4456448 | tf_op jit(solution)/shard_map/all_gather | solution.py:148
  8.3 25.9 %collective-permute-start = (bf16[8,256,256]{2,1,0:T(8,128)(2,1)}, bf16[8,256,256]{2,1,0:T(8,128)(2,1)S(1)}, u32[]{:S(2)}, u32[]{:S(2)}) collective-permute-start(bf16[8,256,256]{2,1,0:T(8,128)(2,1)} %refs_0_.1), channel_id=1, source_target_pairs={{0,128},{1,385},{128,256},{129,1},{256,384},{257,129},{384,0},{385... | collective-permute-start | bytes 3145736 | tf_op jit(solution)/shard_map/ppermute | solution.py:130
  15.3 19.0 %all-to-all-start = ((bf16[16,32,256]{2,1,0:T(8,128)(2,1)}), bf16[16,32,256]{2,1,0:T(8,128)(2,1)S(1)}, u32[]{:S(2)}, u32[]{:S(2)}) async-start(bf16[16,32,256]{2,1,0:T(8,128)(2,1)} %bitcast.4), calls=%async_computation | async-start | bytes 524288 | tf_op jit(solution)/shard_map/all_to_all | solution.py:152
  34.3 10.8 %collective-permute-start.1 = (bf16[4,256,256]{2,1,0:T(8,128)(2,1)S(1)}, bf16[4,256,256]{2,1,0:T(8,128)(2,1)S(1)}, u32[]{:S(2)}, u32[]{:S(2)}) collective-permute-start(bf16[4,256,256]{2,1,0:T(8,128)(2,1)S(1)} %constant_dynamic-slice_fusion.1), channel_id=1, source_target_pairs={{0,128},{1,385},{128,256},{129,1},{256,384},{257,129},{384,0},{385... | collective-permute-start | bytes 1572872 | tf_op jit(solution)/shard_map/ppermute | solution.py:130
  39.0 19.2 %collective-permute-start.2 = (bf16[8,256,256]{2,1,0:T(8,128)(2,1)S(1)}, bf16[8,256,256]{2,1,0:T(8,128)(2,1)}, u32[]{:S(2)}, u32[]{:S(2)}) collective-permute-start(bf16[8,256,256]{2,1,0:T(8,128)(2,1)S(1)} %collective-permute-done.refs_1_), channel_id=1, source_target_pairs={{0,1},{1,0},{2,3},{3,2},{4,5},{5,4},{6,7},{7,6},{8,9},{9,8},{10,11... | collective-permute-start | bytes 3145736 | tf_op jit(solution)/shard_map/ppermute | solution.py:122
  45.1 13.1 %collective-permute-start.3 = (bf16[4,256,256]{2,1,0:T(8,128)(2,1)S(1)}, bf16[4,256,256]{2,1,0:T(8,128)(2,1)}, u32[]{:S(2)}, u32[]{:S(2)}) collective-permute-start(bf16[4,256,256]{2,1,0:T(8,128)(2,1)S(1)} %collective-permute-done.1.refs_0_), channel_id=1, source_target_pairs={{0,1},{1,0},{2,3},{3,2},{4,5},{5,4},{6,7},{7,6},{8,9},{9,8},{10,11... | collective-permute-start | bytes 1572872 | tf_op jit(solution)/shard_map/ppermute | solution.py:122
  49.3 14.8 %all-to-all-start.1 = ((s32[64,1,16]{2,1,0:T(1,128)}), s32[64,1,16]{2,1,0:T(1,128)S(1)}, u32[]{:S(2)}, u32[]{:S(2)}) async-start(s32[64,1,16]{2,1,0:T(1,128)} %bitcast.7), calls=%async_computation.1 | async-start | bytes 65536 | tf_op jit(solution)/shard_map/all_to_all | solution.py:160
  56.2 2.0 %copy-start.1 = (bf16[32,16,16,256]{3,2,1,0:T(8,128)(2,1)}, bf16[32,16,16,256]{3,2,1,0:T(8,128)(2,1)S(1)}, u32[]{:S(2)}) copy-start(bf16[32,16,16,256]{3,2,1,0:T(8,128)(2,1)S(1)} %halves.2.half_a) | copy-start | bytes 12582916
  60.8 2.0 %copy-start.2 = (bf16[32,16,16,256]{3,2,1,0:T(8,128)(2,1)}, bf16[32,16,16,256]{3,2,1,0:T(8,128)(2,1)S(1)}, u32[]{:S(2)}) copy-start(bf16[32,16,16,256]{3,2,1,0:T(8,128)(2,1)S(1)} %halves.3.half_b) | copy-start | bytes 12582916
  64.1 0.6 copy-start.4
Sparse Core Ops, SparseCore 0:
  9.5 51.2 all-gather.1

commit v9 on v8

--- a/solution.py
+++ b/solution.py
@@ -10,19 +10,23 @@
 X = XB * XA
 AXIS_X, SEC, MPO = ("xb", "xa"), ("xb", "xa", "z"), ("y", "c")
 BF16, F32 = jnp.bfloat16, jnp.float32
-STEPS = 2
+STEPS = 4
 
 
 def half_kernel(left_ref, *refs):
-    half_ref = refs[-1]
-    terms, _, rows, width = half_ref.shape
+    psi_refs, (half_ref, held_ref, sems) = refs[:-3], refs[-3:]
+    _, terms, rows, width = held_ref.shape
     lefts = left_ref[...]
-    at = 0
-    for psi_ref in refs[:-1]:
+    copies = []
+    for psi_ref in psi_refs:
         for k in range(psi_ref.shape[0]):
+            at = len(copies)
             out = jnp.dot(lefts, psi_ref[k], preferred_element_type=F32).astype(BF16)
-            half_ref[:, at] = out.reshape(terms, rows, width)
-            at += 1
+            held_ref[at] = out.reshape(terms, rows, width)
+            copies.append(pltpu.make_async_copy(held_ref.at[at], half_ref.at[at], sems.at[at]))
+            copies[-1].start()
+    for copy in copies:
+        copy.wait()
 
 
 def halves(lefts, pieces, terms):
@@ -31,7 +35,13 @@
     rows = lefts.shape[0] // terms
     return pl.pallas_call(
         half_kernel,
-        out_shape=jax.ShapeDtypeStruct((terms, count, rows, width), BF16),
+        in_specs=[pl.BlockSpec(memory_space=pltpu.VMEM)] * (1 + len(pieces)),
+        out_specs=pl.BlockSpec(memory_space=pltpu.HBM),
+        out_shape=pltpu.HBM((count, terms, rows, width), BF16),
+        scratch_shapes=[
+            pltpu.VMEM((count, terms, rows, width), BF16),
+            pltpu.SemaphoreType.DMA((count,)),
+        ],
         compiler_params=pltpu.CompilerParams(vmem_limit_bytes=16 << 20),
         cost_estimate=pl.CostEstimate(
             flops=2 * terms * rows * width * width * count,
@@ -44,8 +54,8 @@
 
 def sums_kernel(place_ref, tag_ref, half_a, half_b, right_ref, out_ref, *total_refs):
     step = pl.program_id(0)
-    terms, sectors_a, rows, width = half_a.shape
-    sectors_b = half_b.shape[1]
+    sectors_a, terms, rows, width = half_a.shape
+    sectors_b = half_b.shape[0]
     x, core = place_ref[0], place_ref[1]
     xb = x // XA
     count = out_ref.shape[0]
@@ -68,8 +78,8 @@
     for w in range(terms):
         row = step * (terms // own) + w // own
         for half_ref, some in zip((half_a, half_b), runs, strict=True):
-            number = half_ref.shape[1]
-            lhs = half_ref[w].reshape(number * rows, width)
+            number = half_ref.shape[0]
+            lhs = half_ref[:, w].reshape(number * rows, width)
             full = jnp.dot(lhs, right_ref[w], preferred_element_type=F32).astype(BF16)
             full = full.astype(F32).reshape(number, rows, width)
             s = 0
@@ -91,16 +101,16 @@
 
 
 def sums(place, tags, half_a, half_b, rights, count, steps):
-    terms, _, rows, width = half_a.shape
+    _, terms, rows, width = half_a.shape
     each = terms // steps
-    pairs = terms * (half_a.shape[1] + half_b.shape[1])
+    pairs = terms * (half_a.shape[0] + half_b.shape[0])
     return pl.pallas_call(
         sums_kernel,
         grid_spec=pltpu.PrefetchScalarGridSpec(
             num_scalar_prefetch=2,
             grid=(steps,),
             in_specs=[
-                pl.BlockSpec((each, h.shape[1], rows, width), lambda i, *_: (i, 0, 0, 0))
+                pl.BlockSpec((h.shape[0], each, rows, width), lambda i, *_: (0, i, 0, 0))
                 for h in (half_a, half_b)
             ]
             + [pl.BlockSpec((each, width, width), lambda i, *_: (i, 0, 0))],

time: 120 us -> 120 us (level)
  local copies, waits for them, and re-layouts: 8.73 us -> 4.81 us
  Pallas kernels: 13.5 us -> 16.2 us
  waiting for transfers between devices: 16.6 us -> 18.2 us
    unnamed x10 -> x6, local copies, waits for them, and re-layouts: 5.56 us -> 1.65 us
    pallas_call x2, Pallas kernels: 3.88 us -> 6.26 us  [halves(): pl.pallas_call(half_kernel, in_specs=[pl.BlockSpec(memory_space=pltpu.VME...]
    all_to_all x1, waiting for transfers between devices: 1.39 us -> 2.91 us  [on_device(): lax.all_to_all(target.reshape(X * shards, -1), (*AXIS_X, *MPO), split_axi...]
  transfers between devices with their start and end apart: 7 -> 7, of which waited for: 3 -> 3; matrix products, arithmetic and copies ran while one was open for 3% -> 3% of each run, Pallas kernels for 3% -> 5%
where the time goes in v9:
time: 120 us; the launch traced here: 119 us
  blocking collectives  36.4 us (30%)
  starting transfers between devices  27.6 us (23%)
  waiting for transfers between devices  18.2 us (15%)
  Pallas kernels  16.2 us (14%)
  between operations  13.5 us (11%)
  local copies, waits for them, and re-layouts  4.81 us (4%)
  other arithmetic  2.05 us (2%)
    all_to_all x1, blocking collectives, on_device(): lax.all_to_all(partial, ('xa', 'z'), split_axis=0, concat_axis=0, tiled=T...  36.4 us
    all_to_all x1, waiting for transfers between devices, on_device(): lefts = lax.all_to_all(left, MPO, split_axis=0, concat_axis=0, tiled=True)  11.1 us
    pallas_call x1, Pallas kernels, sums(): pl.pallas_call(sums_kernel, grid_spec=pltpu.PrefetchScalarGridSpec(num_sc...  9.97 us
    ppermute x2, starting transfers between devices, both_ways(): return lax.ppermute(block, (*AXIS_X, 'c'), pairs)  9.92 us
    all_to_all x1, starting transfers between devices, on_device(): lefts = lax.all_to_all(left, MPO, split_axis=0, concat_axis=0, tiled=True)  7.23 us
    pallas_call x2, Pallas kernels, halves(): pl.pallas_call(half_kernel, in_specs=[pl.BlockSpec(memory_space=pltpu.VME...  6.26 us
    all_to_all x1, starting transfers between devices, on_device(): lax.all_to_all(target.reshape(X * shards, -1), (*AXIS_X, *MPO), split_axi...  5.6 us
    ppermute x2, starting transfers between devices, moved(): lax.ppermute(block, axis, [(i, (i + by) % size) for i in range(size)])  4.84 us
  transfers between devices with their start and end apart: 7, of which 3 were waited for; matrix products, arithmetic and copies ran while one was open for 3% of the time, Pallas kernels for 5%

profile of v9, /device:TPU:1, one launch (start us, length us, event | category | flops | bytes accessed | tf_op | source)
XLA Modules:
  0.0 118.8 jit_solution(7108095991548252846)
XLA Ops:
  6.5 0.0 copy-start
  6.5 0.0 copy-start.1
  6.5 0.0 all-gather.2.cloned.1.call-start
  6.5 1.0 copy-done
  7.6 0.7 constant_dynamic-slice_fusion
  8.3 0.0 all-gather.2.cloned.1.call-update
  8.3 5.2 %collective-permute-start = (bf16[8,256,256]{2,1,0:T(8,128)(2,1)}, bf16[8,256,256]{2,1,0:T(8,128)(2,1)S(1)}, u32[]{:S(2)}, u32[]{:S(2)}) collective-permute-start(bf16[8,256,256]{2,1,0:T(8,128)(2,1)} %refs_0_.1), channel_id=1, source_target_pairs={{0,128},{1,385},{128,256},{129,1},{256,384},{257,129},{384,0},{385... | collective-permute-start | bytes 3145736 | tf_op jit(solution)/shard_map/ppermute | solution.py:140
  13.6 1.0 constant_dynamic-slice_fusion.2
  14.5 0.7 copy.7
  15.3 7.2 %all-to-all-start = ((bf16[16,32,256]{2,1,0:T(8,128)(2,1)}), bf16[16,32,256]{2,1,0:T(8,128)(2,1)S(1)}, u32[]{:S(2)}, u32[]{:S(2)}) async-start(bf16[16,32,256]{2,1,0:T(8,128)(2,1)} %bitcast.4), calls=%async_computation | async-start | bytes 524288 | tf_op jit(solution)/shard_map/all_to_all | solution.py:162
  22.5 0.7 bitcast_add_fusion
  23.2 11.1 %all-to-all-done = bf16[16,32,256]{2,1,0:T(8,128)(2,1)S(1)} async-done(((bf16[16,32,256]{2,1,0:T(8,128)(2,1)}), bf16[16,32,256]{2,1,0:T(8,128)(2,1)S(1)}, u32[]{:S(2)}, u32[]{:S(2)}) %all-to-all-start) | async-done | bytes 262176 | tf_op jit(solution)/shard_map/all_to_all | solution.py:162
  34.2 0.0 collective-permute-done.refs_1_
  34.3 4.7 %collective-permute-start.1 = (bf16[4,256,256]{2,1,0:T(8,128)(2,1)S(1)}, bf16[4,256,256]{2,1,0:T(8,128)(2,1)S(1)}, u32[]{:S(2)}, u32[]{:S(2)}) collective-permute-start(bf16[4,256,256]{2,1,0:T(8,128)(2,1)S(1)} %constant_dynamic-slice_fusion.1), channel_id=1, source_target_pairs={{0,128},{1,385},{128,256},{129,1},{256,384},{257,129},{384,0},{385... | collective-permute-start | bytes 1572872 | tf_op jit(solution)/shard_map/ppermute | solution.py:140
  39.0 1.9 %collective-permute-start.2 = (bf16[8,256,256]{2,1,0:T(8,128)(2,1)S(1)}, bf16[8,256,256]{2,1,0:T(8,128)(2,1)}, u32[]{:S(2)}, u32[]{:S(2)}) collective-permute-start(bf16[8,256,256]{2,1,0:T(8,128)(2,1)S(1)} %collective-permute-done.refs_1_), channel_id=1, source_target_pairs={{0,1},{1,0},{2,3},{3,2},{4,5},{5,4},{6,7},{7,6},{8,9},{9,8},{10,11... | collective-permute-start | bytes 3145736 | tf_op jit(solution)/shard_map/ppermute | solution.py:132
  40.9 4.2 %collective-permute-done.1.refs_0_ = bf16[4,256,256]{2,1,0:T(8,128)(2,1)S(1)} collective-permute-done((bf16[4,256,256]{2,1,0:T(8,128)(2,1)S(1)}, bf16[4,256,256]{2,1,0:T(8,128)(2,1)S(1)}, u32[]{:S(2)}, u32[]{:S(2)}) %collective-permute-start.1) | collective-permute-done | bytes 524320 | tf_op jit(solution)/shard_map/ppermute | solution.py:140
  45.1 2.9 %collective-permute-start.3 = (bf16[4,256,256]{2,1,0:T(8,128)(2,1)S(1)}, bf16[4,256,256]{2,1,0:T(8,128)(2,1)}, u32[]{:S(2)}, u32[]{:S(2)}) collective-permute-start(bf16[4,256,256]{2,1,0:T(8,128)(2,1)S(1)} %collective-permute-done.1.refs_0_), channel_id=1, source_target_pairs={{0,1},{1,0},{2,3},{3,2},{4,5},{5,4},{6,7},{7,6},{8,9},{9,8},{10,11... | collective-permute-start | bytes 1572872 | tf_op jit(solution)/shard_map/ppermute | solution.py:132
  48.0 0.6 pad_add_fusion.place_ref
  48.6 0.1 broadcast_in_dim.7
  48.7 0.6 broadcast_in_dim.8
  49.3 5.6 %all-to-all-start.1 = ((s32[64,1,16]{2,1,0:T(1,128)}), s32[64,1,16]{2,1,0:T(1,128)S(1)}, u32[]{:S(2)}, u32[]{:S(2)}) async-start(s32[64,1,16]{2,1,0:T(1,128)} %bitcast.7), calls=%async_computation.1 | async-start | bytes 65536 | tf_op jit(solution)/shard_map/all_to_all | solution.py:170
  54.9 0.0 copy-done.1
  54.9 2.5 %halves.2.half_a = bf16[16,32,16,256]{3,2,1,0:T(8,128)(2,1)} custom-call(bf16[512,256]{1,0:T(8,128)(2,1)S(1)} %bitcast.21, bf16[8,256,256]{2,1,0:T(8,128)(2,1)S(1)} %copy-done.1, bf16[8,256,256]{2,1,0:T(8,128)(2,1)S(1)} %collective-permute-done.refs_1_), custom_call_target="tpu_custom_call" | custom-call | flops 1073741824 | bytes 6291456 | tf_op jit(solution)/shard_map/halves/pallas_call | solution.py:36
  57.4 0.0 collective-permute-done.3.refs_2_
  57.4 0.0 collective-permute-done.2.refs_1_
  57.4 3.8 %halves.3.half_b = bf16[16,32,16,256]{3,2,1,0:T(8,128)(2,1)} custom-call(bf16[512,256]{1,0:T(8,128)(2,1)S(1)} %bitcast.22, bf16[4,256,256]{2,1,0:T(8,128)(2,1)S(1)} %collective-permute-done.1.refs_0_, bf16[8,256,256]{2,1,0:T(8,128)(2,1)} %collective-permute-done.2.refs_1_, bf16[4,256,256]{2,1,0:T(8,128)(2,1)} %collective-permute-done.3.refs_2_), custom_call_target="tpu_custom_call" | custom-call | flops 1073741824 | bytes 6291456 | tf_op jit(solution)/shard_map/halves/pallas_call | solution.py:36
  61.2 2.9 %all-to-all-done.1 = s32[64,1,16]{2,1,0:T(1,128)S(1)} async-done(((s32[64,1,16]{2,1,0:T(1,128)}), s32[64,1,16]{2,1,0:T(1,128)S(1)}, u32[]{:S(2)}, u32[]{:S(2)}) %all-to-all-start.1) | async-done | bytes 4128 | tf_op jit(solution)/shard_map/all_to_all | solution.py:170
  64.1 0.0 copy-start.2
  64.1 0.6 copy-done.2
  64.7 10.0 %sums.1 = bf16[128,16,256]{2,1,0:T(8,128)(2,1)} custom-call(s32[2]{0:T(128)} %pad_add_fusion.place_ref, s32[64,16]{1,0:T(8,128)} %bitcast.25, bf16[16,32,16,256]{3,2,1,0:T(8,128)(2,1)} %halves.2.half_a, bf16[16,32,16,256]{3,2,1,0:T(8,128)(2,1)} %halves.3.half_b, bf16[32,256,256]{2,1,0:T(8,128)(2,1)} %all-gather.2.cloned.1.call-done.right_ref), custom_call_target="tpu_custom_call" | custom-call | flops 2147483648 | bytes 12582912 | tf_op jit(solution)/shard_map/sums/pallas_call | solution.py:107
  74.7 36.4 %all_to_all.21 = bf16[16,8,16,256]{3,2,1,0:T(8,128)(2,1)S(1)} all-to-all(bf16[16,8,16,256]{3,2,1,0:T(8,128)(2,1)} %bitcast.23), channel_id=1, replica_groups=mesh['xb'=2,'xa'=2,'z'=8,'y'=8,'c'=2] {'xa','z'}, dimensions={0} | all-to-all | bytes 2097152 | tf_op jit(solution)/shard_map/all_to_all | solution.py:180
  111.1 0.8 convert_add_fusion
  (2 shorter events, 0.0 us)
Async XLA Ops:
  6.5 1.0 copy-start
  6.5 48.4 %copy-start.1 = (bf16[8,256,256]{2,1,0:T(8,128)(2,1)S(1)}, bf16[8,256,256]{2,1,0:T(8,128)(2,1)}, u32[]{:S(2)}) copy-start(bf16[8,256,256]{2,1,0:T(8,128)(2,1)} %refs_0_.1) | copy-start | bytes 3145732
  6.5 57.6 %all-gather.2.cloned.1.call-start = ((), (), s32[]{:S(2)}) async-start(), calls=%async_computation.3 | async-start | bytes 4456448 | tf_op jit(solution)/shard_map/all_gather | solution.py:158
  8.3 25.9 %collective-permute-start = (bf16[8,256,256]{2,1,0:T(8,128)(2,1)}, bf16[8,256,256]{2,1,0:T(8,128)(2,1)S(1)}, u32[]{:S(2)}, u32[]{:S(2)}) collective-permute-start(bf16[8,256,256]{2,1,0:T(8,128)(2,1)} %refs_0_.1), channel_id=1, source_target_pairs={{0,128},{1,385},{128,256},{129,1},{256,384},{257,129},{384,0},{385... | collective-permute-start | bytes 3145736 | tf_op jit(solution)/shard_map/ppermute | solution.py:140
  15.3 19.0 %all-to-all-start = ((bf16[16,32,256]{2,1,0:T(8,128)(2,1)}), bf16[16,32,256]{2,1,0:T(8,128)(2,1)S(1)}, u32[]{:S(2)}, u32[]{:S(2)}) async-start(bf16[16,32,256]{2,1,0:T(8,128)(2,1)} %bitcast.4), calls=%async_computation | async-start | bytes 524288 | tf_op jit(solution)/shard_map/all_to_all | solution.py:162
  34.3 10.8 %collective-permute-start.1 = (bf16[4,256,256]{2,1,0:T(8,128)(2,1)S(1)}, bf16[4,256,256]{2,1,0:T(8,128)(2,1)S(1)}, u32[]{:S(2)}, u32[]{:S(2)}) collective-permute-start(bf16[4,256,256]{2,1,0:T(8,128)(2,1)S(1)} %constant_dynamic-slice_fusion.1), channel_id=1, source_target_pairs={{0,128},{1,385},{128,256},{129,1},{256,384},{257,129},{384,0},{385... | collective-permute-start | bytes 1572872 | tf_op jit(solution)/shard_map/ppermute | solution.py:140
  39.0 18.4 %collective-permute-start.2 = (bf16[8,256,256]{2,1,0:T(8,128)(2,1)S(1)}, bf16[8,256,256]{2,1,0:T(8,128)(2,1)}, u32[]{:S(2)}, u32[]{:S(2)}) collective-permute-start(bf16[8,256,256]{2,1,0:T(8,128)(2,1)S(1)} %collective-permute-done.refs_1_), channel_id=1, source_target_pairs={{0,1},{1,0},{2,3},{3,2},{4,5},{5,4},{6,7},{7,6},{8,9},{9,8},{10,11... | collective-permute-start | bytes 3145736 | tf_op jit(solution)/shard_map/ppermute | solution.py:132
  45.1 12.3 %collective-permute-start.3 = (bf16[4,256,256]{2,1,0:T(8,128)(2,1)S(1)}, bf16[4,256,256]{2,1,0:T(8,128)(2,1)}, u32[]{:S(2)}, u32[]{:S(2)}) collective-permute-start(bf16[4,256,256]{2,1,0:T(8,128)(2,1)S(1)} %collective-permute-done.1.refs_0_), channel_id=1, source_target_pairs={{0,1},{1,0},{2,3},{3,2},{4,5},{5,4},{6,7},{7,6},{8,9},{9,8},{10,11... | collective-permute-start | bytes 1572872 | tf_op jit(solution)/shard_map/ppermute | solution.py:132
  49.3 14.8 %all-to-all-start.1 = ((s32[64,1,16]{2,1,0:T(1,128)}), s32[64,1,16]{2,1,0:T(1,128)S(1)}, u32[]{:S(2)}, u32[]{:S(2)}) async-start(s32[64,1,16]{2,1,0:T(1,128)} %bitcast.7), calls=%async_computation.1 | async-start | bytes 65536 | tf_op jit(solution)/shard_map/all_to_all | solution.py:170
  64.1 0.6 copy-start.2
Sparse Core Ops, SparseCore 0:
  9.5 51.2 all-gather.1

commit v10 on v9

--- a/solution.py
+++ b/solution.py
@@ -156,20 +156,18 @@
     xb, xa, core = lax.axis_index("xb"), lax.axis_index("xa"), lax.axis_index("c")
     right = lax.dynamic_slice_in_dim(right_env, xa * terms, terms, 0)
     rights = lax.all_gather(right, MPO, axis=0, tiled=True)
+    target = (dest_index[0, 0, :, 0] * sectors + dest_slot[0, 0]).reshape(1, XA, 1, -1)
+    target = jnp.broadcast_to(target, (XB, XA, shards, terms * sectors))
+    tags = lax.all_to_all(
+        target.reshape(X * shards, -1), (*AXIS_X, *MPO), split_axis=0, concat_axis=0, tiled=True
+    )
+    psi_next = both_ways(psi_blocks, 1)
     left = lax.dynamic_slice_in_dim(left_env, xa * terms, terms, 0)
     left = left.reshape(terms, shards, rows, width).transpose(1, 0, 2, 3)
     left = left.reshape(shards, terms * rows, width)
+    tags, psi_next, left = lax.optimization_barrier((tags, psi_next, left))
     lefts = lax.all_to_all(left, MPO, split_axis=0, concat_axis=0, tiled=True)
-    psi_next = both_ways(psi_blocks, 1)
-    target = dest_index[0, 0, :, 0] * sectors + dest_slot[0, 0]
-    lefts, psi_next, target = lax.optimization_barrier((lefts, psi_next, target))
     psi_far = both_ways(lax.dynamic_slice_in_dim(psi_next, core * part, part, 0), 1)
-    target = jnp.broadcast_to(
-        target.reshape(1, XA, 1, terms * sectors), (XB, XA, shards, terms * sectors)
-    )
-    tags = lax.all_to_all(
-        target.reshape(X * shards, -1), (*AXIS_X, *MPO), split_axis=0, concat_axis=0, tiled=True
-    )
     place = jnp.stack([xb * XA + xa, core]).astype(jnp.int32)
     lefts = lefts.reshape(shards * terms * rows, width)
     half_a = halves(lefts, [psi_blocks, psi_next], shards * terms)

time: 120 us -> 120 us (level)
  waiting for transfers between devices: 18.2 us -> 16.5 us
  blocking collectives: 36.4 us -> 34.9 us
  other arithmetic: 2.05 us -> 3.46 us
    all_to_all x1, waiting for transfers between devices: 2.91 us -> 7.52 us  [on_device(): lax.all_to_all(target.reshape(X * shards, -1), (*AXIS_X, *MPO), split_axi...]
    all_to_all x1, waiting for transfers between devices: 11.1 us -> 7.01 us  [on_device(): lefts = lax.all_to_all(left, MPO, split_axis=0, concat_axis=0, tiled=True)]
    all_to_all x1, starting transfers between devices: 5.6 us -> 9.51 us  [on_device(): lax.all_to_all(target.reshape(X * shards, -1), (*AXIS_X, *MPO), split_axi...]
    all_to_all x1, starting transfers between devices: 7.23 us -> 3.44 us  [on_device(): lefts = lax.all_to_all(left, MPO, split_axis=0, concat_axis=0, tiled=True)]
    ppermute x2, waiting for transfers between devices: 4.18 us -> 1.9 us  [both_ways(): return lax.ppermute(block, (*AXIS_X, 'c'), pairs)]
    ppermute x2, starting transfers between devices: 4.84 us -> 7.05 us  [moved(): lax.ppermute(block, axis, [(i, (i + by) % size) for i in range(size)])]
    ppermute x2, starting transfers between devices: 9.92 us -> 7.87 us  [both_ways(): return lax.ppermute(block, (*AXIS_X, 'c'), pairs)]
    all_to_all x1, blocking collectives: 36.4 us -> 34.9 us  [on_device(): lax.all_to_all(partial, ('xa', 'z'), split_axis=0, concat_axis=0, tiled=T...]
  transfers between devices with their start and end apart: 7 -> 7, of which waited for: 3 -> 3; matrix products, arithmetic and copies ran while one was open for 3% -> 6% of each run, Pallas kernels for 5% -> 5%
where the time goes in v10:
time: 120 us; the launch traced here: 118 us
  blocking collectives  34.9 us (29%)
  starting transfers between devices  27.9 us (23%)
  waiting for transfers between devices  16.5 us (14%)
  Pallas kernels  16.3 us (14%)
  between operations  13.5 us (11%)
  local copies, waits for them, and re-layouts  5.63 us (5%)
  other arithmetic  3.46 us (3%)
    all_to_all x1, blocking collectives, on_device(): lax.all_to_all(partial, ('xa', 'z'), split_axis=0, concat_axis=0, tiled=T...  34.9 us
    pallas_call x1, Pallas kernels, sums(): pl.pallas_call(sums_kernel, grid_spec=pltpu.PrefetchScalarGridSpec(num_sc...  9.93 us
    all_to_all x1, starting transfers between devices, on_device(): lax.all_to_all(target.reshape(X * shards, -1), (*AXIS_X, *MPO), split_axi...  9.51 us
    ppermute x2, starting transfers between devices, both_ways(): return lax.ppermute(block, (*AXIS_X, 'c'), pairs)  7.87 us
    all_to_all x1, waiting for transfers between devices, on_device(): lax.all_to_all(target.reshape(X * shards, -1), (*AXIS_X, *MPO), split_axi...  7.52 us
    ppermute x2, starting transfers between devices, moved(): lax.ppermute(block, axis, [(i, (i + by) % size) for i in range(size)])  7.05 us
    all_to_all x1, waiting for transfers between devices, on_device(): lefts = lax.all_to_all(left, MPO, split_axis=0, concat_axis=0, tiled=True)  7.01 us
    pallas_call x2, Pallas kernels, halves(): pl.pallas_call(half_kernel, in_specs=[pl.BlockSpec(memory_space=pltpu.VME...  6.36 us
  transfers between devices with their start and end apart: 7, of which 3 were waited for; matrix products, arithmetic and copies ran while one was open for 6% of the time, Pallas kernels for 5%

profile of v10, /device:TPU:1, one launch (start us, length us, event | category | flops | bytes accessed | tf_op | source)
XLA Modules:
  0.0 118.1 jit_solution(10971874180953438127)
XLA Ops:
  6.5 1.0 copy-done
  7.6 0.7 constant_dynamic-slice_fusion
  8.3 0.0 all-gather.2.cloned.1.call-update
  8.3 5.2 %collective-permute-start = (bf16[8,256,256]{2,1,0:T(8,128)(2,1)}, bf16[8,256,256]{2,1,0:T(8,128)(2,1)S(1)}, u32[]{:S(2)}, u32[]{:S(2)}) collective-permute-start(bf16[8,256,256]{2,1,0:T(8,128)(2,1)} %refs_0_.1), channel_id=1, source_target_pairs={{0,128},{1,385},{128,256},{129,1},{256,384},{257,129},{384,0},{385... | collective-permute-start | bytes 3145736 | tf_op jit(solution)/shard_map/ppermute | solution.py:140
  13.5 0.5 broadcast.12
  14.1 1.3 %reduce.7 = s32[32]{0:T(128)S(1)} reduce(s32[1,1,32]{2,1,0:T(1,128)} %param.9, s32[]{:T(128)} %broadcast.12), dimensions={0,1}, to_apply=%param.9.reduce_sub_computation.3 | reduce | bytes 260 | tf_op args[4]
  15.4 0.1 squeeze.2
  15.5 0.7 multiply_reduce_fusion
  16.1 0.1 mul.26
  16.2 0.6 broadcast_in_dim.2
  16.8 9.5 %all-to-all-start = ((s32[64,1,16]{2,1,0:T(1,128)}), s32[64,1,16]{2,1,0:T(1,128)S(1)}, u32[]{:S(2)}, u32[]{:S(2)}) async-start(s32[64,1,16]{2,1,0:T(1,128)} %bitcast.2), calls=%async_computation | async-start | bytes 65536 | tf_op jit(solution)/shard_map/all_to_all | solution.py:161
  26.4 1.0 constant_dynamic-slice_fusion.2
  27.3 0.8 copy.7
  28.1 7.5 %all-to-all-done = s32[64,1,16]{2,1,0:T(1,128)S(1)} async-done(((s32[64,1,16]{2,1,0:T(1,128)}), s32[64,1,16]{2,1,0:T(1,128)S(1)}, u32[]{:S(2)}, u32[]{:S(2)}) %all-to-all-start) | async-done | bytes 4128 | tf_op jit(solution)/shard_map/all_to_all | solution.py:161
  35.6 0.0 collective-permute-done.refs_1_
  35.6 0.8 constant_dynamic-slice_fusion.1
  36.5 2.7 %collective-permute-start.1 = (bf16[4,256,256]{2,1,0:T(8,128)(2,1)}, bf16[4,256,256]{2,1,0:T(8,128)(2,1)S(1)}, u32[]{:S(2)}, u32[]{:S(2)}) collective-permute-start(bf16[4,256,256]{2,1,0:T(8,128)(2,1)} %constant_dynamic-slice_fusion.1), channel_id=1, source_target_pairs={{0,128},{1,385},{128,256},{129,1},{256,384},{257,129},{384,0},{385... | collective-permute-start | bytes 1572872 | tf_op jit(solution)/shard_map/ppermute | solution.py:140
  39.1 2.5 %collective-permute-start.2 = (bf16[8,256,256]{2,1,0:T(8,128)(2,1)S(1)}, bf16[8,256,256]{2,1,0:T(8,128)(2,1)}, u32[]{:S(2)}, u32[]{:S(2)}) collective-permute-start(bf16[8,256,256]{2,1,0:T(8,128)(2,1)S(1)} %collective-permute-done.refs_1_), channel_id=1, source_target_pairs={{0,1},{1,0},{2,3},{3,2},{4,5},{5,4},{6,7},{7,6},{8,9},{9,8},{10,11... | collective-permute-start | bytes 3145736 | tf_op jit(solution)/shard_map/ppermute | solution.py:132
  41.6 3.4 %all-to-all-start.1 = ((bf16[16,32,256]{2,1,0:T(8,128)(2,1)}), bf16[16,32,256]{2,1,0:T(8,128)(2,1)S(1)}, u32[]{:S(2)}, u32[]{:S(2)}) async-start(bf16[16,32,256]{2,1,0:T(8,128)(2,1)} %bitcast.21), calls=%async_computation.1 | async-start | bytes 524288 | tf_op jit(solution)/shard_map/all_to_all | solution.py:169
  45.1 1.9 %collective-permute-done.1.refs_0_ = bf16[4,256,256]{2,1,0:T(8,128)(2,1)S(1)} collective-permute-done((bf16[4,256,256]{2,1,0:T(8,128)(2,1)}, bf16[4,256,256]{2,1,0:T(8,128)(2,1)S(1)}, u32[]{:S(2)}, u32[]{:S(2)}) %collective-permute-start.1) | collective-permute-done | bytes 524320 | tf_op jit(solution)/shard_map/ppermute | solution.py:140
  47.0 4.5 %collective-permute-start.3 = (bf16[4,256,256]{2,1,0:T(8,128)(2,1)S(1)}, bf16[4,256,256]{2,1,0:T(8,128)(2,1)}, u32[]{:S(2)}, u32[]{:S(2)}) collective-permute-start(bf16[4,256,256]{2,1,0:T(8,128)(2,1)S(1)} %collective-permute-done.1.refs_0_), channel_id=1, source_target_pairs={{0,1},{1,0},{2,3},{3,2},{4,5},{5,4},{6,7},{7,6},{8,9},{9,8},{10,11... | collective-permute-start | bytes 1572872 | tf_op jit(solution)/shard_map/ppermute | solution.py:132
  51.5 0.7 pad_add_fusion.place_ref
  52.2 7.0 %all-to-all-done.1 = bf16[16,32,256]{2,1,0:T(8,128)(2,1)S(1)} async-done(((bf16[16,32,256]{2,1,0:T(8,128)(2,1)}), bf16[16,32,256]{2,1,0:T(8,128)(2,1)S(1)}, u32[]{:S(2)}, u32[]{:S(2)}) %all-to-all-start.1) | async-done | bytes 262176 | tf_op jit(solution)/shard_map/all_to_all | solution.py:169
  59.2 2.5 %halves.2.half_a = bf16[16,32,16,256]{3,2,1,0:T(8,128)(2,1)} custom-call(bf16[512,256]{1,0:T(8,128)(2,1)S(1)} %bitcast.17, bf16[8,256,256]{2,1,0:T(8,128)(2,1)S(1)} %copy-done.1, bf16[8,256,256]{2,1,0:T(8,128)(2,1)S(1)} %collective-permute-done.refs_1_), custom_call_target="tpu_custom_call" | custom-call | flops 1073741824 | bytes 6291456 | tf_op jit(solution)/shard_map/halves/pallas_call | solution.py:36
  61.7 0.0 collective-permute-done.3.refs_2_
  61.7 0.0 collective-permute-done.2.refs_1_
  61.7 3.9 %halves.3.half_b = bf16[16,32,16,256]{3,2,1,0:T(8,128)(2,1)} custom-call(bf16[512,256]{1,0:T(8,128)(2,1)S(1)} %bitcast.18, bf16[4,256,256]{2,1,0:T(8,128)(2,1)S(1)} %collective-permute-done.1.refs_0_, bf16[8,256,256]{2,1,0:T(8,128)(2,1)} %collective-permute-done.2.refs_1_, bf16[4,256,256]{2,1,0:T(8,128)(2,1)} %collective-permute-done.3.refs_2_), custom_call_target="tpu_custom_call" | custom-call | flops 1073741824 | bytes 6291456 | tf_op jit(solution)/shard_map/halves/pallas_call | solution.py:36
  65.6 0.0 copy-done.2
  65.6 0.0 all-gather.2.cloned.1.call-done.right_ref
  65.7 9.9 %sums.1 = bf16[128,16,256]{2,1,0:T(8,128)(2,1)} custom-call(s32[2]{0:T(128)} %pad_add_fusion.place_ref, s32[64,16]{1,0:T(8,128)} %bitcast.22, bf16[16,32,16,256]{3,2,1,0:T(8,128)(2,1)} %halves.2.half_a, bf16[16,32,16,256]{3,2,1,0:T(8,128)(2,1)} %halves.3.half_b, bf16[32,256,256]{2,1,0:T(8,128)(2,1)} %all-gather.2.cloned.1.call-done.right_ref), custom_call_target="tpu_custom_call" | custom-call | flops 2147483648 | bytes 12582912 | tf_op jit(solution)/shard_map/sums/pallas_call | solution.py:107
  75.6 34.9 %all_to_all.22 = bf16[16,8,16,256]{3,2,1,0:T(8,128)(2,1)S(1)} all-to-all(bf16[16,8,16,256]{3,2,1,0:T(8,128)(2,1)} %bitcast.19), channel_id=1, replica_groups=mesh['xb'=2,'xa'=2,'z'=8,'y'=8,'c'=2] {'xa','z'}, dimensions={0} | all-to-all | bytes 2097152 | tf_op jit(solution)/shard_map/all_to_all | solution.py:178
  110.5 0.8 convert_add_fusion
  (6 shorter events, 0.0 us)
Async XLA Ops:
  6.5 1.0 copy-start
  6.5 52.7 %copy-start.1 = (bf16[8,256,256]{2,1,0:T(8,128)(2,1)S(1)}, bf16[8,256,256]{2,1,0:T(8,128)(2,1)}, u32[]{:S(2)}) copy-start(bf16[8,256,256]{2,1,0:T(8,128)(2,1)} %refs_0_.1) | copy-start | bytes 3145732
  6.5 59.1 %all-gather.2.cloned.1.call-start = ((), (), s32[]{:S(2)}) async-start(), calls=%async_computation.3 | async-start | bytes 4456448 | tf_op jit(solution)/shard_map/all_gather | solution.py:158
  8.3 27.3 %collective-permute-start = (bf16[8,256,256]{2,1,0:T(8,128)(2,1)}, bf16[8,256,256]{2,1,0:T(8,128)(2,1)S(1)}, u32[]{:S(2)}, u32[]{:S(2)}) collective-permute-start(bf16[8,256,256]{2,1,0:T(8,128)(2,1)} %refs_0_.1), channel_id=1, source_target_pairs={{0,128},{1,385},{128,256},{129,1},{256,384},{257,129},{384,0},{385... | collective-permute-start | bytes 3145736 | tf_op jit(solution)/shard_map/ppermute | solution.py:140
  16.8 18.8 %all-to-all-start = ((s32[64,1,16]{2,1,0:T(1,128)}), s32[64,1,16]{2,1,0:T(1,128)S(1)}, u32[]{:S(2)}, u32[]{:S(2)}) async-start(s32[64,1,16]{2,1,0:T(1,128)} %bitcast.2), calls=%async_computation | async-start | bytes 65536 | tf_op jit(solution)/shard_map/all_to_all | solution.py:161
  35.6 30.0 %copy-start.2 = (s32[64,1,16]{2,1,0:T(1,128)}, s32[64,1,16]{2,1,0:T(1,128)S(1)}, u32[]{:S(2)}) copy-start(s32[64,1,16]{2,1,0:T(1,128)S(1)} %all-to-all-done) | copy-start | bytes 12292
  36.5 10.5 %collective-permute-start.1 = (bf16[4,256,256]{2,1,0:T(8,128)(2,1)}, bf16[4,256,256]{2,1,0:T(8,128)(2,1)S(1)}, u32[]{:S(2)}, u32[]{:S(2)}) collective-permute-start(bf16[4,256,256]{2,1,0:T(8,128)(2,1)} %constant_dynamic-slice_fusion.1), channel_id=1, source_target_pairs={{0,128},{1,385},{128,256},{129,1},{256,384},{257,129},{384,0},{385... | collective-permute-start | bytes 1572872 | tf_op jit(solution)/shard_map/ppermute | solution.py:140
  39.1 22.6 %collective-permute-start.2 = (bf16[8,256,256]{2,1,0:T(8,128)(2,1)S(1)}, bf16[8,256,256]{2,1,0:T(8,128)(2,1)}, u32[]{:S(2)}, u32[]{:S(2)}) collective-permute-start(bf16[8,256,256]{2,1,0:T(8,128)(2,1)S(1)} %collective-permute-done.refs_1_), channel_id=1, source_target_pairs={{0,1},{1,0},{2,3},{3,2},{4,5},{5,4},{6,7},{7,6},{8,9},{9,8},{10,11... | collective-permute-start | bytes 3145736 | tf_op jit(solution)/shard_map/ppermute | solution.py:132
  41.6 17.6 %all-to-all-start.1 = ((bf16[16,32,256]{2,1,0:T(8,128)(2,1)}), bf16[16,32,256]{2,1,0:T(8,128)(2,1)S(1)}, u32[]{:S(2)}, u32[]{:S(2)}) async-start(bf16[16,32,256]{2,1,0:T(8,128)(2,1)} %bitcast.21), calls=%async_computation.1 | async-start | bytes 524288 | tf_op jit(solution)/shard_map/all_to_all | solution.py:169
  47.0 14.7 %collective-permute-start.3 = (bf16[4,256,256]{2,1,0:T(8,128)(2,1)S(1)}, bf16[4,256,256]{2,1,0:T(8,128)(2,1)}, u32[]{:S(2)}, u32[]{:S(2)}) collective-permute-start(bf16[4,256,256]{2,1,0:T(8,128)(2,1)S(1)} %collective-permute-done.1.refs_0_), channel_id=1, source_target_pairs={{0,1},{1,0},{2,3},{3,2},{4,5},{5,4},{6,7},{7,6},{8,9},{9,8},{10,11... | collective-permute-start | bytes 1572872 | tf_op jit(solution)/shard_map/ppermute | solution.py:132
Sparse Core Ops, SparseCore 0:
  9.5 55.3 all-gather.1

commit v11 on v9

--- a/solution.py
+++ b/solution.py
@@ -10,7 +10,7 @@
 X = XB * XA
 AXIS_X, SEC, MPO = ("xb", "xa"), ("xb", "xa", "z"), ("y", "c")
 BF16, F32 = jnp.bfloat16, jnp.float32
-STEPS = 4
+STEPS = 2
 
 
 def half_kernel(left_ref, *refs):

time: 120 us -> 120 us (level)
  no operation moved by 1% of the time
where the time goes in v11:
time: 120 us; the launch traced here: 118 us
  blocking collectives  36.4 us (30%)
  starting transfers between devices  27.6 us (23%)
  waiting for transfers between devices  18.2 us (15%)
  Pallas kernels  15.9 us (13%)
  between operations  13.5 us (11%)
  local copies, waits for them, and re-layouts  4.81 us (4%)
  other arithmetic  2.05 us (2%)
    all_to_all x1, blocking collectives, on_device(): lax.all_to_all(partial, ('xa', 'z'), split_axis=0, concat_axis=0, tiled=T...  36.4 us
    all_to_all x1, waiting for transfers between devices, on_device(): lefts = lax.all_to_all(left, MPO, split_axis=0, concat_axis=0, tiled=True)  11.1 us
    ppermute x2, starting transfers between devices, both_ways(): return lax.ppermute(block, (*AXIS_X, 'c'), pairs)  9.92 us
    pallas_call x1, Pallas kernels, sums(): pl.pallas_call(sums_kernel, grid_spec=pltpu.PrefetchScalarGridSpec(num_sc...  9.65 us
    all_to_all x1, starting transfers between devices, on_device(): lefts = lax.all_to_all(left, MPO, split_axis=0, concat_axis=0, tiled=True)  7.23 us
    pallas_call x2, Pallas kernels, halves(): pl.pallas_call(half_kernel, in_specs=[pl.BlockSpec(memory_space=pltpu.VME...  6.26 us
    all_to_all x1, starting transfers between devices, on_device(): lax.all_to_all(target.reshape(X * shards, -1), (*AXIS_X, *MPO), split_axi...  5.6 us
    ppermute x2, starting transfers between devices, moved(): lax.ppermute(block, axis, [(i, (i + by) % size) for i in range(size)])  4.84 us
  transfers between devices with their start and end apart: 7, of which 3 were waited for; matrix products, arithmetic and copies ran while one was open for 3% of the time, Pallas kernels for 5%

profile of v11, /device:TPU:1, one launch (start us, length us, event | category | flops | bytes accessed | tf_op | source)
XLA Modules:
  0.0 118.5 jit_solution(6220944465145657173)
XLA Ops:
  6.5 0.0 copy-start
  6.5 0.0 copy-start.1
  6.5 0.0 all-gather.2.cloned.1.call-start
  6.5 1.0 copy-done
  7.6 0.7 constant_dynamic-slice_fusion
  8.3 0.0 all-gather.2.cloned.1.call-update
  8.3 5.2 %collective-permute-start = (bf16[8,256,256]{2,1,0:T(8,128)(2,1)}, bf16[8,256,256]{2,1,0:T(8,128)(2,1)S(1)}, u32[]{:S(2)}, u32[]{:S(2)}) collective-permute-start(bf16[8,256,256]{2,1,0:T(8,128)(2,1)} %refs_0_.1), channel_id=1, source_target_pairs={{0,128},{1,385},{128,256},{129,1},{256,384},{257,129},{384,0},{385... | collective-permute-start | bytes 3145736 | tf_op jit(solution)/shard_map/ppermute | solution.py:140
  13.6 1.0 constant_dynamic-slice_fusion.2
  14.5 0.7 copy.7
  15.3 7.2 %all-to-all-start = ((bf16[16,32,256]{2,1,0:T(8,128)(2,1)}), bf16[16,32,256]{2,1,0:T(8,128)(2,1)S(1)}, u32[]{:S(2)}, u32[]{:S(2)}) async-start(bf16[16,32,256]{2,1,0:T(8,128)(2,1)} %bitcast.4), calls=%async_computation | async-start | bytes 524288 | tf_op jit(solution)/shard_map/all_to_all | solution.py:162
  22.5 0.7 bitcast_add_fusion
  23.2 11.1 %all-to-all-done = bf16[16,32,256]{2,1,0:T(8,128)(2,1)S(1)} async-done(((bf16[16,32,256]{2,1,0:T(8,128)(2,1)}), bf16[16,32,256]{2,1,0:T(8,128)(2,1)S(1)}, u32[]{:S(2)}, u32[]{:S(2)}) %all-to-all-start) | async-done | bytes 262176 | tf_op jit(solution)/shard_map/all_to_all | solution.py:162
  34.2 0.0 collective-permute-done.refs_1_
  34.3 4.7 %collective-permute-start.1 = (bf16[4,256,256]{2,1,0:T(8,128)(2,1)S(1)}, bf16[4,256,256]{2,1,0:T(8,128)(2,1)S(1)}, u32[]{:S(2)}, u32[]{:S(2)}) collective-permute-start(bf16[4,256,256]{2,1,0:T(8,128)(2,1)S(1)} %constant_dynamic-slice_fusion.1), channel_id=1, source_target_pairs={{0,128},{1,385},{128,256},{129,1},{256,384},{257,129},{384,0},{385... | collective-permute-start | bytes 1572872 | tf_op jit(solution)/shard_map/ppermute | solution.py:140
  39.0 1.9 %collective-permute-start.2 = (bf16[8,256,256]{2,1,0:T(8,128)(2,1)S(1)}, bf16[8,256,256]{2,1,0:T(8,128)(2,1)}, u32[]{:S(2)}, u32[]{:S(2)}) collective-permute-start(bf16[8,256,256]{2,1,0:T(8,128)(2,1)S(1)} %collective-permute-done.refs_1_), channel_id=1, source_target_pairs={{0,1},{1,0},{2,3},{3,2},{4,5},{5,4},{6,7},{7,6},{8,9},{9,8},{10,11... | collective-permute-start | bytes 3145736 | tf_op jit(solution)/shard_map/ppermute | solution.py:132
  40.9 4.2 %collective-permute-done.1.refs_0_ = bf16[4,256,256]{2,1,0:T(8,128)(2,1)S(1)} collective-permute-done((bf16[4,256,256]{2,1,0:T(8,128)(2,1)S(1)}, bf16[4,256,256]{2,1,0:T(8,128)(2,1)S(1)}, u32[]{:S(2)}, u32[]{:S(2)}) %collective-permute-start.1) | collective-permute-done | bytes 524320 | tf_op jit(solution)/shard_map/ppermute | solution.py:140
  45.1 2.9 %collective-permute-start.3 = (bf16[4,256,256]{2,1,0:T(8,128)(2,1)S(1)}, bf16[4,256,256]{2,1,0:T(8,128)(2,1)}, u32[]{:S(2)}, u32[]{:S(2)}) collective-permute-start(bf16[4,256,256]{2,1,0:T(8,128)(2,1)S(1)} %collective-permute-done.1.refs_0_), channel_id=1, source_target_pairs={{0,1},{1,0},{2,3},{3,2},{4,5},{5,4},{6,7},{7,6},{8,9},{9,8},{10,11... | collective-permute-start | bytes 1572872 | tf_op jit(solution)/shard_map/ppermute | solution.py:132
  48.0 0.6 pad_add_fusion.place_ref
  48.6 0.1 broadcast_in_dim.7
  48.7 0.6 broadcast_in_dim.8
  49.3 5.6 %all-to-all-start.1 = ((s32[64,1,16]{2,1,0:T(1,128)}), s32[64,1,16]{2,1,0:T(1,128)S(1)}, u32[]{:S(2)}, u32[]{:S(2)}) async-start(s32[64,1,16]{2,1,0:T(1,128)} %bitcast.7), calls=%async_computation.1 | async-start | bytes 65536 | tf_op jit(solution)/shard_map/all_to_all | solution.py:170
  54.9 0.0 copy-done.1
  54.9 2.5 %halves.2.half_a = bf16[16,32,16,256]{3,2,1,0:T(8,128)(2,1)} custom-call(bf16[512,256]{1,0:T(8,128)(2,1)S(1)} %bitcast.21, bf16[8,256,256]{2,1,0:T(8,128)(2,1)S(1)} %copy-done.1, bf16[8,256,256]{2,1,0:T(8,128)(2,1)S(1)} %collective-permute-done.refs_1_), custom_call_target="tpu_custom_call" | custom-call | flops 1073741824 | bytes 6291456 | tf_op jit(solution)/shard_map/halves/pallas_call | solution.py:36
  57.4 0.0 collective-permute-done.3.refs_2_
  57.4 0.0 collective-permute-done.2.refs_1_
  57.4 3.8 %halves.3.half_b = bf16[16,32,16,256]{3,2,1,0:T(8,128)(2,1)} custom-call(bf16[512,256]{1,0:T(8,128)(2,1)S(1)} %bitcast.22, bf16[4,256,256]{2,1,0:T(8,128)(2,1)S(1)} %collective-permute-done.1.refs_0_, bf16[8,256,256]{2,1,0:T(8,128)(2,1)} %collective-permute-done.2.refs_1_, bf16[4,256,256]{2,1,0:T(8,128)(2,1)} %collective-permute-done.3.refs_2_), custom_call_target="tpu_custom_call" | custom-call | flops 1073741824 | bytes 6291456 | tf_op jit(solution)/shard_map/halves/pallas_call | solution.py:36
  61.2 2.9 %all-to-all-done.1 = s32[64,1,16]{2,1,0:T(1,128)S(1)} async-done(((s32[64,1,16]{2,1,0:T(1,128)}), s32[64,1,16]{2,1,0:T(1,128)S(1)}, u32[]{:S(2)}, u32[]{:S(2)}) %all-to-all-start.1) | async-done | bytes 4128 | tf_op jit(solution)/shard_map/all_to_all | solution.py:170
  64.1 0.0 copy-start.2
  64.1 0.6 copy-done.2
  64.7 9.7 %sums.1 = bf16[128,16,256]{2,1,0:T(8,128)(2,1)} custom-call(s32[2]{0:T(128)} %pad_add_fusion.place_ref, s32[64,16]{1,0:T(8,128)} %bitcast.25, bf16[16,32,16,256]{3,2,1,0:T(8,128)(2,1)} %halves.2.half_a, bf16[16,32,16,256]{3,2,1,0:T(8,128)(2,1)} %halves.3.half_b, bf16[32,256,256]{2,1,0:T(8,128)(2,1)} %all-gather.2.cloned.1.call-done.right_ref), custom_call_target="tpu_custom_call" | custom-call | flops 2147483648 | bytes 12582912 | tf_op jit(solution)/shard_map/sums/pallas_call | solution.py:107
  74.4 36.4 %all_to_all.21 = bf16[16,8,16,256]{3,2,1,0:T(8,128)(2,1)S(1)} all-to-all(bf16[16,8,16,256]{3,2,1,0:T(8,128)(2,1)} %bitcast.23), channel_id=1, replica_groups=mesh['xb'=2,'xa'=2,'z'=8,'y'=8,'c'=2] {'xa','z'}, dimensions={0} | all-to-all | bytes 2097152 | tf_op jit(solution)/shard_map/all_to_all | solution.py:180
  110.8 0.8 convert_add_fusion
  (2 shorter events, 0.0 us)
Async XLA Ops:
  6.5 1.0 copy-start
  6.5 48.4 %copy-start.1 = (bf16[8,256,256]{2,1,0:T(8,128)(2,1)S(1)}, bf16[8,256,256]{2,1,0:T(8,128)(2,1)}, u32[]{:S(2)}) copy-start(bf16[8,256,256]{2,1,0:T(8,128)(2,1)} %refs_0_.1) | copy-start | bytes 3145732
  6.5 57.6 %all-gather.2.cloned.1.call-start = ((), (), s32[]{:S(2)}) async-start(), calls=%async_computation.3 | async-start | bytes 4456448 | tf_op jit(solution)/shard_map/all_gather | solution.py:158
  8.3 25.9 %collective-permute-start = (bf16[8,256,256]{2,1,0:T(8,128)(2,1)}, bf16[8,256,256]{2,1,0:T(8,128)(2,1)S(1)}, u32[]{:S(2)}, u32[]{:S(2)}) collective-permute-start(bf16[8,256,256]{2,1,0:T(8,128)(2,1)} %refs_0_.1), channel_id=1, source_target_pairs={{0,128},{1,385},{128,256},{129,1},{256,384},{257,129},{384,0},{385... | collective-permute-start | bytes 3145736 | tf_op jit(solution)/shard_map/ppermute | solution.py:140
  15.3 19.0 %all-to-all-start = ((bf16[16,32,256]{2,1,0:T(8,128)(2,1)}), bf16[16,32,256]{2,1,0:T(8,128)(2,1)S(1)}, u32[]{:S(2)}, u32[]{:S(2)}) async-start(bf16[16,32,256]{2,1,0:T(8,128)(2,1)} %bitcast.4), calls=%async_computation | async-start | bytes 524288 | tf_op jit(solution)/shard_map/all_to_all | solution.py:162
  34.3 10.8 %collective-permute-start.1 = (bf16[4,256,256]{2,1,0:T(8,128)(2,1)S(1)}, bf16[4,256,256]{2,1,0:T(8,128)(2,1)S(1)}, u32[]{:S(2)}, u32[]{:S(2)}) collective-permute-start(bf16[4,256,256]{2,1,0:T(8,128)(2,1)S(1)} %constant_dynamic-slice_fusion.1), channel_id=1, source_target_pairs={{0,128},{1,385},{128,256},{129,1},{256,384},{257,129},{384,0},{385... | collective-permute-start | bytes 1572872 | tf_op jit(solution)/shard_map/ppermute | solution.py:140
  39.0 18.4 %collective-permute-start.2 = (bf16[8,256,256]{2,1,0:T(8,128)(2,1)S(1)}, bf16[8,256,256]{2,1,0:T(8,128)(2,1)}, u32[]{:S(2)}, u32[]{:S(2)}) collective-permute-start(bf16[8,256,256]{2,1,0:T(8,128)(2,1)S(1)} %collective-permute-done.refs_1_), channel_id=1, source_target_pairs={{0,1},{1,0},{2,3},{3,2},{4,5},{5,4},{6,7},{7,6},{8,9},{9,8},{10,11... | collective-permute-start | bytes 3145736 | tf_op jit(solution)/shard_map/ppermute | solution.py:132
  45.1 12.3 %collective-permute-start.3 = (bf16[4,256,256]{2,1,0:T(8,128)(2,1)S(1)}, bf16[4,256,256]{2,1,0:T(8,128)(2,1)}, u32[]{:S(2)}, u32[]{:S(2)}) collective-permute-start(bf16[4,256,256]{2,1,0:T(8,128)(2,1)S(1)} %collective-permute-done.1.refs_0_), channel_id=1, source_target_pairs={{0,1},{1,0},{2,3},{3,2},{4,5},{5,4},{6,7},{7,6},{8,9},{9,8},{10,11... | collective-permute-start | bytes 1572872 | tf_op jit(solution)/shard_map/ppermute | solution.py:132
  49.3 14.8 %all-to-all-start.1 = ((s32[64,1,16]{2,1,0:T(1,128)}), s32[64,1,16]{2,1,0:T(1,128)S(1)}, u32[]{:S(2)}, u32[]{:S(2)}) async-start(s32[64,1,16]{2,1,0:T(1,128)} %bitcast.7), calls=%async_computation.1 | async-start | bytes 65536 | tf_op jit(solution)/shard_map/all_to_all | solution.py:170
  64.1 0.6 copy-start.2
Sparse Core Ops, SparseCore 0:
  9.5 51.2 all-gather.1
